TPU v7x, 32 devices: a whole 2x2x4 slice. The times are simulated.
32 devices in a mesh: group: 2 (over y), expert: 4 (over x, core), shard: 4 (over z).
Axes of the slice: x: 2, y: 2, z: 4, core: 2. Of those that a mesh axis runs over, the one named last changes fastest.
Arguments:
- tokens: bfloat16 [8192, 2048], P(('group', 'expert', 'shard')), may hold values from -6 to 6
- cotangent: bfloat16 [8192, 2048], P(('group', 'expert', 'shard')), may hold values from -6 to 6
- gain_attn: float32 [2048], replicated, may hold values from 0.1 to 1.9
- w_query: bfloat16 [2048, 3072], P('shard'), may hold values from -0.125 to 0.125
- w_latent: bfloat16 [2048, 576], P('shard'), may hold values from -0.125 to 0.125
- gain_latent: float32 [512], replicated, may hold values from 0.1 to 1.9
- w_keyval: bfloat16 [512, 4096], P('shard'), may hold values from -0.25 to 0.25
- w_output: bfloat16 [2048, 2048], P('shard'), may hold values from -0.75 to 0.75
- gain_ffn: float32 [2048], replicated, may hold values from 0.1 to 1.9
- w_shared_gate: bfloat16 [2048, 2816], P('shard'), may hold values from -0.125 to 0.125
- w_shared_up: bfloat16 [2048, 2816], P('shard'), may hold values from -0.125 to 0.125
- w_shared_down: bfloat16 [2816, 2048], P('shard'), may hold values from -0.109375 to 0.109375
- w_router: bfloat16 [2048, 16], P('shard'), may hold values from -0.25 to 0.25
- expert_gate: bfloat16 [16, 2048, 1408], P(('expert', 'shard')), may hold values from -0.125 to 0.125
- expert_up: bfloat16 [16, 2048, 1408], P(('expert', 'shard')), may hold values from -0.125 to 0.125
- expert_down: bfloat16 [16, 1408, 2048], P(('expert', 'shard')), may hold values from -0.875 to 0.875
- segments: int32 [8192], P('group'), may hold values from 0 to 8, as said below
- positions: int32 [8192], P('group'), may hold values from 0 to 2303, as said below
- routes: int32 [8192, 6], P(('group', 'expert', 'shard')), may hold values from 0 to 15, all different within a row; in each aligned block of 256 rows (0 to 255, 256 to 511, ...) at most 144 rows name the same one
Outputs:
- output: bfloat16 [8192, 2048], P(('group', 'expert', 'shard'))
- grad_tokens: float32 [8192, 2048], P(('group', 'expert', 'shard'))
- grad_gain_attn: float32 [2048], P(('group', 'expert', 'shard'))
- grad_w_query: float32 [2048, 3072], P(('group', 'expert', 'shard'))
- grad_w_latent: float32 [2048, 576], P(('group', 'expert', 'shard'))
- grad_gain_latent: float32 [512], P(('group', 'expert', 'shard'))
- grad_w_keyval: float32 [512, 4096], P(('group', 'expert', 'shard'))
- grad_w_output: float32 [2048, 2048], P(('group', 'expert', 'shard'))
- grad_gain_ffn: float32 [2048], P(('group', 'expert', 'shard'))
- grad_w_shared_gate: float32 [2048, 2816], P(('group', 'expert', 'shard'))
- grad_w_shared_up: float32 [2048, 2816], P(('group', 'expert', 'shard'))
- grad_w_shared_down: float32 [2816, 2048], P(('group', 'expert', 'shard'))
- grad_w_router: float32 [2048, 16], P(('group', 'expert', 'shard'))
- grad_expert_gate: float32 [16, 2048, 1408], P(('expert', 'shard'), 'group')
- grad_expert_up: float32 [16, 2048, 1408], P(('expert', 'shard'), 'group')
- grad_expert_down: float32 [16, 1408, 2048], P(('expert', 'shard'), 'group')
Inputs may be any that keep to these rules, and one draw needn't show every extreme that they name: `segments`: each aligned run of 256 tokens is one piece of one sequence: either 256 consecutive prompt positions starting at a multiple of 256, or a whole continuation. Each run of 4096 tokens holds 1 prompt group whole, in any order of pieces; a group's prompt has segment id group * (9) and its continuations group * 9 + 1 to group * 9 + 8. Prompt tokens have positions 0 to 2047 in order within each piece; a continuation's tokens have positions 2048 to 2303 in order. `routes`: each row names 6 different experts; among the 256 rows of one device no expert is named more than 144 times.
All inputs are finite; a program needn't handle non-finite values.
Results may differ from a plain program's by a relative error of at most 0.023.
Values may be sent and summed in bfloat16 or wider, within the bound.
No kernel may reach another device: no remote copies, remote signals or barrier semaphores. Data moves between devices by JAX's collectives and lax.ppermute only.
A program may use at most 576 MiB of HBM per device.

v0:
```python
import math

import jax
import jax.numpy as jnp
from jax import lax
from jax.sharding import PartitionSpec as P

HEADS = 16
NOPE = 128
ROPE = 64
VDIM = 128
LATENT = 512
BLOCK = 256
PROMPT = 2048
NCONT = 8


EPS = 1e-06
HIGH = lax.Precision.HIGHEST


def matmul(left, right):
    return jnp.dot(left, right, preferred_element_type=jnp.float32)


def matmul_nt(left, right):
    return lax.dot_general(
        left, right, (((1,), (1,)), ((), ())), preferred_element_type=jnp.float32
    )


def matmul_tn(left, right):
    return lax.dot_general(
        left, right, (((0,), (0,)), ((), ())), preferred_element_type=jnp.float32
    )


def rms_parts(values):
    inverse = lax.rsqrt(jnp.mean(values * values, axis=-1, keepdims=True) + EPS)
    return (values * inverse, inverse)


def norm_back(grad_in, normed, inverse, gain):
    scaled = grad_in * gain
    gain_grad = jnp.sum(grad_in * normed, axis=0)
    input_grad = inverse * (scaled - normed * jnp.mean(scaled * normed, axis=-1, keepdims=True))
    return (input_grad, gain_grad)


def angles(pos_list, rot_width):
    half_width = rot_width // 2
    freq = 10000.0 ** (-2.0 * jnp.arange(half_width, dtype=jnp.float32) / rot_width)
    theta = pos_list.astype(jnp.float32)[:, None] * freq[None, :]
    return (jnp.cos(theta), jnp.sin(theta))


def rotate(values, cosine, sine):
    half_width = values.shape[-1] // 2
    first_half = values[..., :half_width]
    second_half = values[..., half_width:]
    return jnp.concatenate(
        [first_half * cosine - second_half * sine, second_half * cosine + first_half * sine],
        axis=-1,
    )


def unrotate(grad_in, cosine, sine):
    half_width = grad_in.shape[-1] // 2
    first_half = grad_in[..., :half_width]
    second_half = grad_in[..., half_width:]
    return jnp.concatenate(
        [first_half * cosine + second_half * sine, second_half * cosine - first_half * sine],
        axis=-1,
    )


def silu_parts(values):
    sigmoid = jax.nn.sigmoid(values)
    return (values * sigmoid, sigmoid * (1.0 + values * (1.0 - sigmoid)))


def trade(buffer):
    return lax.all_to_all(buffer, ("expert", "shard"), split_axis=0, concat_axis=0, tiled=True)


def per_device(
    tokens,
    cotangent,
    gain_attn,
    w_query,
    w_latent,
    gain_latent,
    w_keyval,
    w_output,
    gain_ffn,
    w_shared_gate,
    w_shared_up,
    w_shared_down,
    w_router,
    expert_gate,
    expert_up,
    expert_down,
    segments,
    positions,
    routes,
):
    tok_rows = tokens.shape[0]
    row_tokens = segments.shape[0]
    dev_index = lax.axis_index(("expert", "shard"))
    row_start = dev_index * tok_rows
    own_seg = lax.dynamic_slice_in_dim(segments, row_start, tok_rows)
    own_pos = lax.dynamic_slice_in_dim(positions, row_start, tok_rows)
    inputs = tokens.astype(jnp.float32)
    w_q, w_l, w_kv, w_o = (
        lax.all_gather(w_query, "shard", axis=0, tiled=True),
        lax.all_gather(w_latent, "shard", axis=0, tiled=True),
        lax.all_gather(w_keyval, "shard", axis=0, tiled=True),
        lax.all_gather(w_output, "shard", axis=0, tiled=True),
    )
    normed1, inverse1 = rms_parts(inputs)
    hidden1 = (normed1 * gain_attn).astype(jnp.bfloat16)
    query_full = matmul(hidden1, w_q).reshape(tok_rows, HEADS, NOPE + ROPE)
    cosine, sine = angles(own_pos, ROPE)
    query_nope = query_full[..., :NOPE].astype(jnp.bfloat16)
    query_rope = rotate(query_full[..., NOPE:], cosine[:, None, :], sine[:, None, :]).astype(
        jnp.bfloat16
    )
    latent = matmul(hidden1, w_l)
    normed_c, inverse_c = rms_parts(latent[:, :LATENT])
    compressed = (normed_c * gain_latent).astype(jnp.bfloat16)
    key_rope = rotate(latent[:, LATENT:], cosine, sine).astype(jnp.bfloat16)
    all_comp, all_rope = (
        lax.all_gather(compressed, ("expert", "shard"), axis=0, tiled=True),
        lax.all_gather(key_rope, ("expert", "shard"), axis=0, tiled=True),
    )
    score_scale = 1.0 / math.sqrt(NOPE + ROPE)
    lead_seg = own_seg[0]
    group_id = lead_seg // (NCONT + 1)
    is_cont = lead_seg % (NCONT + 1) != 0
    prompt_match = segments == group_id * (NCONT + 1)
    key_index = (
        jnp.zeros((PROMPT,), jnp.int32)
        .at[jnp.where(prompt_match, positions, PROMPT)]
        .set(jnp.arange(row_tokens, dtype=jnp.int32), mode="drop")
    )
    keys_comp = jnp.concatenate([all_comp[key_index], compressed], axis=0)
    keys_rope = jnp.concatenate([all_rope[key_index], key_rope], axis=0)
    keyval = (
        matmul(keys_comp, w_kv).astype(jnp.bfloat16).reshape(PROMPT + BLOCK, HEADS, NOPE + VDIM)
    )
    key_pos = jnp.concatenate([jnp.arange(PROMPT, dtype=jnp.int32), own_pos], axis=0)
    key_open = jnp.concatenate([jnp.ones((PROMPT,), bool), jnp.full((BLOCK,), is_cont)], axis=0)
    allowed_keys = ((key_pos[None, :] <= own_pos[:, None]) & key_open[None, :])[None, :, :]
    scores = jnp.einsum(
        "qhn,khn->hqk", query_nope, keyval[..., :NOPE], preferred_element_type=jnp.float32
    )
    scores = (
        scores
        + jnp.einsum("qhr,kr->hqk", query_rope, keys_rope, preferred_element_type=jnp.float32)
    ) * score_scale
    top_score = jnp.max(jnp.where(allowed_keys, scores, -jnp.inf), axis=-1, keepdims=True)
    exp_terms = jnp.where(
        allowed_keys, jnp.exp(jnp.where(allowed_keys, scores, top_score) - top_score), 0.0
    )
    total = jnp.sum(exp_terms, axis=-1, keepdims=True)
    prob_attn = (exp_terms / total).astype(jnp.bfloat16)
    log_total = top_score + jnp.log(total)
    block_mixed = jnp.einsum(
        "hqk,khv->qhv", prob_attn, keyval[..., NOPE:], preferred_element_type=jnp.float32
    )
    mixed_parts = block_mixed.reshape(BLOCK, HEADS * VDIM)
    kept_block = (key_index, keys_comp, keys_rope, keyval, allowed_keys, log_total)
    mixed = mixed_parts.astype(jnp.bfloat16)
    after = inputs + matmul(mixed, w_o)
    w_sg, w_su, w_sd, w_r = (
        lax.all_gather(w_shared_gate, "shard", axis=0, tiled=True),
        lax.all_gather(w_shared_up, "shard", axis=0, tiled=True),
        lax.all_gather(w_shared_down, "shard", axis=0, tiled=True),
        lax.all_gather(w_router, "shard", axis=0, tiled=True),
    )
    normed2, inverse2 = rms_parts(after)
    hidden2 = (normed2 * gain_ffn).astype(jnp.bfloat16)
    shared_gate = matmul(hidden2, w_sg)
    shared_up = matmul(hidden2, w_su)
    shared_act, shared_slope = silu_parts(shared_gate)
    shared_mid = (shared_act * shared_up).astype(jnp.bfloat16)
    shared = matmul(shared_mid, w_sd)
    logits = matmul(hidden2, w_r)
    logit_exp = jnp.exp(logits - jnp.max(logits, axis=-1, keepdims=True))
    router_prob = logit_exp / jnp.sum(logit_exp, axis=-1, keepdims=True)
    expert_count = w_r.shape[1]
    top_count = routes.shape[1]
    capacity = 3 * tok_rows * top_count // (2 * expert_count)
    route_hot = (
        routes[:, :, None] == jnp.arange(expert_count, dtype=jnp.int32)[None, None, :]
    ).astype(jnp.float32)
    route_weight = jnp.einsum(
        "tke,te->tk", route_hot, router_prob, precision=HIGH, preferred_element_type=jnp.float32
    )
    flat_route = routes.reshape(-1)
    flat_hot = (flat_route[:, None] == jnp.arange(expert_count, dtype=jnp.int32)[None, :]).astype(
        jnp.int32
    )
    before = jnp.cumsum(flat_hot, axis=0) - flat_hot
    slot_num = jnp.sum(before * flat_hot, axis=1)
    places = flat_route * capacity + slot_num
    pair_count = tok_rows * top_count
    row_of = (
        jnp.full((expert_count * capacity,), pair_count, jnp.int32)
        .at[places]
        .set(jnp.arange(pair_count, dtype=jnp.int32))
    )
    token_of = jnp.where(row_of < pair_count, row_of // top_count, tok_rows)
    padded = jnp.concatenate([hidden2, jnp.zeros((1, hidden2.shape[1]), jnp.bfloat16)], axis=0)
    outgoing = padded[token_of].reshape(expert_count, capacity, hidden2.shape[1])
    incoming = trade(outgoing)
    expert_rows = incoming.reshape(expert_count * capacity, hidden2.shape[1])
    e_gate = matmul(expert_rows, expert_gate[0])
    e_up = matmul(expert_rows, expert_up[0])
    e_act, e_slope = silu_parts(e_gate)
    e_mid = (e_act * e_up).astype(jnp.bfloat16)
    e_out = (
        matmul(e_mid, expert_down[0])
        .astype(jnp.bfloat16)
        .reshape(expert_count, capacity, hidden2.shape[1])
    )
    returned = trade(e_out).reshape(expert_count * capacity, hidden2.shape[1])
    picked = returned[places].reshape(tok_rows, top_count, hidden2.shape[1])
    routed = jnp.einsum(
        "tk,tkd->td", route_weight, picked, precision=HIGH, preferred_element_type=jnp.float32
    )
    output = (after + shared + routed).astype(jnp.bfloat16)
    grad_out = cotangent.astype(jnp.float32)
    grad_weight = jnp.einsum(
        "td,tkd->tk", grad_out, picked, precision=HIGH, preferred_element_type=jnp.float32
    )
    grad_pairs = (
        (route_weight[:, :, None] * grad_out[:, None, :])
        .astype(jnp.bfloat16)
        .reshape(pair_count, hidden2.shape[1])
    )
    grad_padded = jnp.concatenate(
        [grad_pairs, jnp.zeros((1, hidden2.shape[1]), jnp.bfloat16)], axis=0
    )
    grad_outgoing = grad_padded[row_of].reshape(expert_count, capacity, hidden2.shape[1])
    grad_incoming = trade(grad_outgoing).reshape(expert_count * capacity, hidden2.shape[1])
    grad_e_mid = matmul_nt(grad_incoming, expert_down[0])
    grad_e_gate = (grad_e_mid * e_up * e_slope).astype(jnp.bfloat16)
    grad_e_up = (grad_e_mid * e_act).astype(jnp.bfloat16)
    grad_e_rows = (
        matmul_nt(grad_e_gate, expert_gate[0]) + matmul_nt(grad_e_up, expert_up[0])
    ).astype(jnp.bfloat16)
    grad_back = trade(grad_e_rows.reshape(expert_count, capacity, hidden2.shape[1])).reshape(
        expert_count * capacity, hidden2.shape[1]
    )
    egrad_gate = matmul_tn(expert_rows, grad_e_gate)
    egrad_up = matmul_tn(expert_rows, grad_e_up)
    egrad_down = matmul_tn(e_mid, grad_incoming)
    grad_hidden2 = jnp.sum(
        grad_back[places].reshape(tok_rows, top_count, hidden2.shape[1]).astype(jnp.float32), axis=1
    )
    grad_prob = jnp.einsum(
        "tke,tk->te", route_hot, grad_weight, precision=HIGH, preferred_element_type=jnp.float32
    )
    grad_logits = (
        router_prob * (grad_prob - jnp.sum(router_prob * grad_prob, axis=-1, keepdims=True))
    ).astype(jnp.bfloat16)
    grad_hidden2 = grad_hidden2 + matmul_nt(grad_logits, w_r)
    grad_s_mid = matmul_nt(cotangent, w_sd)
    grad_s_gate = (grad_s_mid * shared_up * shared_slope).astype(jnp.bfloat16)
    grad_s_up = (grad_s_mid * shared_act).astype(jnp.bfloat16)
    grad_hidden2 = grad_hidden2 + matmul_nt(grad_s_gate, w_sg) + matmul_nt(grad_s_up, w_su)
    grad_after_norm, grad_gain_ffn = norm_back(grad_hidden2, normed2, inverse2, gain_ffn)
    grad_after = grad_out + grad_after_norm
    grad_attn = grad_after.astype(jnp.bfloat16)
    grad_mixed = matmul_nt(grad_attn, w_o).astype(jnp.bfloat16).reshape(tok_rows, HEADS, VDIM)
    w_kv_wide = w_kv.astype(jnp.float32)
    buffer_comp = jnp.zeros((row_tokens, LATENT), jnp.float32)
    buffer_rope = jnp.zeros((row_tokens, ROPE), jnp.float32)
    key_index, keys_comp, keys_rope, keyval, allowed_keys, log_total = kept_block
    scores = jnp.einsum(
        "qhn,khn->hqk", query_nope, keyval[..., :NOPE], preferred_element_type=jnp.float32
    )
    scores = (
        scores
        + jnp.einsum("qhr,kr->hqk", query_rope, keys_rope, preferred_element_type=jnp.float32)
    ) * score_scale
    prob_attn = jnp.where(allowed_keys, jnp.exp(scores - log_total), 0.0)
    grad_p = jnp.einsum(
        "qhv,khv->hqk", grad_mixed, keyval[..., NOPE:], preferred_element_type=jnp.float32
    )
    row_delta = jnp.sum(prob_attn * grad_p, axis=-1, keepdims=True)
    grad_s = (prob_attn * (grad_p - row_delta)).astype(jnp.bfloat16)
    grad_v = jnp.einsum(
        "hqk,qhv->khv",
        prob_attn.astype(jnp.bfloat16),
        grad_mixed,
        preferred_element_type=jnp.float32,
    )
    grad_kn = score_scale * jnp.einsum(
        "hqk,qhn->khn", grad_s, query_nope, preferred_element_type=jnp.float32
    )
    grad_kr = score_scale * jnp.einsum(
        "hqk,qhr->kr", grad_s, query_rope, preferred_element_type=jnp.float32
    )
    grad_q_nope = score_scale * jnp.einsum(
        "hqk,khn->qhn", grad_s, keyval[..., :NOPE], preferred_element_type=jnp.float32
    )
    grad_q_rope = score_scale * jnp.einsum(
        "hqk,kr->qhr", grad_s, keys_rope, preferred_element_type=jnp.float32
    )
    grad_kv = jnp.concatenate([grad_kn, grad_v], axis=-1).reshape(
        PROMPT + BLOCK, HEADS * (NOPE + VDIM)
    )
    grad_keys_comp = lax.dot_general(
        grad_kv,
        w_kv_wide,
        (((1,), (1,)), ((), ())),
        precision=HIGH,
        preferred_element_type=jnp.float32,
    )
    grad_wkv = lax.dot_general(
        keys_comp.astype(jnp.float32),
        grad_kv,
        (((0,), (0,)), ((), ())),
        precision=HIGH,
        preferred_element_type=jnp.float32,
    )
    own_rows = row_start + 0 + jnp.arange(BLOCK, dtype=jnp.int32)
    buffer_comp = (
        buffer_comp.at[key_index]
        .add(grad_keys_comp[:PROMPT])
        .at[own_rows]
        .add(grad_keys_comp[PROMPT:])
    )
    buffer_rope = buffer_rope.at[key_index].add(grad_kr[:PROMPT]).at[own_rows].add(grad_kr[PROMPT:])
    grad_comp, grad_krope = (
        lax.psum_scatter(
            buffer_comp.astype(jnp.bfloat16), ("expert", "shard"), scatter_dimension=0, tiled=True
        ).astype(jnp.float32),
        lax.psum_scatter(
            buffer_rope.astype(jnp.bfloat16), ("expert", "shard"), scatter_dimension=0, tiled=True
        ).astype(jnp.float32),
    )
    grad_latent_c, grad_gain_latent = norm_back(grad_comp, normed_c, inverse_c, gain_latent)
    grad_latent = jnp.concatenate(
        [grad_latent_c, unrotate(grad_krope, cosine, sine)], axis=-1
    ).astype(jnp.bfloat16)
    grad_qr = unrotate(grad_q_rope, cosine[:, None, :], sine[:, None, :])
    grad_query = (
        jnp.concatenate([grad_q_nope, grad_qr], axis=-1)
        .reshape(tok_rows, HEADS * (NOPE + ROPE))
        .astype(jnp.bfloat16)
    )
    grad_hidden1 = matmul_nt(grad_query, w_q) + matmul_nt(grad_latent, w_l)
    grad_in_norm, grad_gain_attn = norm_back(grad_hidden1, normed1, inverse1, gain_attn)
    grad_tokens = grad_after + grad_in_norm
    grad_wq = matmul_tn(hidden1, grad_query)
    grad_wl = matmul_tn(hidden1, grad_latent)
    grad_wo = matmul_tn(mixed, grad_attn)
    grad_sg = matmul_tn(hidden2, grad_s_gate)
    grad_su = matmul_tn(hidden2, grad_s_up)
    grad_sd = matmul_tn(shared_mid, cotangent)
    grad_router = matmul_tn(hidden2, grad_logits)
    reduced = (
        lax.psum_scatter(
            grad_gain_attn, ("group", "expert", "shard"), scatter_dimension=0, tiled=True
        ),
        lax.psum_scatter(grad_wq, ("group", "expert", "shard"), scatter_dimension=0, tiled=True),
        lax.psum_scatter(grad_wl, ("group", "expert", "shard"), scatter_dimension=0, tiled=True),
        lax.psum_scatter(
            grad_gain_latent, ("group", "expert", "shard"), scatter_dimension=0, tiled=True
        ),
        lax.psum_scatter(grad_wkv, ("group", "expert", "shard"), scatter_dimension=0, tiled=True),
        lax.psum_scatter(grad_wo, ("group", "expert", "shard"), scatter_dimension=0, tiled=True),
        lax.psum_scatter(
            grad_gain_ffn, ("group", "expert", "shard"), scatter_dimension=0, tiled=True
        ),
        lax.psum_scatter(grad_sg, ("group", "expert", "shard"), scatter_dimension=0, tiled=True),
        lax.psum_scatter(grad_su, ("group", "expert", "shard"), scatter_dimension=0, tiled=True),
        lax.psum_scatter(grad_sd, ("group", "expert", "shard"), scatter_dimension=0, tiled=True),
        lax.psum_scatter(
            grad_router, ("group", "expert", "shard"), scatter_dimension=0, tiled=True
        ),
    )
    expert_sums = (
        lax.psum_scatter(
            egrad_gate[None].astype(jnp.bfloat16), "group", scatter_dimension=1, tiled=True
        ).astype(jnp.float32),
        lax.psum_scatter(
            egrad_up[None].astype(jnp.bfloat16), "group", scatter_dimension=1, tiled=True
        ).astype(jnp.float32),
        lax.psum_scatter(
            egrad_down[None].astype(jnp.bfloat16), "group", scatter_dimension=1, tiled=True
        ).astype(jnp.float32),
    )
    return (
        output,
        grad_tokens,
        reduced[0],
        reduced[1],
        reduced[2],
        reduced[3],
        reduced[4],
        reduced[5],
        reduced[6],
        reduced[7],
        reduced[8],
        reduced[9],
        reduced[10],
        expert_sums[0],
        expert_sums[1],
        expert_sums[2],
    )


def solution(mesh):
    return jax.shard_map(
        per_device,
        mesh=mesh,
        in_specs=(
            P(("group", "expert", "shard"), None),
            P(("group", "expert", "shard"), None),
            P(),
            P("shard", None),
            P("shard", None),
            P(),
            P("shard", None),
            P("shard", None),
            P(),
            P("shard", None),
            P("shard", None),
            P("shard", None),
            P("shard", None),
            P(("expert", "shard"), None, None),
            P(("expert", "shard"), None, None),
            P(("expert", "shard"), None, None),
            P("group"),
            P("group"),
            P(("group", "expert", "shard"), None),
        ),
        out_specs=(
            P(("group", "expert", "shard"), None),
            P(("group", "expert", "shard"), None),
            P(("group", "expert", "shard")),
            P(("group", "expert", "shard"), None),
            P(("group", "expert", "shard"), None),
            P(("group", "expert", "shard")),
            P(("group", "expert", "shard"), None),
            P(("group", "expert", "shard"), None),
            P(("group", "expert", "shard")),
            P(("group", "expert", "shard"), None),
            P(("group", "expert", "shard"), None),
            P(("group", "expert", "shard"), None),
            P(("group", "expert", "shard"), None),
            P(("expert", "shard"), "group", None),
            P(("expert", "shard"), "group", None),
            P(("expert", "shard"), "group", None),
        ),
        check_vma=False,
    )
```

profile of v0, /device:TPU:0, one launch (start us, length us, event | category | flops | bytes accessed | tf_op | source)
XLA Modules:
  0.0 5267.6 jit_solution(9007942556276186518)
XLA Ops:
  9.5 53.2 %all-gather.9.cloned.1.call-done = bf16[2048,576]{0,1:T(8,128)(2,1)} async-done(((bf16[512,576]{0,1:T(8,128)(2,1)}), bf16[2048,576]{0,1:T(8,128)(2,1)}) %all-gather.9.cloned.1.call-update) | async-done | bytes 2359312 | tf_op jit(solution)/shard_map/all_gather | solution.py:116
  71.8 15.5 scatter_custom_fusion
  102.0 39.4 all_gather.34
  166.8 36.6 all-gather.13.cloned.1.call-done
  203.4 16.4 convolution_convert_fusion
  251.9 170.2 %all-gather.15.cloned.1.call-done = bf16[2048,3072]{1,0:T(8,128)(2,1)} async-done(((bf16[512,3072]{1,0:T(8,128)(2,1)}), bf16[2048,3072]{1,0:T(8,128)(2,1)}) %all-gather.15.cloned.1.call-update) | async-done | bytes 12582928 | tf_op jit(solution)/shard_map/all_gather | solution.py:115
  430.5 15.4 fusion.79
  445.9 28.9 select_reduce_fusion
  474.8 18.2 fusion.1
  493.6 19.9 fusion.54
  513.5 57.9 %all-gather.17.cloned.1.call-done = bf16[2048,2048]{1,0:T(8,128)(2,1)} async-done(((bf16[512,2048]{1,0:T(8,128)(2,1)}), bf16[2048,2048]{1,0:T(8,128)(2,1)}) %all-gather.17.cloned.1.call-update) | async-done | bytes 8388624 | tf_op jit(solution)/shard_map/all_gather | solution.py:118
  602.5 16.4 mul.414
  618.9 372.0 %all_gather.39 = bf16[2048,16]{0,1:T(8,128)(2,1)S(1)} all-gather(bf16[512,16]{0,1:T(8,128)(2,1)S(1)} %copy-done.83), channel_id=1, replica_groups=mesh['group'=2,'expert'=4,'shard'=4] {'shard'}, dimensions={0}, use_global_device_ids=true | all-gather | bytes 81920 | tf_op jit(solution)/shard_map/all_gather | solution.py:179
  1007.8 21.9 gather_fusion.4
  1035.6 21.1 fusion.23
  1056.8 19.1 fusion.27
  1075.9 351.1 %all-to-all-done.2 = bf16[16,144,2048]{2,1,0:T(8,128)(2,1)} async-done(((bf16[16,144,2048]{2,1,0:T(8,128)(2,1)}), bf16[16,144,2048]{2,1,0:T(8,128)(2,1)}, u32[]{:S(2)}, u32[]{:S(2)}) %all-to-all-start.2) | async-done | bytes 9437216 | tf_op jit(solution)/shard_map/all_to_all | solution.py:83
  1427.0 29.5 multiply_convert_fusion.1
  1456.5 20.5 convolution_convert_fusion.1
  1482.7 20.8 fusion.25
  1503.5 21.3 add_convert_fusion
  1524.9 349.2 %all-to-all-done.1 = bf16[16,144,2048]{2,1,0:T(8,128)(2,1)} async-done(((bf16[16,144,2048]{2,1,0:T(8,128)(2,1)}), bf16[16,144,2048]{2,1,0:T(8,128)(2,1)}, u32[]{:S(2)}, u32[]{:S(2)}) %all-to-all-start.1) | async-done | bytes 9437216 | tf_op jit(solution)/shard_map/all_to_all | solution.py:83
  1923.8 17.6 gather_fusion.3
  1962.9 122.8 %all-to-all-done.3 = bf16[16,144,2048]{2,1,0:T(8,128)(2,1)} async-done(((bf16[16,144,2048]{2,1,0:T(8,128)(2,1)}), bf16[16,144,2048]{2,1,0:T(8,128)(2,1)}, u32[]{:S(2)}, u32[]{:S(2)}) %all-to-all-start.3) | async-done | bytes 9437216 | tf_op jit(solution)/shard_map/all_to_all | solution.py:83
  2085.7 17.6 gather_fusion.5
  2138.2 21.5 fusion.10
  2159.7 29.4 multiply_reduce_fusion
  2189.1 31.0 multiply_convert_fusion
  2228.7 15.7 multiply_bitcast_fusion
  2260.8 26.3 pad_maximum_fusion
  2287.1 64.6 %fusion.140 = f32[2304,512]{1,0:T(8,128)} fusion(f32[2304,4096]{0,1:T(8,128)} %bitcast.175, bf16[512,4096]{1,0:T(8,128)(2,1)} %all-gather.13.cloned.1.call-done), kind=kOutput, calls=%fused_computation.229 | convolution fusion | flops 57982058496 | bytes 46661632 | tf_op jit(solution)/shard_map/dot_general | solution.py:315
  2351.8 17.7 scatter_custom_fusion.2
  2386.1 20.0 fusion.18
  2406.1 20.4 fusion.17
  2426.6 20.4 fusion.16
  2489.9 40.8 fusion.53
  2558.5 13.8 fusion.56
  2590.6 13.8 reduce-scatter.36.cloned.1.call-done
  2609.1 69.6 %reduce-scatter.34.cloned.1.call-done = bf16[1,1024,1408]{2,1,0:T(8,128)(2,1)} async-done(((bf16[1,2048,1408]{2,1,0:T(8,128)(2,1)}), bf16[1,1024,1408]{2,1,0:T(8,128)(2,1)}) %reduce-scatter.34.cloned.1.call-update) | async-done | bytes 2883600 | tf_op jit(solution)/shard_map/reduce_scatter | solution.py:387
  2709.9 106.4 %reduce-scatter.40.cloned.1.call-done = f32[64,16]{1,0:T(8,128)} async-done(((f32[2048,16]{1,0:T(8,128)}), f32[64,16]{1,0:T(8,128)}) %reduce-scatter.40.cloned.1.call-update) | async-done | bytes 4112
  2822.7 40.0 all-reduce.6
  2867.9 443.1 %reduce-scatter.30.cloned.1.call-done = f32[64,2816]{1,0:T(8,128)} async-done(((f32[2048,2816]{1,0:T(8,128)}), f32[64,2816]{1,0:T(8,128)}) %reduce-scatter.30.cloned.1.call-update) | async-done | bytes 720912 | tf_op jit(solution)/shard_map/reduce_scatter | solution.py:380
  3311.0 495.7 %reduce-scatter.28.cloned.1.call-done = f32[64,2816]{1,0:T(8,128)} async-done(((f32[2048,2816]{1,0:T(8,128)}), f32[64,2816]{1,0:T(8,128)}) %reduce-scatter.28.cloned.1.call-update) | async-done | bytes 720912 | tf_op jit(solution)/shard_map/reduce_scatter | solution.py:379
  3806.7 495.8 %reduce-scatter.32.cloned.1.call-done = f32[88,2048]{1,0:T(8,128)} async-done(((f32[2816,2048]{1,0:T(8,128)}), f32[88,2048]{1,0:T(8,128)}) %reduce-scatter.32.cloned.1.call-update) | async-done | bytes 720912 | tf_op jit(solution)/shard_map/reduce_scatter | solution.py:381
  4302.6 155.5 %reduce-scatter.22.cloned.1.call-done = f32[64,576]{1,0:T(8,128)} async-done(((f32[2048,576]{1,0:T(8,128)}), f32[64,576]{1,0:T(8,128)}) %reduce-scatter.22.cloned.1.call-update) | async-done | bytes 147472 | tf_op jit(solution)/shard_map/reduce_scatter | solution.py:370
  4458.1 187.3 %reduce-scatter.24.cloned.1.call-done = f32[16,4096]{1,0:T(8,128)} async-done(((f32[512,4096]{1,0:T(8,128)}), f32[16,4096]{1,0:T(8,128)}) %reduce-scatter.24.cloned.1.call-update) | async-done | bytes 262160 | tf_op jit(solution)/shard_map/reduce_scatter | solution.py:374
  4645.4 364.6 %reduce-scatter.26.cloned.1.call-done = f32[64,2048]{1,0:T(8,128)} async-done(((f32[2048,2048]{1,0:T(8,128)}), f32[64,2048]{1,0:T(8,128)}) %reduce-scatter.26.cloned.1.call-update) | async-done | bytes 524304 | tf_op jit(solution)/shard_map/reduce_scatter | solution.py:375
  5010.1 250.4 %reduce-scatter.20.cloned.1.call-done = f32[64,3072]{1,0:T(8,128)} async-done(((f32[2048,3072]{1,0:T(8,128)}), f32[64,3072]{1,0:T(8,128)}) %reduce-scatter.20.cloned.1.call-update) | async-done | bytes 786448 | tf_op jit(solution)/shard_map/reduce_scatter | solution.py:369
  (378 shorter events, 432.9 us)
Async XLA Ops:
  7.2 58.6 %copy-start.79 = (f32[512]{0:T(512)S(1)}, f32[512]{0:T(512)}, u32[]{:S(2)}) copy-start(f32[512]{0:T(512)} %param.24) | copy-start | bytes 6148
  7.2 55.6 %all-gather.9.cloned.1.call-start = ((), (), s32[]{:S(2)}) async-start(), calls=%async_computation.17 | async-start | bytes 2949120 | tf_op jit(solution)/shard_map/all_gather | solution.py:116
  7.9 140.4 %all-gather.11.cloned.1.call-start = ((), (), s32[]{:S(2)}) async-start(), calls=%async_computation.18 | async-start | bytes 4456448 | tf_op jit(solution)/shard_map/all_gather | solution.py:133
  9.5 412.6 %copy-start.61 = (f32[256]{0:T(256)}, f32[256]{0:T(256)S(1)}, u32[]{:S(2)}) copy-start(f32[256]{0:T(256)S(1)} %add_rsqrt_fusion.2) | copy-start | bytes 3076
  9.5 59.1 %copy-start.78 = (s32[4096]{0:T(1024)S(1)}, s32[4096]{0:T(1024)}, u32[]{:S(2)}) copy-start(s32[4096]{0:T(1024)} %param.35) | copy-start | bytes 49156
  9.5 61.7 %copy-start.72 = (s32[256,6]{0,1:T(8,128)S(1)}, s32[256,6]{0,1:T(8,128)}, u32[]{:S(2)}) copy-start(s32[256,6]{0,1:T(8,128)} %param.37) | copy-start | bytes 18436
  9.5 62.1 %copy-start.77 = (s32[4096]{0:T(1024)S(1)}, s32[4096]{0:T(1024)}, u32[]{:S(2)}) copy-start(s32[4096]{0:T(1024)} %param.36) | copy-start | bytes 49156
  65.7 36.3 copy-start.17
  66.7 34.9 copy-start.32
  66.7 136.7 %all-gather.13.cloned.1.call-start = ((), (), s32[]{:S(2)}) async-start(), calls=%async_computation.19 | async-start | bytes 5242880 | tf_op jit(solution)/shard_map/all_gather | solution.py:117
  67.4 354.7 %all-gather.15.cloned.1.call-start = ((), (), s32[]{:S(2)}) async-start(), calls=%async_computation.20 | async-start | bytes 15728640 | tf_op jit(solution)/shard_map/all_gather | solution.py:115
  68.0 503.4 %all-gather.17.cloned.1.call-start = ((), (), s32[]{:S(2)}) async-start(), calls=%async_computation.21 | async-start | bytes 10485760 | tf_op jit(solution)/shard_map/all_gather | solution.py:118
  101.5 391.5 %copy-start = (pred[256,2304]{1,0:T(8,128)(4,1)}, pred[256,2304]{1,0:T(8,128)(4,1)S(1)}, u32[]{:S(2)}) copy-start(pred[256,2304]{1,0:T(8,128)(4,1)S(1)} %compare_and_fusion) | copy-start | bytes 1769476
  101.7 101.7 %copy-start.57 = (bf16[256,512]{1,0:T(8,128)(2,1)}, bf16[256,512]{1,0:T(8,128)(2,1)S(1)}, u32[]{:S(2)}) copy-start(bf16[256,512]{1,0:T(8,128)(2,1)S(1)} %copy.98) | copy-start | bytes 786436
  101.9 328.3 %copy-start.49 = (f32[256,32]{0,1:T(8,128)}, f32[256,32]{0,1:T(8,128)S(1)}, u32[]{:S(2)}) copy-start(f32[256,32]{0,1:T(8,128)S(1)} %get-tuple-element.47) | copy-start | bytes 98308
  101.9 328.3 %copy-start.51 = (f32[256,32]{0,1:T(8,128)}, f32[256,32]{0,1:T(8,128)S(1)}, u32[]{:S(2)}) copy-start(f32[256,32]{0,1:T(8,128)S(1)} %get-tuple-element.48) | copy-start | bytes 98308
  101.9 328.5 %copy-start.53 = (bf16[256,32]{0,1:T(8,128)(2,1)}, bf16[256,32]{0,1:T(8,128)(2,1)S(1)}, u32[]{:S(2)}) copy-start(bf16[256,32]{0,1:T(8,128)(2,1)S(1)} %get-tuple-element.39) | copy-start | bytes 49156
  101.9 328.5 %copy-start.55 = (bf16[256,32]{0,1:T(8,128)(2,1)}, bf16[256,32]{0,1:T(8,128)(2,1)S(1)}, u32[]{:S(2)}) copy-start(bf16[256,32]{0,1:T(8,128)(2,1)S(1)} %get-tuple-element.40) | copy-start | bytes 49156
  148.3 282.2 %copy-start.24 = (bf16[2048,64]{0,1:T(8,128)(2,1)}, bf16[2048,64]{0,1:T(8,128)(2,1)S(1)}, u32[]{:S(2)}) copy-start(bf16[2048,64]{0,1:T(8,128)(2,1)S(1)} %copy.104) | copy-start | bytes 786436
  239.0 183.1 %copy-start.5 = (bf16[256,2048]{1,0:T(8,128)(2,1)S(1)}, bf16[256,2048]{1,0:T(8,128)(2,1)}, u32[]{:S(2)}) copy-start(bf16[256,2048]{1,0:T(8,128)(2,1)} %param.19) | copy-start | bytes 3145732
  239.0 183.1 %copy-start.47 = (f32[2048]{0:T(1024)S(1)}, f32[2048]{0:T(1024)}, u32[]{:S(2)}) copy-start(f32[2048]{0:T(1024)} %param.21) | copy-start | bytes 24580
  513.5 63.7 %copy-start.21 = (bf16[16,128,256]{2,1,0:T(8,128)(2,1)}, bf16[16,128,256]{2,1,0:T(8,128)(2,1)S(1)}, u32[]{:S(2)}) copy-start(bf16[16,128,256]{2,1,0:T(8,128)(2,1)S(1)} %fusion.54) | copy-start | bytes 3145732
  578.8 412.1 %copy-start.2 = (bf16[256,2048]{1,0:T(8,128)(2,1)}, bf16[256,2048]{1,0:T(8,128)(2,1)S(1)}, u32[]{:S(2)}) copy-start(bf16[256,2048]{1,0:T(8,128)(2,1)S(1)} %multiply_convert_fusion.9) | copy-start | bytes 3145732
  589.0 440.8 %all-to-all-start = ((bf16[16,144,2048]{2,1,0:T(8,128)(2,1)}), bf16[16,144,2048]{2,1,0:T(8,128)(2,1)}, u32[]{:S(2)}, u32[]{:S(2)}) async-start(bf16[16,144,2048]{2,1,0:T(8,128)(2,1)} %bitcast.177), calls=%async_computation | async-start | bytes 18874368 | tf_op jit(solution)/shard_map/all_to_all | solution.py:83
  593.9 1285.8 %all-gather.23.cloned.1.call-start = ((), (), s32[]{:S(2)}) async-start(), calls=%async_computation.24 | async-start | bytes 14417920 | tf_op jit(solution)/shard_map/all_gather | solution.py:178
  602.5 389.7 %copy-start.39 = (s32[256,6]{1,0:T(8,128)S(1)}, s32[256,6]{1,0:T(8,128)}, u32[]{:S(2)}) copy-start(s32[256,6]{1,0:T(8,128)} %copy-done.38) | copy-start | bytes 18436
  1029.8 397.3 %all-to-all-start.2 = ((bf16[16,144,2048]{2,1,0:T(8,128)(2,1)}), bf16[16,144,2048]{2,1,0:T(8,128)(2,1)}, u32[]{:S(2)}, u32[]{:S(2)}) async-start(bf16[16,144,2048]{2,1,0:T(8,128)(2,1)} %bitcast.178), calls=%async_computation.2 | async-start | bytes 18874368 | tf_op jit(solution)/shard_map/all_to_all | solution.py:83
  1034.9 854.0 %all-gather.21.cloned.1.call-start = ((), (), s32[]{:S(2)}) async-start(), calls=%async_computation.23 | async-start | bytes 14417920 | tf_op jit(solution)/shard_map/all_gather | solution.py:177
  1477.0 397.0 %all-to-all-start.1 = ((bf16[16,144,2048]{2,1,0:T(8,128)(2,1)}), bf16[16,144,2048]{2,1,0:T(8,128)(2,1)}, u32[]{:S(2)}, u32[]{:S(2)}) async-start(bf16[16,144,2048]{2,1,0:T(8,128)(2,1)} %bitcast.187), calls=%async_computation.1 | async-start | bytes 18874368 | tf_op jit(solution)/shard_map/all_to_all | solution.py:83
  1481.9 415.9 %all-gather.19.cloned.1.call-start = ((), (), s32[]{:S(2)}) async-start(), calls=%async_computation.22 | async-start | bytes 14417920 | tf_op jit(solution)/shard_map/all_gather | solution.py:176
  1874.0 211.7 %all-to-all-start.3 = ((bf16[16,144,2048]{2,1,0:T(8,128)(2,1)}), bf16[16,144,2048]{2,1,0:T(8,128)(2,1)}, u32[]{:S(2)}, u32[]{:S(2)}) async-start(bf16[16,144,2048]{2,1,0:T(8,128)(2,1)} %bitcast.186), calls=%async_computation.3 | async-start | bytes 18874368 | tf_op jit(solution)/shard_map/all_to_all | solution.py:83
  1879.0 603.0 %reduce-scatter.18.cloned.1.call-start = ((), (), s32[]{:S(2)}) async-start(), calls=%async_computation.26 | async-start | bytes 557056 | tf_op jit(solution)/shard_map/reduce_scatter | solution.py:341
  1962.9 162.5 %copy-start.65 = (bf16[256,16]{0,1:T(8,128)(2,1)}, bf16[256,16]{0,1:T(8,128)(2,1)S(1)}, u32[]{:S(2)}) copy-start(bf16[256,16]{0,1:T(8,128)(2,1)S(1)} %fusion.105) | copy-start | bytes 24580
  2260.7 222.3 %reduce-scatter.16.cloned.1.call-start = ((), (), s32[]{:S(2)}) async-start(), calls=%async_computation.25 | async-start | bytes 4456448 | tf_op jit(solution)/shard_map/reduce_scatter | solution.py:338
  2386.1 199.4 %reduce-scatter.38.cloned.1.call-start = ((), (), s32[]{:S(2)}) async-start(), calls=%async_computation.36 | async-start | bytes 8650752 | tf_op jit(solution)/shard_map/reduce_scatter | solution.py:393
  2406.1 198.3 %reduce-scatter.36.cloned.1.call-start = ((), (), s32[]{:S(2)}) async-start(), calls=%async_computation.35 | async-start | bytes 8650752 | tf_op jit(solution)/shard_map/reduce_scatter | solution.py:390
  2426.6 252.1 %reduce-scatter.34.cloned.1.call-start = ((), (), s32[]{:S(2)}) async-start(), calls=%async_computation.34 | async-start | bytes 8650752 | tf_op jit(solution)/shard_map/reduce_scatter | solution.py:387
  2447.0 369.3 %reduce-scatter.40.cloned.1.call-start = ((), (), s32[]{:S(2)}) async-start(), calls=%async_computation.37 | async-start | bytes 1081344
  2449.8 861.2 %reduce-scatter.30.cloned.1.call-start = ((), (), s32[]{:S(2)}) async-start(), calls=%async_computation.32 | async-start | bytes 23789568 | tf_op jit(solution)/shard_map/reduce_scatter | solution.py:380
  2459.3 1347.4 %reduce-scatter.28.cloned.1.call-start = ((), (), s32[]{:S(2)}) async-start(), calls=%async_computation.31 | async-start | bytes 23789568 | tf_op jit(solution)/shard_map/reduce_scatter | solution.py:379
  2470.7 1831.9 %reduce-scatter.32.cloned.1.call-start = ((), (), s32[]{:S(2)}) async-start(), calls=%async_computation.33 | async-start | bytes 23789568 | tf_op jit(solution)/shard_map/reduce_scatter | solution.py:381
  2481.9 1976.2 %reduce-scatter.22.cloned.1.call-start = ((), (), s32[]{:S(2)}) async-start(), calls=%async_computation.28 | async-start | bytes 5406720 | tf_op jit(solution)/shard_map/reduce_scatter | solution.py:370
  2489.8 2155.7 %reduce-scatter.24.cloned.1.call-start = ((), (), s32[]{:S(2)}) async-start(), calls=%async_computation.29 | async-start | bytes 8650752 | tf_op jit(solution)/shard_map/reduce_scatter | solution.py:374
  2530.7 2479.3 %reduce-scatter.26.cloned.1.call-start = ((), (), s32[]{:S(2)}) async-start(), calls=%async_computation.30 | async-start | bytes 17301504 | tf_op jit(solution)/shard_map/reduce_scatter | solution.py:375
  2542.4 2718.1 %reduce-scatter.20.cloned.1.call-start = ((), (), s32[]{:S(2)}) async-start(), calls=%async_computation.27 | async-start | bytes 25952256 | tf_op jit(solution)/shard_map/reduce_scatter | solution.py:369
  2609.1 74.3 %copy-start.42 = (f32[256,1,6]{2,1,0:T(1,128)S(1)}, f32[256,1,6]{2,1,0:T(1,128)}, u32[]{:S(2)}) copy-start(f32[256,1,6]{2,1,0:T(1,128)} %copy-done.41) | copy-start | bytes 18436
  2700.9 116.8 %copy-start.31 = (bf16[256,512]{0,1:T(8,128)(2,1)S(1)}, bf16[256,512]{0,1:T(8,128)(2,1)}, u32[]{:S(2)}) copy-start(bf16[256,512]{0,1:T(8,128)(2,1)} %copy-done.30) | copy-start | bytes 786436
  2709.9 112.8 %copy-start.71 = (f32[2048]{0:T(1024)S(1)}, f32[2048]{0:T(1024)}, u32[]{:S(2)}) copy-start(f32[2048]{0:T(1024)} %get-tuple-element.16) | copy-start | bytes 24580
  (77 other events, 741.0 us)
Sparse Core Ops, SparseCore 0:
  9.6 53.1 all-gather.8
  66.8 54.9 all-gather.10
  123.3 80.0 all-gather.12
  204.8 217.2 all-gather.14
  423.5 147.8 all-gather.16
  596.0 382.6 all-gather.22
  1037.3 382.0 all-gather.20
  1484.4 381.9 all-gather.18
  2260.9 54.3 reduce-scatter.17
  2386.2 70.5 reduce-scatter.15
  2459.6 70.4 reduce-scatter.37
  2533.0 71.3 reduce-scatter.35
  2607.2 71.3 reduce-scatter.33
  2680.9 135.4 reduce-scatter.39
  2819.0 491.9 reduce-scatter.29
  3313.7 492.9 reduce-scatter.27
  3809.5 493.0 reduce-scatter.31
  4305.3 152.7 reduce-scatter.21
  4461.0 184.4 reduce-scatter.23
  4648.2 361.8 reduce-scatter.25
  5017.1 243.3 reduce-scatter.19
where the time goes:
time: 5280 us; the launch traced here: 5270 us
  waiting for transfers between devices  3730 us (71%)
  matrix products  650 us (12%)
  blocking collectives  451 us (9%)
  local copies, waits for them, and re-layouts  228 us (4%)
  other arithmetic  172 us (3%)
    all_to_all x4, waiting for transfers between devices, trade(): lax.all_to_all(buffer, ('expert', 'shard'), split_axis=0, concat_axis=0,...  823 us
    reduce_scatter x1, waiting for transfers between devices, per_device(): lax.psum_scatter(grad_sd, ('group', 'expert', 'shard'), scatter_dimension...  496 us
    reduce_scatter x1, waiting for transfers between devices, per_device(): lax.psum_scatter(grad_sg, ('group', 'expert', 'shard'), scatter_dimension...  496 us
    reduce_scatter x1, waiting for transfers between devices, per_device(): lax.psum_scatter(grad_su, ('group', 'expert', 'shard'), scatter_dimension...  443 us
    all_gather x1, blocking collectives, per_device(): lax.all_gather(w_router, 'shard', axis=0, tiled=True)  372 us
    reduce_scatter x1, waiting for transfers between devices, per_device(): lax.psum_scatter(grad_wo, ('group', 'expert', 'shard'), scatter_dimension...  365 us
    reduce_scatter x1, waiting for transfers between devices, per_device(): lax.psum_scatter(grad_wq, ('group', 'expert', 'shard'), scatter_dimension...  250 us
    reduce_scatter x1, waiting for transfers between devices, per_device(): lax.psum_scatter(grad_wkv, ('group', 'expert', 'shard'), scatter_dimensio...  187 us
  transfers between devices with their start and end apart: 25, of which 17 were waited for; matrix products, arithmetic and copies ran while one was open for 16% of the time, Pallas kernels for 0%

commit v1 on v0

v1 whole, which is shorter than its diff:
```python
import functools
import math

import jax
import jax.numpy as jnp
from jax import lax
from jax.experimental import pallas as pl
from jax.experimental.pallas import tpu as pltpu
from jax.sharding import PartitionSpec as P

HEADS = 16
NOPE = 128
ROPE = 64
VDIM = 128
LATENT = 512
BLOCK = 256
PROMPT = 2048
NCONT = 8
QDIM = NOPE + ROPE
KVDIM = NOPE + VDIM
GROUP_BLOCKS = PROMPT // BLOCK + NCONT
GROUP_TOK = GROUP_BLOCKS * BLOCK

EPS = 1e-06
ALL = ("group", "expert", "shard")
ROW = ("expert", "shard")
SCALE = 1.0 / math.sqrt(NOPE + ROPE)
F32 = jnp.float32
BF16 = jnp.bfloat16


def matmul(left, right):
    return jnp.dot(left, right, preferred_element_type=F32)


def matmul_nt(left, right):
    return lax.dot_general(left, right, (((1,), (1,)), ((), ())), preferred_element_type=F32)


def matmul_tn(left, right):
    return lax.dot_general(left, right, (((0,), (0,)), ((), ())), preferred_element_type=F32)


def rms_parts(values):
    inverse = lax.rsqrt(jnp.mean(values * values, axis=-1, keepdims=True) + EPS)
    return (values * inverse, inverse)


def norm_back(grad_in, normed, inverse, gain):
    scaled = grad_in * gain
    gain_grad = jnp.sum(grad_in * normed, axis=0)
    input_grad = inverse * (scaled - normed * jnp.mean(scaled * normed, axis=-1, keepdims=True))
    return (input_grad, gain_grad)


def angles(pos_list, rot_width):
    half_width = rot_width // 2
    freq = 10000.0 ** (-2.0 * jnp.arange(half_width, dtype=F32) / rot_width)
    theta = pos_list.astype(F32)[:, None] * freq[None, :]
    return (jnp.cos(theta), jnp.sin(theta))


def rotate(values, cosine, sine):
    half_width = values.shape[-1] // 2
    first_half = values[..., :half_width]
    second_half = values[..., half_width:]
    return jnp.concatenate(
        [first_half * cosine - second_half * sine, second_half * cosine + first_half * sine],
        axis=-1,
    )


def unrotate(grad_in, cosine, sine):
    return rotate(grad_in, cosine, -sine)


def silu_parts(values):
    sigmoid = jax.nn.sigmoid(values)
    return (values * sigmoid, sigmoid * (1.0 + values * (1.0 - sigmoid)))


def trade(buffer, axes):
    return lax.all_to_all(buffer, axes, split_axis=0, concat_axis=0, tiled=True)


def take_blocks(blocks, index):
    shape = blocks.shape[1:]

    def body(index_ref, src_ref, dst_ref):
        dst_ref[...] = src_ref[...]

    return pl.pallas_call(
        body,
        grid_spec=pltpu.PrefetchScalarGridSpec(
            num_scalar_prefetch=1,
            grid=(index.shape[0],),
            in_specs=[pl.BlockSpec((1,) + shape, lambda i, at: (at[i], 0, 0))],
            out_specs=pl.BlockSpec((1,) + shape, lambda i, at: (i, 0, 0)),
        ),
        out_shape=jax.ShapeDtypeStruct((index.shape[0],) + shape, blocks.dtype),
        name="take_blocks",
    )(index, blocks)


def causal(count):
    rows = lax.broadcasted_iota(jnp.int32, (count, count), 0)
    cols = lax.broadcasted_iota(jnp.int32, (count, count), 1)
    return cols <= rows


def attend(query, key, value):
    q_p, q_c = query[:PROMPT], query[PROMPT:]
    k_p, k_c = key[:PROMPT], key[PROMPT:]
    v_p, v_c = value[:PROMPT], value[PROMPT:]
    own = lambda a: a.reshape(NCONT, BLOCK, a.shape[-1])
    s_p = jnp.where(causal(PROMPT), matmul_nt(q_p, k_p) * SCALE, -jnp.inf)
    s_cp = matmul_nt(q_c, k_p) * SCALE
    s_cc = jnp.einsum("cqd,ckd->cqk", own(q_c), own(k_c), preferred_element_type=F32) * SCALE
    s_cc = jnp.where(causal(BLOCK)[None], s_cc, -jnp.inf)
    m_p = jnp.max(s_p, axis=-1, keepdims=True)
    e_p = jnp.exp(s_p - m_p)
    z_p = jnp.sum(e_p, axis=-1, keepdims=True)
    o_p = matmul((e_p / z_p).astype(BF16), v_p)
    m_c = jnp.maximum(
        jnp.max(s_cp, axis=-1, keepdims=True),
        jnp.max(s_cc, axis=-1, keepdims=True).reshape(NCONT * BLOCK, 1),
    )
    e_cp = jnp.exp(s_cp - m_c)
    e_cc = jnp.exp(s_cc - own(m_c))
    z_c = jnp.sum(e_cp, axis=-1, keepdims=True) + jnp.sum(e_cc, axis=-1, keepdims=True).reshape(
        NCONT * BLOCK, 1
    )
    o_c = matmul((e_cp / z_c).astype(BF16), v_p) + jnp.einsum(
        "cqk,ckd->cqd", (e_cc / own(z_c)).astype(BF16), own(v_c), preferred_element_type=F32
    ).reshape(NCONT * BLOCK, VDIM)
    total = jnp.concatenate([m_p + jnp.log(z_p), m_c + jnp.log(z_c)], axis=0)
    return jnp.concatenate([o_p, o_c], axis=0), total


def attend_back(query, key, value, mixed, total, grad_mixed):
    delta = jnp.sum(grad_mixed.astype(F32) * mixed, axis=-1, keepdims=True)
    own = lambda a: a.reshape(NCONT, BLOCK, a.shape[-1])
    flat = lambda a: a.reshape(NCONT * BLOCK, a.shape[-1])
    q_p, q_c = query[:PROMPT], query[PROMPT:]
    k_p, k_c = key[:PROMPT], key[PROMPT:]
    v_p, v_c = value[:PROMPT], value[PROMPT:]
    g_p, g_c = grad_mixed[:PROMPT], grad_mixed[PROMPT:]
    t_p, t_c = total[:PROMPT], total[PROMPT:]
    d_p, d_c = delta[:PROMPT], delta[PROMPT:]

    def part(q, k, v, g, t, d, mask):
        batch = "c" if q.ndim == 3 else ""
        prob = jnp.exp(
            jnp.einsum(f"{batch}qd,{batch}kd->{batch}qk", q, k, preferred_element_type=F32) * SCALE
            - t
        )
        if mask is not None:
            prob = jnp.where(mask, prob, 0.0)
        grad_p = jnp.einsum(f"{batch}qd,{batch}kd->{batch}qk", g, v, preferred_element_type=F32)
        grad_s = (prob * (grad_p - d)).astype(BF16)
        back = f"{batch}qk,{batch}qd->{batch}kd"
        grad_v = jnp.einsum(back, prob.astype(BF16), g, preferred_element_type=F32)
        grad_k = jnp.einsum(back, grad_s, q, preferred_element_type=F32) * SCALE
        grad_q = (
            jnp.einsum(f"{batch}qk,{batch}kd->{batch}qd", grad_s, k, preferred_element_type=F32)
            * SCALE
        )
        return grad_q, grad_k, grad_v

    gq_p, gk_p, gv_p = part(q_p, k_p, v_p, g_p, t_p, d_p, causal(PROMPT))
    gq_1, gk_1, gv_1 = part(q_c, k_p, v_p, g_c, t_c, d_c, None)
    gq_2, gk_2, gv_2 = part(
        own(q_c), own(k_c), own(v_c), own(g_c), own(t_c), own(d_c), causal(BLOCK)[None]
    )
    join = lambda a, b: jnp.concatenate([a, b], axis=0)
    return (
        join(gq_p, gq_1 + flat(gq_2)),
        join(gk_p + gk_1, flat(gk_2)),
        join(gv_p + gv_1, flat(gv_2)),
    )


def places_of(hit):
    grid = hit.reshape(-1, 128)
    rows = grid.shape[0]
    upper = (
        lax.broadcasted_iota(jnp.int32, (128, 128), 0)
        < lax.broadcasted_iota(jnp.int32, (128, 128), 1)
    ).astype(BF16)
    lower = (
        lax.broadcasted_iota(jnp.int32, (rows, rows), 1)
        < lax.broadcasted_iota(jnp.int32, (rows, rows), 0)
    ).astype(BF16)
    inside = matmul(grid.astype(BF16), upper)
    sums = jnp.sum(grid, axis=1, keepdims=True).astype(BF16)
    ahead = matmul(lower, sums)
    return (inside + ahead).astype(jnp.int32).reshape(-1)


def per_device(
    sizes,
    tokens,
    cotangent,
    gain_attn,
    w_query,
    w_latent,
    gain_latent,
    w_keyval,
    w_output,
    gain_ffn,
    w_shared_gate,
    w_shared_up,
    w_shared_down,
    w_router,
    expert_gate,
    expert_up,
    expert_down,
    segments,
    positions,
    routes,
):
    n_group, n_expert, n_shard = sizes
    n_row = n_expert * n_shard
    n_all = n_group * n_row
    tok_rows, width = tokens.shape
    row_tokens = segments.shape[0]
    n_prompt = row_tokens // GROUP_TOK
    e_per_prompt = n_expert // n_prompt
    group_at = lax.axis_index("group")
    expert_at = lax.axis_index("expert")
    shard_at = lax.axis_index("shard")
    row_at = expert_at * n_shard + shard_at
    prompt_at = expert_at // e_per_prompt
    head_group = expert_at % e_per_prompt

    seg_block = segments[::BLOCK]
    pos_block = positions[::BLOCK]
    prompt_of = seg_block // (NCONT + 1)
    prompt_of = prompt_of - jnp.min(prompt_of)
    cont_of = seg_block % (NCONT + 1)
    piece = jnp.where(cont_of == 0, pos_block // BLOCK, PROMPT // BLOCK - 1 + cont_of)
    slot_of = prompt_of * GROUP_BLOCKS + piece
    block_ids = jnp.arange(n_row, dtype=jnp.int32)
    block_at = jnp.sum(
        jnp.where(slot_of[None, :] == block_ids[:, None], block_ids[None, :], 0), axis=1
    )
    my_blocks = lax.dynamic_slice_in_dim(block_at, prompt_at * GROUP_BLOCKS, GROUP_BLOCKS)
    local_slot = slot_of - prompt_at * GROUP_BLOCKS
    mine = (local_slot >= 0) & (local_slot < GROUP_BLOCKS)
    local_slot = jnp.clip(local_slot, 0, GROUP_BLOCKS - 1)
    own_prompt = jnp.sum(jnp.where(block_ids == row_at, prompt_of, 0))

    def to_pieces(all_rows):
        return take_blocks(all_rows.reshape(n_row, BLOCK, -1), my_blocks).reshape(GROUP_TOK, -1)

    def from_pieces(rows, clear=False):
        picked = take_blocks(rows.reshape(GROUP_BLOCKS, BLOCK, -1), local_slot)
        if clear and n_prompt > 1:
            picked = jnp.where(mine[:, None, None], picked, jnp.zeros_like(picked))
        return picked

    def heads_home(rows):
        got = trade(from_pieces(rows), ROW)
        if n_prompt > 1:
            got = lax.dynamic_slice_in_dim(got, own_prompt * GROUP_BLOCKS, GROUP_BLOCKS)
        return jnp.swapaxes(got, 0, 1).reshape(BLOCK, -1)

    def heads_out(rows):
        split = jnp.swapaxes(rows.reshape(BLOCK, HEADS, -1), 0, 1)
        if n_prompt > 1:
            split = jnp.tile(split, (n_prompt, 1, 1))
            keep = (block_ids // GROUP_BLOCKS) == own_prompt
            split = jnp.where(keep[:, None, None], split, jnp.zeros_like(split))
        return to_pieces(trade(split, ROW))

    def head_columns(weight, per_head):
        cols = lax.dynamic_slice_in_dim(
            weight, head_group * (n_shard * per_head), n_shard * per_head, axis=1
        )
        cols = jnp.swapaxes(cols.reshape(-1, n_shard, per_head), 0, 1)
        return trade(cols, "shard").reshape(-1, per_head)

    def unit_columns(weight):
        units = weight.shape[1] // n_row
        cols = weight.reshape(weight.shape[0], n_shard, n_expert, units)
        cols = lax.dynamic_index_in_dim(cols, expert_at, axis=2, keepdims=False)
        return jnp.swapaxes(cols, 0, 1)

    def gather_rows(weight):
        part = weight.shape[0] // (n_group * n_expert)
        at = (group_at * n_expert + expert_at) * part
        return lax.all_gather(
            lax.dynamic_slice_in_dim(weight, at, part), ("shard", "group", "expert"), tiled=True
        )

    tok_all = lax.all_gather(tokens, ROW, axis=0, tiled=True)
    routes_all = lax.all_gather(routes, ROW, axis=0, tiled=True)
    w_l = lax.all_gather(w_latent, "shard", axis=0, tiled=True)
    w_r = lax.all_gather(w_router, "shard", axis=0, tiled=True)
    wq_h = head_columns(w_query, QDIM)
    wkv_h = head_columns(w_keyval, KVDIM)
    units = w_shared_gate.shape[1] // n_row
    w_gu = trade(
        jnp.concatenate([unit_columns(w_shared_gate), unit_columns(w_shared_up)], axis=-1), "shard"
    ).reshape(width, 2 * units)
    w_sd = lax.dynamic_slice_in_dim(w_shared_down, expert_at * units, units)
    w_o = gather_rows(w_output)
    c_all = lax.all_gather(cotangent, ROW, axis=0, tiled=True)
    w_q = gather_rows(w_query)

    expert_count = w_r.shape[1]
    top_count = routes.shape[1]
    capacity = n_row * (3 * tok_rows * top_count // (2 * expert_count))
    hit = jnp.any(routes_all == row_at, axis=1)
    place = places_of(hit.astype(F32))
    count = jnp.sum(hit.astype(jnp.int32))
    token_of = (
        jnp.zeros((capacity,), jnp.int32)
        .at[jnp.where(hit, place, capacity)]
        .set(jnp.arange(row_tokens, dtype=jnp.int32), mode="drop")
    )
    filled = jnp.arange(capacity, dtype=jnp.int32) < count
    place = jnp.where(hit, place, 0)

    tok_p = to_pieces(tok_all).astype(F32)
    hidden1 = (rms_parts(tok_p)[0] * gain_attn).astype(BF16)
    pos_p = jnp.arange(GROUP_TOK, dtype=jnp.int32)
    pos_p = jnp.where(pos_p < PROMPT, pos_p, PROMPT + pos_p % BLOCK)
    cos_p, sin_p = angles(pos_p, ROPE)
    joint = matmul(hidden1, jnp.concatenate([wq_h, w_l], axis=1))
    query_f, latent_f = joint[:, :QDIM], joint[:, QDIM:]
    query = jnp.concatenate(
        [query_f[:, :NOPE], rotate(query_f[:, NOPE:], cos_p, sin_p)], axis=1
    ).astype(BF16)
    comp = (rms_parts(latent_f[:, :LATENT])[0] * gain_latent).astype(BF16)
    key_rope = rotate(latent_f[:, LATENT:], cos_p, sin_p).astype(BF16)
    keyval = matmul(comp, wkv_h).astype(BF16)
    key = jnp.concatenate([keyval[:, :NOPE], key_rope], axis=1)
    value = keyval[:, NOPE:]
    mixed_h, total_h = attend(query, key, value)
    mixed = heads_home(mixed_h.astype(BF16))

    inputs = tokens.astype(F32)
    grad_out = cotangent.astype(F32)
    normed1, inverse1 = rms_parts(inputs)
    hidden1_own = (normed1 * gain_attn).astype(BF16)
    latent_own = matmul(hidden1_own, w_l)
    normed_c, inverse_c = rms_parts(latent_own[:, :LATENT])
    after = inputs + matmul(mixed, w_o)
    normed2, inverse2 = rms_parts(after)
    hidden2 = (normed2 * gain_ffn).astype(BF16)
    logits = matmul(hidden2, w_r)
    router_prob = jax.nn.softmax(logits, axis=-1)

    h2_all = lax.all_gather(hidden2, ROW, axis=0, tiled=True)
    wide = matmul(h2_all, jnp.concatenate([w_gu, w_r], axis=1))
    s_gate, s_up = wide[:, :units], wide[:, units : 2 * units]
    prob_all = jax.nn.softmax(wide[:, 2 * units :], axis=-1)
    my_col = (jnp.arange(expert_count) == row_at).astype(F32)
    weight_of = jnp.sum(prob_all * my_col[None, :], axis=1) * hit.astype(F32)
    s_act, s_slope = silu_parts(s_gate)
    s_mid = (s_act * s_up).astype(BF16)
    shared = matmul(s_mid, w_sd)
    rows = h2_all[token_of]
    c_rows = c_all[token_of]
    w_rows = jnp.where(filled, weight_of[token_of], 0.0)
    d_out = (w_rows[:, None] * c_rows.astype(F32)).astype(BF16)
    e_gate = matmul(rows, expert_gate[0])
    e_up = matmul(rows, expert_up[0])
    e_act, e_slope = silu_parts(e_gate)
    e_mid = (e_act * e_up).astype(BF16)
    e_out = matmul(e_mid, expert_down[0]).astype(BF16)
    picked = jnp.where(hit[:, None], e_out[place].astype(F32), 0.0)
    out_part = (weight_of[:, None] * picked + shared).astype(BF16)
    d_prob_col = jnp.sum(c_all.astype(F32) * picked, axis=1)
    ffn = lax.psum_scatter(out_part, ROW, scatter_dimension=0, tiled=True)
    output = (after + ffn.astype(F32)).astype(BF16)

    d_mid = matmul_nt(d_out, expert_down[0])
    d_gate = (d_mid * e_up * e_slope).astype(BF16)
    d_up = (d_mid * e_act).astype(BF16)
    d_rows = (matmul_nt(d_gate, expert_gate[0]) + matmul_nt(d_up, expert_up[0])).astype(BF16)
    ds_mid = matmul_nt(c_all, w_sd)
    ds_gate = (ds_mid * s_up * s_slope).astype(BF16)
    ds_up = (ds_mid * s_act).astype(BF16)
    ds_gu = jnp.concatenate([ds_gate, ds_up], axis=1)
    dh_part = jnp.where(hit[:, None], d_rows[place].astype(F32), 0.0) + matmul_nt(ds_gu, w_gu)
    d_h2 = lax.psum_scatter(dh_part.astype(BF16), ROW, scatter_dimension=0, tiled=True)
    d_prob = trade(d_prob_col.reshape(n_row, tok_rows), ROW).T
    route_hot = jnp.any(
        routes[:, :, None] == jnp.arange(expert_count, dtype=jnp.int32)[None, None, :], axis=1
    )
    d_prob = jnp.where(route_hot, d_prob, 0.0)
    d_logits = (
        router_prob * (d_prob - jnp.sum(router_prob * d_prob, axis=-1, keepdims=True))
    ).astype(BF16)
    grad_router = matmul_tn(hidden2, d_logits)

    def group_sum(left, right):
        whole = matmul_tn(left, right)
        half = whole.shape[0] // n_group
        if n_group != 2:
            return lax.psum_scatter(
                whole.astype(BF16), "group", scatter_dimension=0, tiled=True
            ).astype(F32)[None]
        send = lax.dynamic_slice_in_dim(whole, (1 - group_at) * half, half).astype(BF16)
        keep = lax.dynamic_slice_in_dim(whole, group_at * half, half)
        return (keep + lax.ppermute(send, "group", [(0, 1), (1, 0)]).astype(F32))[None]

    egrad_gate = group_sum(rows, d_gate)
    egrad_up = group_sum(rows, d_up)
    egrad_down = group_sum(e_mid, d_out)

    grad_gu = matmul_tn(h2_all, ds_gu).astype(BF16).reshape(n_all, width // n_all, 2 * units)
    got = trade(grad_gu, ALL).astype(F32)
    got = jnp.sum(got.reshape(n_group, n_expert, n_shard, -1, 2 * units), axis=0)
    got = jnp.transpose(got, (2, 1, 0, 3))
    grad_sg = got[..., :units].reshape(got.shape[0], -1)
    grad_su = got[..., units:].reshape(got.shape[0], -1)
    grad_sd_part = matmul_tn(s_mid, c_all).astype(BF16).reshape(n_group, units // n_group, width)
    grad_sd = 0.0
    for turn in range(n_group):
        piece_at = (group_at + turn) % n_group
        moves = []
        for g in range(n_group):
            for e in range(n_expert):
                for s in range(n_shard):
                    target = (s * n_expert + e) * n_group + (g + turn) % n_group
                    moves.append(((g * n_expert + e) * n_shard + s, target))
        sent = lax.dynamic_index_in_dim(grad_sd_part, piece_at, axis=0, keepdims=False)
        grad_sd = grad_sd + lax.ppermute(sent, ALL, moves).astype(F32)

    d_hidden2 = d_h2.astype(F32) + matmul_nt(d_logits, w_r)
    d_after, grad_gain_ffn = norm_back(d_hidden2, normed2, inverse2, gain_ffn)
    grad_after = grad_out + d_after
    grad_attn = grad_after.astype(BF16)
    d_mixed = matmul_nt(grad_attn, w_o).astype(BF16)
    d_mixed_h = heads_out(d_mixed)
    grad_wo = lax.psum_scatter(
        matmul_tn(mixed, grad_attn).astype(BF16), ALL, scatter_dimension=0, tiled=True
    ).astype(F32)

    d_query, d_key, d_value = attend_back(query, key, value, mixed_h, total_h, d_mixed_h)
    d_query = jnp.concatenate(
        [d_query[:, :NOPE], unrotate(d_query[:, NOPE:], cos_p, sin_p)], axis=1
    ).astype(BF16)
    d_keyval = jnp.concatenate([d_key[:, :NOPE], d_value], axis=1).astype(BF16)
    d_comp = matmul_nt(d_keyval, wkv_h)
    d_latent_part = jnp.concatenate([d_comp, d_key[:, NOPE:]], axis=1).astype(BF16)
    d_lat = lax.psum_scatter(
        from_pieces(d_latent_part, clear=True).reshape(row_tokens, LATENT + ROPE),
        ROW,
        scatter_dimension=0,
        tiled=True,
    ).astype(F32)
    d_query_own = heads_home(d_query)

    grad_wq_h = matmul_tn(hidden1, d_query).astype(BF16).reshape(n_all, width // n_all, QDIM)
    grad_wkv_h = matmul_tn(comp, d_keyval).astype(BF16)
    grad_wkv_h = grad_wkv_h.reshape(n_all, width // n_all, -1)
    got = trade(jnp.concatenate([grad_wq_h, grad_wkv_h], axis=-1), ALL).astype(F32)
    got = jnp.sum(got.reshape(n_group * n_prompt, HEADS, got.shape[1], got.shape[2]), axis=0)
    grad_wq = jnp.swapaxes(got[..., :QDIM], 0, 1).reshape(got.shape[1], -1)
    grad_wkv = jnp.swapaxes(
        got[..., QDIM:].reshape(HEADS, LATENT // n_all, KVDIM), 0, 1
    ).reshape(LATENT // n_all, -1)

    own_pos = lax.dynamic_slice_in_dim(positions, row_at * tok_rows, tok_rows)
    cosine, sine = angles(own_pos, ROPE)
    d_lat_c, grad_gain_latent = norm_back(d_lat[:, :LATENT], normed_c, inverse_c, gain_latent)
    d_latent = jnp.concatenate([d_lat_c, unrotate(d_lat[:, LATENT:], cosine, sine)], axis=1).astype(
        BF16
    )
    d_hidden1 = matmul_nt(d_query_own, w_q) + matmul_nt(d_latent, w_l)
    d_tok, grad_gain_attn = norm_back(d_hidden1, normed1, inverse1, gain_attn)
    grad_tokens = grad_after + d_tok
    grad_wl = lax.psum_scatter(
        matmul_tn(hidden1_own, d_latent).astype(BF16), ALL, scatter_dimension=0, tiled=True
    ).astype(F32)

    small = jnp.concatenate(
        [
            grad_router.reshape(n_all, -1),
            grad_gain_attn.reshape(n_all, -1),
            grad_gain_ffn.reshape(n_all, -1),
            grad_gain_latent.reshape(n_all, -1),
        ],
        axis=1,
    ).reshape(-1)
    small = lax.psum_scatter(small, ALL, scatter_dimension=0, tiled=True)
    own = width // n_all
    at = own * expert_count
    return (
        output,
        grad_tokens,
        small[at : at + own],
        grad_wq,
        grad_wl,
        small[at + 2 * own :],
        grad_wkv,
        grad_wo,
        small[at + own : at + 2 * own],
        grad_sg,
        grad_su,
        grad_sd,
        small[:at].reshape(own, expert_count),
        egrad_gate,
        egrad_up,
        egrad_down,
    )


def solution(mesh):
    sizes = tuple(mesh.shape[name] for name in ALL)
    return jax.shard_map(
        functools.partial(per_device, sizes),
        mesh=mesh,
        in_specs=(
            P(ALL, None),
            P(ALL, None),
            P(),
            P("shard", None),
            P("shard", None),
            P(),
            P("shard", None),
            P("shard", None),
            P(),
            P("shard", None),
            P("shard", None),
            P("shard", None),
            P("shard", None),
            P(ROW, None, None),
            P(ROW, None, None),
            P(ROW, None, None),
            P("group"),
            P("group"),
            P(ALL, None),
        ),
        out_specs=(
            P(ALL, None),
            P(ALL, None),
            P(ALL),
            P(ALL, None),
            P(ALL, None),
            P(ALL),
            P(ALL, None),
            P(ALL, None),
            P(ALL),
            P(ALL, None),
            P(ALL, None),
            P(ALL, None),
            P(ALL, None),
            P(ROW, "group", None),
            P(ROW, "group", None),
            P(ROW, "group", None),
        ),
        check_vma=False,
    )
```

time: 5280 us -> 1970 us (0.37)
  waiting for transfers between devices: 3730 us -> 787 us
  blocking collectives: 451 us -> 144 us
  matrix products: 650 us -> 469 us
  Pallas kernels: 0 us -> 59.1 us
  local copies, waits for them, and re-layouts: 228 us -> 287 us
    reduce_scatter x12 -> x5, waiting for transfers between devices: 2480 us -> 418 us  [the longest x1 177 us: per_device(): ffn = lax.psum_scatter(out_part, ROW, scatter_dimension=0, tiled=True)]
    all_to_all x4 -> x8, waiting for transfers between devices: 823 us -> 131 us  [trade(): return lax.all_to_all(buffer, axes, split_axis=0, concat_axis=0, tiled=True)]
    all_gather x2, blocking collectives: 411 us -> 88.3 us  [the longest x1 74.8 us: per_device(): routes_all = lax.all_gather(routes, ROW, axis=0, tiled=True)]
    dot_general x26 -> x28, matrix products: 416 us -> 209 us  [the longest x14 134 us: matmul(): return jnp.dot(left, right, preferred_element_type=F32)]
    all_gather x8 -> x6, waiting for transfers between devices: 318 us -> 135 us  [the longest x1 81.6 us: per_device(): tok_all = lax.all_gather(tokens, ROW, axis=0, tiled=True)]
    unnamed x22 -> x13, waiting for transfers between devices: 111 us -> 2.05 us
    ppermute x0 -> x5, waiting for transfers between devices: none -> 101 us  [the longest x3 101 us: group_sum(): lax.ppermute(send, 'group', [(0, 1), (1, 0)]).astype(F32)]
    pallas_call x0 -> x5, Pallas kernels: none -> 59.1 us  [take_blocks(): pl.pallas_call(body, grid_spec=pltpu.PrefetchScalarGridSpec(num_scalar_pr...]
  transfers between devices with their start and end apart: 25 -> 25, of which waited for: 17 -> 13; matrix products, arithmetic and copies ran while one was open for 16% -> 33% of each run, Pallas kernels for 0% -> 3%
where the time goes in v1:
time: 1970 us; the launch traced here: 1960 us
  waiting for transfers between devices  787 us (40%)
  matrix products  469 us (24%)
  local copies, waits for them, and re-layouts  287 us (15%)
  other arithmetic  148 us (8%)
  blocking collectives  144 us (7%)
  Pallas kernels  59.1 us (3%)
  starting transfers between devices  47.2 us (2%)
    reduce_scatter x1, waiting for transfers between devices, per_device(): ffn = lax.psum_scatter(out_part, ROW, scatter_dimension=0, tiled=True)  177 us
    reduce_scatter x1, waiting for transfers between devices, per_device(): lax.psum_scatter(matmul_tn(mixed, grad_attn).astype(BF16), ALL, scatter_d...  163 us
    dot_general x12, matrix products, matmul_nt(): lax.dot_general(left, right, (((1,), (1,)), ((), ())), preferred_element_...  150 us
    dot_general x14, matrix products, matmul(): return jnp.dot(left, right, preferred_element_type=F32)  134 us
    all_to_all x8, waiting for transfers between devices, trade(): return lax.all_to_all(buffer, axes, split_axis=0, concat_axis=0, tiled=True)  131 us
    dot_general x10, matrix products, matmul_tn(): lax.dot_general(left, right, (((0,), (0,)), ((), ())), preferred_element_...  110 us
    ppermute x3, waiting for transfers between devices, group_sum(): lax.ppermute(send, 'group', [(0, 1), (1, 0)]).astype(F32)  101 us
    all_gather x1, waiting for transfers between devices, per_device(): tok_all = lax.all_gather(tokens, ROW, axis=0, tiled=True)  81.6 us
  transfers between devices with their start and end apart: 25, of which 13 were waited for; matrix products, arithmetic and copies ran while one was open for 33% of the time, Pallas kernels for 3%

profile of v1, /device:TPU:0, one launch (start us, length us, event | category | flops | bytes accessed | tf_op | source)
XLA Modules:
  0.0 1958.1 jit_solution(10655302525965150984)
XLA Ops:
  22.5 10.7 all-to-all-done.1
  42.5 32.9 %all-to-all-done = bf16[4,512,192]{1,2,0:T(8,128)(2,1)} async-done(((bf16[4,512,192]{1,2,0:T(8,128)(2,1)}), bf16[4,512,192]{1,2,0:T(8,128)(2,1)}, u32[]{:S(2)}, u32[]{:S(2)}) %all-to-all-start) | async-done | bytes 786464 | tf_op jit(solution)/shard_map/all_to_all | solution.py:83
  77.5 81.6 %all-gather.7.cloned.1.call-done = bf16[4096,2048]{1,0:T(8,128)(2,1)} async-done(((bf16[256,2048]{1,0:T(8,128)(2,1)}), bf16[4096,2048]{1,0:T(8,128)(2,1)}) %all-gather.7.cloned.1.call-update) | async-done | bytes 16777232 | tf_op jit(solution)/shard_map/all_gather | solution.py:296
  159.2 18.2 take_blocks.5
  197.0 12.4 all-gather.9.cloned.1.call-done
  209.4 20.3 %fusion.26 = f32[4096,768]{0,1:T(8,128)} fusion(bf16[4096,2048]{1,0:T(8,128)(2,1)} %fusion.1, bf16[2048,576]{0,1:T(8,128)(2,1)} %all-gather.9.cloned.1.call-done, bf16[2048,192]{0,1:T(8,128)(2,1)} %bitcast.233), kind=kOutput, calls=%fused_computation.70 | convolution fusion | flops 12891193344 | bytes 32505856 | tf_op jit(solution)/shard_map/dot_general | solution.py:33
  281.9 9.5 fusion.8
  291.4 10.0 fusion.3
  315.3 9.5 take_blocks.6
  324.9 56.0 %all_to_all.52 = bf16[16,256,128]{2,1,0:T(8,128)(2,1)} all-to-all(bf16[16,256,128]{2,1,0:T(8,128)(2,1)} %take_blocks.6), channel_id=1, replica_groups=mesh['group'=2,'expert'=4,'shard'=4] {'expert','shard'}, dimensions={0} | all-to-all | bytes 2097152 | tf_op jit(solution)/shard_map/all_to_all | solution.py:83
  408.4 74.8 %all_gather.27 = s32[4096,6]{0,1:T(8,128)S(1)} all-gather(s32[256,6]{0,1:T(8,128)S(1)} %copy-done.58), channel_id=1, replica_groups=mesh['group'=2,'expert'=4,'shard'=4] {'expert','shard'}, dimensions={0}, use_global_device_ids=true | all-gather | bytes 104448 | tf_op jit(solution)/shard_map/all_gather | solution.py:297
  483.8 15.5 scatter_custom_fusion
  499.3 13.4 all_gather.29
  516.7 26.3 %gather_fusion.3 = bf16[2304,2048]{1,0:T(8,128)(2,1)} fusion(bf16[4096,2048]{1,0:T(8,128)(2,1)} %all-gather.15.cloned.1.call-done, s32[3072]{0:T(1024)S(1)} %pad_clamp_fusion), kind=kCustom, calls=%fused_computation.3 | custom fusion | bytes 18883584 | tf_op jit(solution)/shard_map/gather | solution.py:365
  543.0 41.1 %all-gather.13.cloned.1.call-done = bf16[4096,2048]{1,0:T(8,128)(2,1)} async-done(((bf16[256,2048]{1,0:T(8,128)(2,1)}), bf16[4096,2048]{1,0:T(8,128)(2,1)}) %all-gather.13.cloned.1.call-update) | async-done | bytes 16777232 | tf_op jit(solution)/shard_map/all_gather | solution.py:355
  584.1 10.4 fusion.68
  597.1 12.3 gather_fusion.2
  609.4 26.2 %gather_fusion = bf16[2304,2048]{1,0:T(8,128)(2,1)} fusion(bf16[4096,2048]{1,0:T(8,128)(2,1)} %all-gather.13.cloned.1.call-done, s32[3072]{0:T(1024)S(1)} %pad_clamp_fusion), kind=kCustom, calls=%fused_computation | custom fusion | bytes 18883584 | tf_op jit(solution)/shard_map/gather | solution.py:364
  635.6 21.0 %fusion.19 = f32[2304,1408]{1,0:T(8,128)} fusion(bf16[2304,2048]{1,0:T(8,128)(2,1)} %gather_fusion, bf16[1,2048,1408]{2,1,0:T(8,128)(2,1)} %param.33), kind=kOutput, calls=%fused_computation.49 | convolution fusion | flops 13287555072 | bytes 28180480 | tf_op jit(solution)/shard_map/dot_general | solution.py:33
  656.6 18.8 fusion.23
  676.1 30.2 %multiply_convert_fusion.3 = (bf16[2304,1408]{1,0:T(8,128)(2,1)}, bf16[2304,1408]{1,0:T(8,128)(2,1)}, bf16[2304,1408]{1,0:T(8,128)(2,1)}) fusion(f32[2304,1408]{1,0:T(8,128)} %fusion.23, f32[2304,1408]{1,0:T(8,128)} %fusion.19, bf16[1,1408,2048]{2,1,0:T(8,128)(2,1)} %param.34, bf16[2304,2048]{1,0:T(8,128)(2,1)} %gather_fusion.3, f32[2304]{0:T(1024)S(1)} %fusion.153), kind=kOutput, calls=%fused_computation.29 | convolution fusion | flops 13350371328 | bytes 60630016 | tf_op jit(solution)/shard_map/dot_general | solution.py:37
  706.3 20.6 %fusion.21 = f32[2304,2048]{1,0:T(8,128)} fusion(bf16[2304,1408]{1,0:T(8,128)(2,1)} %get-tuple-element.129, bf16[1,2048,1408]{2,1,0:T(8,128)(2,1)} %param.32), kind=kOutput, calls=%fused_computation.51 | convolution fusion | flops 13287555072 | bytes 31129600 | tf_op jit(solution)/shard_map/dot_general | solution.py:37
  727.0 22.1 %add_convert_fusion.2 = bf16[2304,2048]{1,0:T(8,128)(2,1)} fusion(f32[2304,2048]{1,0:T(8,128)} %fusion.21, bf16[2304,1408]{1,0:T(8,128)(2,1)} %get-tuple-element.128, bf16[1,2048,1408]{2,1,0:T(8,128)(2,1)} %param.33), kind=kOutput, calls=%fused_computation.14 | convolution fusion | flops 13296992256 | bytes 40566784 | tf_op jit(solution)/shard_map/dot_general | solution.py:37
  749.1 36.3 %gather_fusion.4 = bf16[4096,2048]{1,0:T(8,128)(2,1)} fusion(bf16[2304,2048]{1,0:T(8,128)(2,1)} %add_convert_fusion.2, s32[4096]{0:T(1024)S(1)} %copy-done.44), kind=kCustom, calls=%fused_computation.4 | custom fusion | bytes 33570816 | tf_op jit(solution)/shard_map/gather | solution.py:387
  785.3 12.5 multiply_convert_fusion.10
  797.9 17.9 add_convert_fusion
  815.8 20.3 %convolution_convert_fusion = bf16[2304,2048]{1,0:T(8,128)(2,1)} fusion(bf16[2304,1408]{1,0:T(8,128)(2,1)} %get-tuple-element.130, bf16[1,1408,2048]{2,1,0:T(8,128)(2,1)} %param.34), kind=kOutput, calls=%fused_computation.36 | convolution fusion | flops 13292273664 | bytes 21692416 | tf_op jit(solution)/shard_map/dot_general | solution.py:33
  836.2 37.8 %gather_fusion.1 = bf16[4096,2048]{1,0:T(8,128)(2,1)} fusion(bf16[2304,2048]{1,0:T(8,128)(2,1)} %convolution_convert_fusion, s32[4096]{0:T(1024)S(1)} %copy-done.44), kind=kCustom, calls=%fused_computation.1 | custom fusion | bytes 33570816 | tf_op jit(solution)/shard_map/gather | solution.py:373
  874.0 13.4 add_convert_fusion.1
  890.0 15.1 multiply_reduce_fusion
  915.2 77.8 %reduce-scatter.8.cloned.1.call-done = bf16[256,2048]{1,0:T(8,128)(2,1)} async-done(((bf16[4096,2048]{1,0:T(8,128)(2,1)}), bf16[256,2048]{1,0:T(8,128)(2,1)}) %reduce-scatter.8.cloned.1.call-update) | async-done | bytes 1048592 | tf_op jit(solution)/shard_map/reduce_scatter | solution.py:388
  997.5 177.2 %reduce-scatter.6.cloned.1.call-done = bf16[256,2048]{1,0:T(8,128)(2,1)} async-done(((bf16[4096,2048]{1,0:T(8,128)(2,1)}), bf16[256,2048]{1,0:T(8,128)(2,1)}) %reduce-scatter.6.cloned.1.call-update) | async-done | bytes 1048592 | tf_op jit(solution)/shard_map/reduce_scatter | solution.py:376
  1199.2 39.5 %all-to-all-done.5.src_ref = bf16[16,256,128]{2,1,0:T(8,128)(2,1)} async-done(((bf16[16,256,128]{2,1,0:T(8,128)(2,1)}), bf16[16,256,128]{2,1,0:T(8,128)(2,1)}, u32[]{:S(2)}, u32[]{:S(2)}) %all-to-all-start.5) | async-done | bytes 1048608 | tf_op jit(solution)/shard_map/all_to_all | solution.py:83
  1238.7 10.0 take_blocks.7
  1262.6 11.9 multiply_convert_fusion.2
  1331.6 11.2 take_blocks.9
  1383.6 10.2 take_blocks.8
  1413.7 41.5 %all-to-all-done.6 = bf16[16,256,192]{1,2,0:T(8,128)(2,1)} async-done(((bf16[16,256,192]{1,2,0:T(8,128)(2,1)}), bf16[16,256,192]{1,2,0:T(8,128)(2,1)}, u32[]{:S(2)}, u32[]{:S(2)}) %all-to-all-start.6) | async-done | bytes 1572896 | tf_op jit(solution)/shard_map/all_to_all | solution.py:83
  1455.2 9.9 fusion.188
  1484.8 9.5 convolution_convert_fusion.8
  1500.4 11.0 convolution_convert_fusion.4
  1526.2 18.4 fusion.25
  1551.3 20.3 %fusion.190 = f32[2048,1408]{1,0:T(8,128)S(1)} fusion(bf16[2304,2048]{1,0:T(8,128)(2,1)} %gather_fusion, bf16[2304,1408]{1,0:T(8,128)(2,1)} %get-tuple-element.128), kind=kOutput, calls=%fused_computation.349 | convolution fusion | flops 13287555072 | bytes 27459584 | tf_op jit(solution)/shard_map/dot_general | solution.py:41
  1571.7 21.1 %fusion.189 = f32[2048,1408]{1,0:T(8,128)S(1)} fusion(bf16[2304,2048]{1,0:T(8,128)(2,1)S(1)} %bitcast.201, bf16[2304,1408]{1,0:T(8,128)(2,1)} %get-tuple-element.129), kind=kOutput, calls=%fused_computation.348 | convolution fusion | flops 13287555072 | bytes 27459584 | tf_op jit(solution)/shard_map/dot_general | solution.py:41
  1624.5 10.5 convolution_convert_fusion.7
  1652.8 38.9 %collective-permute-done.3 = bf16[1024,1408]{1,0:T(8,128)(2,1)} collective-permute-done((bf16[1024,1408]{1,0:T(8,128)(2,1)}, bf16[1024,1408]{1,0:T(8,128)(2,1)}, u32[]{:S(2)}, u32[]{:S(2)}) %collective-permute-start.3) | collective-permute-done | bytes 2883616 | tf_op jit(solution)/shard_map/ppermute | solution.py:408
  1698.3 62.2 %collective-permute-done.2 = bf16[1024,1408]{1,0:T(8,128)(2,1)} collective-permute-done((bf16[1024,1408]{1,0:T(8,128)(2,1)}, bf16[1024,1408]{1,0:T(8,128)(2,1)}, u32[]{:S(2)}, u32[]{:S(2)}) %collective-permute-start.2) | collective-permute-done | bytes 2883616 | tf_op jit(solution)/shard_map/ppermute | solution.py:408
  1786.4 162.6 %reduce-scatter.14.cloned.1.call-done = bf16[64,2048]{1,0:T(8,128)(2,1)} async-done(((bf16[2048,2048]{1,0:T(8,128)(2,1)}), bf16[64,2048]{1,0:T(8,128)(2,1)}) %reduce-scatter.14.cloned.1.call-update) | async-done | bytes 262160 | tf_op jit(solution)/shard_map/reduce_scatter | solution.py:439
  (411 shorter events, 450.6 us)
Async XLA Ops:
  7.2 152.0 %all-gather.7.cloned.1.call-start = ((), (), s32[]{:S(2)}) async-start(), calls=%async_computation.14 | async-start | bytes 17825792 | tf_op jit(solution)/shard_map/all_gather | solution.py:296
  7.9 201.5 %all-gather.9.cloned.1.call-start = ((), (), s32[]{:S(2)}) async-start(), calls=%async_computation.15 | async-start | bytes 2949120 | tf_op jit(solution)/shard_map/all_gather | solution.py:298
  8.7 374.5 %all-gather.11.cloned.1.call-start = ((), (), s32[]{:S(2)}) async-start(), calls=%async_computation.16 | async-start | bytes 8650752 | tf_op jit(solution)/shard_map/all_gather | solution.py:292
  10.4 506.3 %all-gather.15.cloned.1.call-start = ((), (), s32[]{:S(2)}) async-start(), calls=%async_computation.19 | async-start | bytes 17825792 | tf_op jit(solution)/shard_map/all_gather | solution.py:308
  12.8 20.3 %all-to-all-start.1 = ((bf16[4,128,256]{1,2,0:T(8,128)(2,1)}), bf16[4,128,256]{1,2,0:T(8,128)(2,1)S(1)}, u32[]{:S(2)}, u32[]{:S(2)}) async-start(bf16[4,128,256]{1,2,0:T(8,128)(2,1)} %bitcast.232), calls=%async_computation.1 | async-start | bytes 524288 | tf_op jit(solution)/shard_map/all_to_all | solution.py:83
  33.2 42.2 %all-to-all-start = ((bf16[4,512,192]{1,2,0:T(8,128)(2,1)}), bf16[4,512,192]{1,2,0:T(8,128)(2,1)}, u32[]{:S(2)}, u32[]{:S(2)}) async-start(bf16[4,512,192]{1,2,0:T(8,128)(2,1)} %bitcast.223), calls=%async_computation | async-start | bytes 1572864 | tf_op jit(solution)/shard_map/all_to_all | solution.py:83
  37.5 546.6 %all-gather.13.cloned.1.call-start = ((), (), s32[]{:S(2)}) async-start(), calls=%async_computation.17 | async-start | bytes 17825792 | tf_op jit(solution)/shard_map/all_gather | solution.py:355
  39.2 203.7 %copy-start.71 = (f32[32]{0:T(128)}, f32[32]{0:T(128)S(1)}, u32[]{:S(2)}) copy-start(f32[32]{0:T(128)S(1)} %multiply_power_fusion) | copy-start | bytes 388
  41.6 201.2 %copy-start.38 = (f32[4096]{0:T(1024)}, f32[4096]{0:T(1024)S(1)}, u32[]{:S(2)}) copy-start(f32[4096]{0:T(1024)S(1)} %fusion.149) | copy-start | bytes 49156
  41.7 237.4 %copy-start.40 = (pred[256,256]{0,1:T(8,128)(4,1)}, pred[256,256]{0,1:T(8,128)(4,1)S(1)}, u32[]{:S(2)}) copy-start(pred[256,256]{0,1:T(8,128)(4,1)S(1)} %iota_compare_fusion.1) | copy-start | bytes 196612
  401.3 98.0 %copy-start.62 = (bf16[512,16]{0,1:T(8,128)(2,1)S(1)}, bf16[512,16]{0,1:T(8,128)(2,1)}, u32[]{:S(2)}) copy-start(bf16[512,16]{0,1:T(8,128)(2,1)} %param.31) | copy-start | bytes 49156
  404.0 110.0 %all-to-all-start.3 = ((bf16[4,512,352]{1,2,0:T(8,128)(2,1)}), bf16[4,512,352]{1,2,0:T(8,128)(2,1)}, u32[]{:S(2)}, u32[]{:S(2)}) async-start(bf16[4,512,352]{1,2,0:T(8,128)(2,1)} %pad_maximum_fusion.8), calls=%async_computation.3 | async-start | bytes 2883584 | tf_op jit(solution)/shard_map/all_to_all | solution.py:83
  408.3 584.6 %reduce-scatter.8.cloned.1.call-start = ((), (), s32[]{:S(2)}) async-start(), calls=%async_computation.20 | async-start | bytes 17825792 | tf_op jit(solution)/shard_map/reduce_scatter | solution.py:388
  483.3 111.5 %copy-start.45 = (pred[4096]{0:T(1024)(128)(4,1)}, pred[4096]{0:T(1024)(128)(4,1)S(1)}, u32[]{:S(2)}) copy-start(pred[4096]{0:T(1024)(128)(4,1)S(1)} %compare_reduce_fusion) | copy-start | bytes 12292
  512.8 71.4 %copy-start.34 = (bf16[2048,16]{0,1:T(8,128)(2,1)}, bf16[2048,16]{0,1:T(8,128)(2,1)S(1)}, u32[]{:S(2)}) copy-start(bf16[2048,16]{0,1:T(8,128)(2,1)S(1)} %all_gather.29) | copy-start | bytes 196612
  635.6 21.0 %copy-start.10 = (bf16[2304,2048]{1,0:T(8,128)(2,1)S(1)}, bf16[2304,2048]{1,0:T(8,128)(2,1)}, u32[]{:S(2)}) copy-start(bf16[2304,2048]{1,0:T(8,128)(2,1)} %gather_fusion) | copy-start | bytes 28311556
  676.1 30.2 %copy-start.65 = (f32[2304]{0:T(1024)}, f32[2304]{0:T(1024)S(1)}, u32[]{:S(2)}) copy-start(f32[2304]{0:T(1024)S(1)} %fusion.153) | copy-start | bytes 27652
  727.0 22.1 %copy-start.44 = (s32[4096]{0:T(1024)S(1)}, s32[4096]{0:T(1024)}, u32[]{:S(2)}) copy-start(s32[4096]{0:T(1024)} %broadcast_clamp_fusion) | copy-start | bytes 49156
  815.8 358.9 %reduce-scatter.6.cloned.1.call-start = ((), (), s32[]{:S(2)}) async-start(), calls=%async_computation.18 | async-start | bytes 17825792 | tf_op jit(solution)/shard_map/reduce_scatter | solution.py:376
  836.2 37.8 %copy-start.2 = (f32[4096]{0:T(1024)S(1)}, f32[4096]{0:T(1024)}, u32[]{:S(2)}) copy-start(f32[4096]{0:T(1024)} %copy-done.1) | copy-start | bytes 49156
  887.4 526.2 %all-gather.17.cloned.1.call-start = ((), (), s32[]{:S(2)}) async-start(), calls=%async_computation.21 | async-start | bytes 12976128 | tf_op jit(solution)/shard_map/all_gather | solution.py:292
  890.0 103.0 %copy-start.51 = (f32[2048]{0:T(1024)S(1)}, f32[2048]{0:T(1024)}, u32[]{:S(2)}) copy-start(f32[2048]{0:T(1024)} %param.27) | copy-start | bytes 24580
  890.0 103.0 %copy-start.61 = (f32[256]{0:T(256)S(1)}, f32[256]{0:T(256)}, u32[]{:S(2)}) copy-start(f32[256]{0:T(256)} %copy-done.60) | copy-start | bytes 3076
  905.1 10.0 all-to-all-start.4
  1191.7 47.0 %all-to-all-start.5 = ((bf16[16,256,128]{2,1,0:T(8,128)(2,1)}), bf16[16,256,128]{2,1,0:T(8,128)(2,1)}, u32[]{:S(2)}, u32[]{:S(2)}) async-start(bf16[16,256,128]{2,1,0:T(8,128)(2,1)} %bitcast.220), calls=%async_computation.7 | async-start | bytes 2097152 | tf_op jit(solution)/shard_map/all_to_all | solution.py:83
  1196.1 269.0 %reduce-scatter.10.cloned.1.call-start = ((), (), s32[]{:S(2)}) async-start(), calls=%async_computation.22 | async-start | bytes 5013504 | tf_op jit(solution)/shard_map/reduce_scatter | solution.py:450
  1196.2 55.1 %copy-start.41 = (pred[256,256]{0,1:T(8,128)(4,1)S(1)}, pred[256,256]{0,1:T(8,128)(4,1)}, u32[]{:S(2)}) copy-start(pred[256,256]{0,1:T(8,128)(4,1)} %copy-done.40) | copy-start | bytes 196612
  1196.2 55.1 %copy-start.70 = (f32[8,256]{1,0:T(8,128)S(1)}, f32[8,256]{1,0:T(8,128)}, u32[]{:S(2)}) copy-start(f32[8,256]{1,0:T(8,128)} %get-tuple-element.122) | copy-start | bytes 24580
  1261.5 36.3 %copy-start.13 = (bf16[8,24,8,256]{3,2,0,1:T(8,128)(2,1)}, bf16[8,24,8,256]{3,2,0,1:T(8,128)(2,1)S(1)}, u32[]{:S(2)}) copy-start(bf16[8,24,8,256]{3,2,0,1:T(8,128)(2,1)S(1)} %copy.333) | copy-start | bytes 2359300
  1262.6 20.6 %slice-start.7 = ((s8[16777216]{0:T(1024)(128)(4,1)}), s8[4194304]{0:T(1024)(128)(4,1)S(1)}, s32[]{:S(2)}) async-start(s8[16777216]{0:T(1024)(128)(4,1)} %bitcast.194), calls=%async_computation.33 | async-start | bytes 8388608
  1397.6 57.6 %all-to-all-start.6 = ((bf16[16,256,192]{1,2,0:T(8,128)(2,1)}), bf16[16,256,192]{1,2,0:T(8,128)(2,1)}, u32[]{:S(2)}, u32[]{:S(2)}) async-start(bf16[16,256,192]{1,2,0:T(8,128)(2,1)} %copy.291), calls=%async_computation.8 | async-start | bytes 3145728 | tf_op jit(solution)/shard_map/all_to_all | solution.py:83
  1402.0 378.6 %all-reduce.3.cloned.1.call-start = ((), (), s32[]{:S(2)}) async-start(), calls=%async_computation.25 | async-start | bytes 303104
  1480.7 304.1 %reduce-scatter.12.cloned.1.call-start = ((), (), s32[]{:S(2)}) async-start(), calls=%async_computation.23 | async-start | bytes 2703360 | tf_op jit(solution)/shard_map/reduce_scatter | solution.py:477
  1495.3 105.2 %collective-permute-start = (bf16[88,2048]{1,0:T(8,128)(2,1)}, bf16[88,2048]{1,0:T(8,128)(2,1)}, u32[]{:S(2)}, u32[]{:S(2)}) collective-permute-start(bf16[88,2048]{1,0:T(8,128)(2,1)} %get-tuple-element.144), channel_id=1, source_target_pairs={{0,0},{1,8},{2,16},{3,24},{4,2},{5,10},{6,18},{7,26},{8,4},{9,12},... | collective-permute-start | bytes 1081352 | tf_op jit(solution)/shard_map/ppermute | solution.py:431
  1499.7 100.9 %collective-permute-start.1 = (bf16[88,2048]{1,0:T(8,128)(2,1)}, bf16[88,2048]{1,0:T(8,128)(2,1)}, u32[]{:S(2)}, u32[]{:S(2)}) collective-permute-start(bf16[88,2048]{1,0:T(8,128)(2,1)} %get-tuple-element.145), channel_id=1, source_target_pairs={{0,1},{1,9},{2,17},{3,25},{4,3},{5,11},{6,19},{7,27},{8,5},{9,13},... | collective-permute-start | bytes 1081352 | tf_op jit(solution)/shard_map/ppermute | solution.py:431
  1514.0 88.6 %all-to-all-start.8 = ((bf16[32,64,352]{2,1,0:T(8,128)(2,1)}), bf16[32,64,352]{2,1,0:T(8,128)(2,1)}, u32[]{:S(2)}, u32[]{:S(2)}) async-start(bf16[32,64,352]{2,1,0:T(8,128)(2,1)} %bitcast.210), calls=%async_computation.13 | async-start | bytes 3145728 | tf_op jit(solution)/shard_map/all_to_all | solution.py:83
  1517.8 431.1 %reduce-scatter.14.cloned.1.call-start = ((), (), s32[]{:S(2)}) async-start(), calls=%async_computation.24 | async-start | bytes 8650752 | tf_op jit(solution)/shard_map/reduce_scatter | solution.py:439
  1544.6 27.0 %slice-start.8 = ((s8[9437184]{0:T(1024)(128)(4,1)}), s8[1048576]{0:T(1024)(128)(4,1)S(1)}, s32[]{:S(2)}) async-start(s8[9437184]{0:T(1024)(128)(4,1)} %bitcast.200), calls=%async_computation.34 | async-start | bytes 2097152
  1546.7 25.0 %slice-start.9 = ((s8[9437184]{0:T(1024)(128)(4,1)}), s8[4194304]{0:T(1024)(128)(4,1)S(1)}, s32[]{:S(2)}) async-start(s8[9437184]{0:T(1024)(128)(4,1)} %bitcast.200), calls=%async_computation.35 | async-start | bytes 8388608
  1546.7 25.0 %slice-start.10 = ((s8[9437184]{0:T(1024)(128)(4,1)}), s8[4194304]{0:T(1024)(128)(4,1)S(1)}, s32[]{:S(2)}) async-start(s8[9437184]{0:T(1024)(128)(4,1)} %bitcast.200), calls=%async_computation.36 | async-start | bytes 8388608
  1546.7 98.6 %collective-permute-start.4 = (bf16[704,2048]{1,0:T(8,128)(2,1)}, bf16[704,2048]{1,0:T(8,128)(2,1)}, u32[]{:S(2)}, u32[]{:S(2)}) collective-permute-start(bf16[704,2048]{1,0:T(8,128)(2,1)} %dynamic-slice_convert_fusion), channel_id=1, source_target_pairs={{0,16},{16,0},{1,17},{17,1},{2,18},{18,2},{3,19},{19,3},{4,20},{20... | collective-permute-start | bytes 8650760 | tf_op jit(solution)/shard_map/ppermute | solution.py:408
  1571.7 21.1 %copy-start.17 = (f32[2048,1408]{1,0:T(8,128)}, f32[2048,1408]{1,0:T(8,128)S(1)}, u32[]{:S(2)}) copy-start(f32[2048,1408]{1,0:T(8,128)S(1)} %fusion.190) | copy-start | bytes 34603012
  1594.9 96.8 %collective-permute-start.3 = (bf16[1024,1408]{1,0:T(8,128)(2,1)}, bf16[1024,1408]{1,0:T(8,128)(2,1)}, u32[]{:S(2)}, u32[]{:S(2)}) collective-permute-start(bf16[1024,1408]{1,0:T(8,128)(2,1)} %dynamic-slice_convert_fusion.1), channel_id=1, source_target_pairs={{0,16},{16,0},{1,17},{17,1},{2,18},{18,2},{3,19},{19,3},{4,20},{20... | collective-permute-start | bytes 8650760 | tf_op jit(solution)/shard_map/ppermute | solution.py:408
  1599.1 161.4 %collective-permute-start.2 = (bf16[1024,1408]{1,0:T(8,128)(2,1)}, bf16[1024,1408]{1,0:T(8,128)(2,1)}, u32[]{:S(2)}, u32[]{:S(2)}) collective-permute-start(bf16[1024,1408]{1,0:T(8,128)(2,1)} %dynamic-slice_convert_fusion.2), channel_id=1, source_target_pairs={{0,16},{16,0},{1,17},{17,1},{2,18},{18,2},{3,19},{19,3},{4,20},{20... | collective-permute-start | bytes 8650760 | tf_op jit(solution)/shard_map/ppermute | solution.py:408
  1639.9 125.4 %all-to-all-start.7 = ((bf16[32,64,256]{2,1,0:T(8,128)(2,1)}), bf16[32,64,256]{2,1,0:T(8,128)(2,1)}, u32[]{:S(2)}, u32[]{:S(2)}) async-start(bf16[32,64,256]{2,1,0:T(8,128)(2,1)} %pad_maximum_fusion.10), calls=%async_computation.10 | async-start | bytes 2097152 | tf_op jit(solution)/shard_map/all_to_all | solution.py:83
  1645.3 115.2 %slice-start.11 = ((s8[11534336]{0:T(1024)(128)(4,1)}), s8[4194304]{0:T(1024)(128)(4,1)S(1)}, s32[]{:S(2)}) async-start(s8[11534336]{0:T(1024)(128)(4,1)} %bitcast.208), calls=%async_computation.37 | async-start | bytes 8388608
  1645.3 115.2 %slice-start.12 = ((s8[11534336]{0:T(1024)(128)(4,1)}), s8[4194304]{0:T(1024)(128)(4,1)S(1)}, s32[]{:S(2)}) async-start(s8[11534336]{0:T(1024)(128)(4,1)} %bitcast.208), calls=%async_computation.38 | async-start | bytes 8388608
  1652.8 107.7 %slice-start.13 = ((s8[11534336]{0:T(1024)(128)(4,1)}), s8[3145728]{0:T(1024)(128)(4,1)S(1)}, s32[]{:S(2)}) async-start(s8[11534336]{0:T(1024)(128)(4,1)} %bitcast.208), calls=%async_computation.39 | async-start | bytes 6291456
  (67 other events, 494.2 us)
Sparse Core Ops, SparseCore 0:
  10.2 148.9 all-gather.6
  160.8 48.6 all-gather.8
  212.9 76.2 all-gather.10
  291.2 163.0 all-gather.14
  456.4 127.6 all-gather.12
  815.9 177.0 reduce-scatter.7
  997.1 177.5 reduce-scatter.5
  1178.1 108.0 all-gather.16
  1357.9 93.7 reduce-scatter.9
  1480.9 131.5 all-reduce.2
  1614.9 148.6 reduce-scatter.11
  1765.8 183.1 reduce-scatter.13

commit v2 on v1

v2 whole, which is shorter than its diff:
```python
import functools
import math

import jax
import jax.numpy as jnp
from jax import lax
from jax.experimental import pallas as pl
from jax.experimental.pallas import tpu as pltpu
from jax.sharding import PartitionSpec as P

HEADS = 16
NOPE = 128
ROPE = 64
VDIM = 128
LATENT = 512
BLOCK = 256
PROMPT = 2048
NCONT = 8
QDIM = NOPE + ROPE
KVDIM = NOPE + VDIM
GROUP_BLOCKS = PROMPT // BLOCK + NCONT
GROUP_TOK = GROUP_BLOCKS * BLOCK

EPS = 1e-06
ALL = ("group", "expert", "shard")
ROW = ("expert", "shard")
SCALE = 1.0 / math.sqrt(NOPE + ROPE)
F32 = jnp.float32
BF16 = jnp.bfloat16


def matmul(left, right):
    return jnp.dot(left, right, preferred_element_type=F32)


def matmul_nt(left, right):
    return lax.dot_general(left, right, (((1,), (1,)), ((), ())), preferred_element_type=F32)


def matmul_tn(left, right):
    return lax.dot_general(left, right, (((0,), (0,)), ((), ())), preferred_element_type=F32)


def rms_parts(values):
    inverse = lax.rsqrt(jnp.mean(values * values, axis=-1, keepdims=True) + EPS)
    return (values * inverse, inverse)


def norm_back(grad_in, normed, inverse, gain):
    scaled = grad_in * gain
    gain_grad = jnp.sum(grad_in * normed, axis=0)
    input_grad = inverse * (scaled - normed * jnp.mean(scaled * normed, axis=-1, keepdims=True))
    return (input_grad, gain_grad)


def angles(pos_list, rot_width):
    half_width = rot_width // 2
    freq = 10000.0 ** (-2.0 * jnp.arange(half_width, dtype=F32) / rot_width)
    theta = pos_list.astype(F32)[:, None] * freq[None, :]
    return (jnp.cos(theta), jnp.sin(theta))


def rotate(values, cosine, sine):
    half_width = values.shape[-1] // 2
    first_half = values[..., :half_width]
    second_half = values[..., half_width:]
    return jnp.concatenate(
        [first_half * cosine - second_half * sine, second_half * cosine + first_half * sine],
        axis=-1,
    )


def unrotate(grad_in, cosine, sine):
    return rotate(grad_in, cosine, -sine)


def silu_parts(values):
    sigmoid = jax.nn.sigmoid(values)
    return (values * sigmoid, sigmoid * (1.0 + values * (1.0 - sigmoid)))


def trade(buffer, axes):
    return lax.all_to_all(buffer, axes, split_axis=0, concat_axis=0, tiled=True)


TILE = 2 * BLOCK
TILES = GROUP_TOK // TILE
PROMPT_TILES = PROMPT // TILE
NEG = -1e30


def dot(left, right, left_dim, right_dim):
    return lax.dot_general(
        left, right, (((left_dim,), (right_dim,)), ((), ())), preferred_element_type=F32
    )


def take_blocks(blocks, index):
    count = index.shape[0]
    shape = blocks.shape[1:]
    unroll = 8 if shape[-1] <= 256 else 4

    def body(index_ref, *refs):
        for i in range(unroll):
            refs[-1][i] = refs[i][0]

    return pl.pallas_call(
        body,
        grid_spec=pltpu.PrefetchScalarGridSpec(
            num_scalar_prefetch=1,
            grid=(count // unroll,),
            in_specs=[
                pl.BlockSpec((1,) + shape, lambda i, at, k=k: (at[i * unroll + k], 0, 0))
                for k in range(unroll)
            ],
            out_specs=pl.BlockSpec((unroll,) + shape, lambda i, at: (i, 0, 0)),
        ),
        out_shape=jax.ShapeDtypeStruct((count,) + shape, blocks.dtype),
        compiler_params=pltpu.CompilerParams(vmem_limit_bytes=40 << 20),
        cost_estimate=pl.CostEstimate(
            flops=0, bytes_accessed=4 * count * shape[0] * shape[1], transcendentals=0
        ),
        name="take_blocks",
    )(index, *([blocks] * unroll))


def project_body(
    at_ref, tok_a, tok_b, gain_ref, w_ref, gain_l_ref, wkv_ref, cos_ref, sin_ref,
    hid_ref, q_ref, k_ref, v_ref, comp_ref,
):
    gain = gain_ref[...]
    gain_l = gain_l_ref[...]
    for part, tok in enumerate((tok_a, tok_b)):
        rows = slice(part * BLOCK, (part + 1) * BLOCK)
        hidden = (rms_parts(tok[0].astype(F32))[0] * gain).astype(BF16)
        hid_ref[rows, :] = hidden
        joint = dot(hidden, w_ref[...], 1, 0)
        cosine, sine = cos_ref[rows, :], sin_ref[rows, :]
        at = NOPE + LATENT
        q_ref[rows, :NOPE] = joint[:, :NOPE].astype(BF16)
        q_ref[rows, NOPE:] = rotate(joint[:, at : at + ROPE], cosine, sine).astype(BF16)
        comp = (rms_parts(joint[:, NOPE:at])[0] * gain_l).astype(BF16)
        comp_ref[rows, :] = comp
        keyval = dot(comp, wkv_ref[...], 1, 0).astype(BF16)
        k_ref[rows, :NOPE] = keyval[:, :NOPE]
        k_ref[rows, NOPE:] = rotate(joint[:, at + ROPE :], cosine, sine).astype(BF16)
        v_ref[rows, :] = keyval[:, NOPE:]


def project(blocks, index, gain, weights, gain_l, wkv, cosine, sine):
    width = blocks.shape[-1]
    whole = lambda a: pl.BlockSpec(a.shape, lambda i, at: (0, 0))
    tiled = lambda cols: pl.BlockSpec((TILE, cols), lambda i, at: (i, 0))
    piece = lambda k: pl.BlockSpec((1, BLOCK, width), lambda i, at: (at[2 * i + k], 0, 0))
    widths = (width, QDIM, QDIM, VDIM, LATENT)
    gain, gain_l = gain.reshape(1, -1), gain_l.reshape(1, -1)
    return pl.pallas_call(
        project_body,
        grid_spec=pltpu.PrefetchScalarGridSpec(
            num_scalar_prefetch=1,
            grid=(TILES,),
            in_specs=[
                piece(0), piece(1), whole(gain), whole(weights), whole(gain_l), whole(wkv),
                tiled(ROPE // 2), tiled(ROPE // 2),
            ],
            out_specs=[tiled(cols) for cols in widths],
        ),
        out_shape=[jax.ShapeDtypeStruct((GROUP_TOK, cols), BF16) for cols in widths],
        compiler_params=pltpu.CompilerParams(vmem_limit_bytes=48 << 20),
        cost_estimate=pl.CostEstimate(
            flops=14_000_000_000, bytes_accessed=48_000_000, transcendentals=0
        ),
        name="project",
    )(index, blocks, blocks, gain, weights, gain_l, wkv, cosine, sine)


def own_mask(tile):
    k_at = lax.broadcasted_iota(jnp.int32, (TILE, TILE), 0)
    q_at = lax.broadcasted_iota(jnp.int32, (TILE, TILE), 1)
    piece = jnp.where(tile < PROMPT_TILES, TILE, BLOCK)
    lowest = jnp.where(q_at >= piece, piece, 0)
    return (k_at <= q_at) & (k_at >= lowest)


def attend_body(q_ref, k_ref, v_ref, o_ref, ob_ref, lse_ref, s_ref):
    tile = pl.program_id(0)
    q = q_ref[...]
    others = jnp.minimum(tile, PROMPT_TILES)

    def rows_of(at):
        return pl.ds(pl.multiple_of(at * TILE, TILE), TILE)

    def fold(values, op):
        return op(values.reshape(TILE // 8, 8, TILE), axis=0)

    own = jnp.where(own_mask(tile), dot(k_ref[rows_of(tile), :], q, 1, 1) * SCALE, NEG)
    s_ref[rows_of(PROMPT_TILES), :] = own

    def raw(at, top):
        s = dot(k_ref[rows_of(at), :], q, 1, 1) * SCALE
        s_ref[rows_of(at), :] = s
        return jnp.maximum(top, fold(s, jnp.max))

    top = lax.fori_loop(0, others, raw, fold(own, jnp.max))
    top = jnp.max(top, axis=0, keepdims=True)

    def mix(s_at, v_at, carry):
        total, out = carry
        p = jnp.exp(s_ref[rows_of(s_at), :] - top)
        return total + fold(p, jnp.sum), out + dot(p.astype(BF16), v_ref[rows_of(v_at), :], 0, 0)

    carry = (jnp.zeros((8, TILE), F32), jnp.zeros((TILE, VDIM), F32))
    carry = mix(PROMPT_TILES, tile, carry)
    total, out = lax.fori_loop(0, others, lambda at, c: mix(at, at, c), carry)
    total = jnp.sum(total, axis=0, keepdims=True)
    lse_ref[...] = top + jnp.log(total)
    scale = jnp.transpose(jnp.broadcast_to(1.0 / total, (VDIM, TILE)))
    out = out * scale
    o_ref[...] = out
    ob_ref[...] = out.astype(BF16)


def attend(query, key, value):
    whole = lambda cols: pl.BlockSpec((GROUP_TOK, cols), lambda i: (0, 0))
    tiled = lambda cols: pl.BlockSpec((TILE, cols), lambda i: (i, 0))
    return pl.pallas_call(
        attend_body,
        grid=(TILES,),
        in_specs=[tiled(QDIM), whole(QDIM), whole(VDIM)],
        out_specs=[tiled(VDIM), tiled(VDIM), pl.BlockSpec((1, TILE), lambda i: (0, i))],
        out_shape=[
            jax.ShapeDtypeStruct((GROUP_TOK, VDIM), F32),
            jax.ShapeDtypeStruct((GROUP_TOK, VDIM), BF16),
            jax.ShapeDtypeStruct((1, GROUP_TOK), F32),
        ],
        scratch_shapes=[pltpu.VMEM((PROMPT + TILE, TILE), F32)],
        compiler_params=pltpu.CompilerParams(vmem_limit_bytes=40 << 20),
        cost_estimate=pl.CostEstimate(
            flops=6_000_000_000, bytes_accessed=10_000_000, transcendentals=8_000_000
        ),
        name="attend",
    )(query, key, value)


def attend_back_body(
    q_ref, k_ref, v_ref, g_ref, o_ref, lse_ref, cos_ref, sin_ref, dq_ref, dk_ref, dv_ref, acc_ref
):
    tile = pl.program_id(0)

    @pl.when(tile == 0)
    def _():
        dk_ref[...] = jnp.zeros_like(dk_ref)
        dv_ref[...] = jnp.zeros_like(dv_ref)

    q = q_ref[...]
    g = g_ref[...]
    lse = lse_ref[...]
    delta = jnp.sum(jnp.transpose(g.astype(F32) * o_ref[...]), axis=0, keepdims=True)

    def step(at, mask):
        rows = pl.ds(pl.multiple_of(at * TILE, TILE), TILE)
        k = k_ref[rows, :]
        p = jnp.exp(dot(k, q, 1, 1) * SCALE - lse)
        if mask is not None:
            p = jnp.where(mask, p, 0.0)
        ds = (p * (dot(v_ref[rows, :], g, 1, 1) - delta)).astype(BF16)
        dv_ref[rows, :] += dot(p.astype(BF16), g, 1, 0)
        dk_ref[rows, :] += dot(ds, q, 1, 0) * SCALE
        return dot(ds, k, 0, 0)

    acc_ref[...] = step(tile, own_mask(tile))

    @pl.loop(0, jnp.minimum(tile, PROMPT_TILES))
    def _(at):
        acc_ref[...] += step(at, None)

    dq = acc_ref[...] * SCALE
    dq_ref[:, :NOPE] = dq[:, :NOPE].astype(BF16)
    dq_ref[:, NOPE:] = rotate(dq[:, NOPE:], cos_ref[...], -sin_ref[...]).astype(BF16)


def attend_back(query, key, value, mixed, lse, grad, cosine, sine):
    whole = lambda cols: pl.BlockSpec((GROUP_TOK, cols), lambda i: (0, 0))
    tiled = lambda cols: pl.BlockSpec((TILE, cols), lambda i: (i, 0))
    return pl.pallas_call(
        attend_back_body,
        grid=(TILES,),
        in_specs=[
            tiled(QDIM), whole(QDIM), whole(VDIM), tiled(VDIM), tiled(VDIM),
            pl.BlockSpec((1, TILE), lambda i: (0, i)), tiled(ROPE // 2), tiled(ROPE // 2),
        ],
        out_specs=[tiled(QDIM), whole(QDIM), whole(VDIM)],
        out_shape=[
            jax.ShapeDtypeStruct((GROUP_TOK, QDIM), BF16),
            jax.ShapeDtypeStruct((GROUP_TOK, QDIM), F32),
            jax.ShapeDtypeStruct((GROUP_TOK, VDIM), F32),
        ],
        scratch_shapes=[pltpu.VMEM((TILE, QDIM), F32)],
        compiler_params=pltpu.CompilerParams(vmem_limit_bytes=48 << 20),
        cost_estimate=pl.CostEstimate(
            flops=16_000_000_000, bytes_accessed=20_000_000, transcendentals=8_000_000
        ),
        name="attend_back",
    )(query, key, value, grad, mixed, lse, cosine, sine)


def latent_back_body(slot_ref, mine_ref, dk_ref, dv_ref, w_ref, dkv_ref, lat_ref):
    kv = jnp.concatenate([dk_ref[:, :NOPE], dv_ref[...]], axis=1).astype(BF16)
    dkv_ref[...] = kv
    keep = mine_ref[pl.program_id(0)] != 0
    comp = jnp.where(keep, dot(kv, w_ref[...], 1, 1), 0.0)
    lat_ref[:, :LATENT] = comp.astype(BF16)
    lat_ref[:, LATENT:] = jnp.where(keep, dk_ref[:, NOPE:], 0.0).astype(BF16)


def latent_back(d_key, d_value, wkv, slot, mine):
    count = slot.shape[0]
    tiled = lambda cols: pl.BlockSpec((BLOCK, cols), lambda i, at, m: (at[i], 0))
    return pl.pallas_call(
        latent_back_body,
        grid_spec=pltpu.PrefetchScalarGridSpec(
            num_scalar_prefetch=2,
            grid=(count,),
            in_specs=[
                tiled(QDIM), tiled(VDIM), pl.BlockSpec(wkv.shape, lambda i, at, m: (0, 0)),
            ],
            out_specs=[
                tiled(KVDIM), pl.BlockSpec((BLOCK, LATENT + ROPE), lambda i, at, m: (i, 0)),
            ],
        ),
        out_shape=[
            jax.ShapeDtypeStruct((GROUP_TOK, KVDIM), BF16),
            jax.ShapeDtypeStruct((count * BLOCK, LATENT + ROPE), BF16),
        ],
        cost_estimate=pl.CostEstimate(
            flops=1_100_000_000, bytes_accessed=14_000_000, transcendentals=0
        ),
        name="latent_back",
    )(slot, mine.astype(jnp.int32), d_key, d_value, wkv)

def line_gather(part, axis, count):
    up = [(i, i + 1) for i in range(count - 1)]
    down = [(i + 1, i) for i in range(count - 1)]
    right, left = [part], [part]
    for _ in range(count - 1):
        right.append(lax.ppermute(right[-1], axis, up))
        left.append(lax.ppermute(left[-1], axis, down))
    line = jnp.stack(right[:0:-1] + left)
    return lax.dynamic_slice_in_dim(line, count - 1 - lax.axis_index(axis), count)


def pair_gather(part, axis, count, flip, bit):
    other = lax.ppermute(part, axis, [(i, i ^ flip) for i in range(count)])
    return lax.dynamic_slice_in_dim(jnp.stack([part, other, part]), bit, 2)


def chunks_of(total, size):
    return [slice(at, min(at + size, total)) for at in range(0, total, size)]


def experts_body(
    groups, units, count, me_ref, place_ref, h_ref, c_ref, wg_ref, wu_ref, wd_ref, ws_ref, wsd_ref,
    outa_ref, outb_ref, dh_ref, dprob_ref, rows_ref, dout_ref, mid_ref, dg_ref, du_ref, smid_ref, ds_ref,
    crow_ref,
):
    width, hidden = wg_ref.shape
    padded = wsd_ref.shape[0]
    h, c = h_ref[...], c_ref[...]

    wide = dot(h, ws_ref[...], 1, 0)
    s_gate, s_up = wide[:, :padded], wide[:, padded:]
    first = units - (padded - 128)
    logits = jnp.transpose(s_gate[:, padded - 128 :])[first : first + count, :]
    powers = jnp.exp(logits - jnp.max(logits, axis=0, keepdims=True))
    mine = lax.broadcasted_iota(jnp.int32, powers.shape, 0) == me_ref[0]
    weight = jnp.sum(jnp.where(mine, powers, 0.0), axis=0, keepdims=True) / jnp.sum(
        powers, axis=0, keepdims=True
    )
    s_act, s_slope = silu_parts(s_gate)
    smid_ref[...] = (s_act * s_up).astype(BF16)
    ds_mid = dot(c, wsd_ref[...], 1, 1)
    ds_ref[:, :padded] = (ds_mid * s_up * s_slope).astype(BF16)
    ds_ref[:, padded:] = (ds_mid * s_act).astype(BF16)

    picks, weights = [], []
    for rows, toks in groups:
        shape = (rows.stop - rows.start, toks.stop - toks.start)
        here = lax.broadcasted_iota(jnp.int32, shape, 0) + rows.start == place_ref[0, :, toks]
        pick = jnp.where(here, 1.0, 0.0).astype(BF16)
        scale = jnp.sum(jnp.where(here, weight[:, toks], 0.0), axis=1, keepdims=True)
        for cols in chunks_of(width, 512):
            rows_ref[rows, cols] = dot(pick, h[toks, cols], 1, 0).astype(BF16)
            c_rows = dot(pick, c[toks, cols], 1, 0)
            crow_ref[rows, cols] = c_rows.astype(BF16)
            dout_ref[rows, cols] = (scale * c_rows).astype(BF16)
        picks.append((rows, toks, here, pick))
        weights.append(scale)
    scale = jnp.concatenate(weights, axis=0) if len(weights) > 1 else weights[0]

    for cols in chunks_of(hidden, 512):
        gate = dot(rows_ref[...], wg_ref[:, cols], 1, 0)
        up = dot(rows_ref[...], wu_ref[:, cols], 1, 0)
        act, slope = silu_parts(gate)
        mid_ref[:, cols] = (act * up).astype(BF16)
        d_mid = dot(dout_ref[...], wd_ref[cols, :], 1, 1)
        dg_ref[:, cols] = (d_mid * up * slope).astype(BF16)
        du_ref[:, cols] = (d_mid * act).astype(BF16)

    d_prob = jnp.zeros(scale.shape, F32)
    for cols in chunks_of(width, 512):
        out = dot(mid_ref[...], wd_ref[:, cols], 1, 0).astype(BF16).astype(F32)
        d_prob = d_prob + jnp.sum(out * crow_ref[:, cols].astype(F32), axis=1, keepdims=True)
        out = (out * scale).astype(BF16)
        d_rows = dot(dg_ref[...], wg_ref[cols, :], 1, 1) + dot(du_ref[...], wu_ref[cols, :], 1, 1)
        d_rows = d_rows.astype(BF16)
        for rows, toks, here, pick in picks:
            shared = dot(smid_ref[toks, :], wsd_ref[:, cols], 1, 0)
            half_ref, at = (outa_ref, 0) if cols.start < width // 2 else (outb_ref, width // 2)
            half_ref[toks, cols.start - at : cols.stop - at] = (
                dot(pick, out[rows, :], 0, 0) + shared
            ).astype(BF16)
            shared = dot(ds_ref[toks, :], ws_ref[cols, :], 1, 1)
            dh_ref[toks, cols] = (dot(pick, d_rows[rows, :], 0, 0) + shared).astype(BF16)
    for rows, toks, here, pick in picks:
        dprob_ref[0, :, toks] = jnp.sum(
            jnp.where(here, d_prob[rows, :], 0.0), axis=0, keepdims=True
        )


def experts(
    me, place, capacity, hidden2, cotangent, w_gate, w_up, w_down, w_shared, w_sdown, units, count
):
    tokens, width = hidden2.shape
    hidden = w_gate.shape[1]
    padded = w_sdown.shape[0]
    blocks = 2
    step = blocks * BLOCK
    steps = tokens // step
    room = blocks * capacity
    if capacity % 16 == 0:
        groups = [
            (slice(b * capacity, (b + 1) * capacity), slice(b * BLOCK, (b + 1) * BLOCK))
            for b in range(blocks)
        ]
    else:
        groups = [(slice(0, room), slice(0, step))]
    once = lambda a: pl.BlockSpec(a.shape, lambda i, me: (0, 0), pipeline_mode=pl.Buffered(1))
    tiled = lambda rows, cols: pl.BlockSpec((rows, cols), lambda i, me: (i, 0))
    line = pl.BlockSpec((1, 1, step), lambda i, me: (i, 0, 0))
    shape = lambda rows, cols, kind=BF16: jax.ShapeDtypeStruct((rows, cols), kind)
    flops = 2 * steps * (6 * room * width * hidden + 6 * step * width * padded)
    return pl.pallas_call(
        functools.partial(experts_body, groups, units, count),
        grid_spec=pltpu.PrefetchScalarGridSpec(
            num_scalar_prefetch=1,
            grid=(steps,),
            in_specs=[
                line, tiled(step, width), tiled(step, width),
                once(w_gate), once(w_up), once(w_down), once(w_shared), once(w_sdown),
            ],
            out_specs=[
                tiled(step, width // 2), tiled(step, width // 2), tiled(step, width), line,
                tiled(room, width),
                tiled(room, width), tiled(room, hidden), tiled(room, hidden),
                tiled(room, hidden), tiled(step, padded), tiled(step, 2 * padded),
            ],
            scratch_shapes=[pltpu.VMEM((room, width), BF16)],
        ),
        out_shape=[
            shape(tokens, width // 2), shape(tokens, width // 2), shape(tokens, width),
            jax.ShapeDtypeStruct((steps, 1, step), F32),
            shape(steps * room, width), shape(steps * room, width), shape(steps * room, hidden),
            shape(steps * room, hidden), shape(steps * room, hidden), shape(tokens, padded),
            shape(tokens, 2 * padded),
        ],
        compiler_params=pltpu.CompilerParams(vmem_limit_bytes=62 << 20),
        cost_estimate=pl.CostEstimate(
            flops=flops, bytes_accessed=130_000_000, transcendentals=5_000_000
        ),
        name="experts",
    )(me, place, hidden2, cotangent, w_gate, w_up, w_down, w_shared, w_sdown)

def places_of(hit):
    count = hit.shape[1]
    upper = (
        lax.broadcasted_iota(jnp.int32, (count, count), 0)
        < lax.broadcasted_iota(jnp.int32, (count, count), 1)
    ).astype(BF16)
    return matmul(hit.astype(BF16), upper).astype(jnp.int32)


def per_device(
    sizes,
    tokens,
    cotangent,
    gain_attn,
    w_query,
    w_latent,
    gain_latent,
    w_keyval,
    w_output,
    gain_ffn,
    w_shared_gate,
    w_shared_up,
    w_shared_down,
    w_router,
    expert_gate,
    expert_up,
    expert_down,
    segments,
    positions,
    routes,
):
    n_group, n_expert, n_shard = sizes
    n_row = n_expert * n_shard
    n_all = n_group * n_row
    tok_rows, width = tokens.shape
    row_tokens = segments.shape[0]
    n_prompt = row_tokens // GROUP_TOK
    e_per_prompt = n_expert // n_prompt
    group_at = lax.axis_index("group")
    expert_at = lax.axis_index("expert")
    shard_at = lax.axis_index("shard")
    row_at = expert_at * n_shard + shard_at
    prompt_at = expert_at // e_per_prompt
    head_group = expert_at % e_per_prompt

    seg_block = segments[::BLOCK]
    pos_block = positions[::BLOCK]
    prompt_of = seg_block // (NCONT + 1)
    prompt_of = prompt_of - jnp.min(prompt_of)
    cont_of = seg_block % (NCONT + 1)
    piece = jnp.where(cont_of == 0, pos_block // BLOCK, PROMPT // BLOCK - 1 + cont_of)
    slot_of = prompt_of * GROUP_BLOCKS + piece
    block_ids = jnp.arange(n_row, dtype=jnp.int32)
    block_at = jnp.sum(
        jnp.where(slot_of[None, :] == block_ids[:, None], block_ids[None, :], 0), axis=1
    )
    my_blocks = lax.dynamic_slice_in_dim(block_at, prompt_at * GROUP_BLOCKS, GROUP_BLOCKS)
    local_slot = slot_of - prompt_at * GROUP_BLOCKS
    mine = (local_slot >= 0) & (local_slot < GROUP_BLOCKS)
    local_slot = jnp.clip(local_slot, 0, GROUP_BLOCKS - 1)
    own_prompt = jnp.sum(jnp.where(block_ids == row_at, prompt_of, 0))

    def to_pieces(all_rows):
        return take_blocks(all_rows.reshape(n_row, BLOCK, -1), my_blocks).reshape(GROUP_TOK, -1)

    def from_pieces(rows):
        return take_blocks(rows.reshape(GROUP_BLOCKS, BLOCK, -1), local_slot)

    def heads_home(rows):
        got = trade(from_pieces(rows), ROW)
        if n_prompt > 1:
            got = lax.dynamic_slice_in_dim(got, own_prompt * GROUP_BLOCKS, GROUP_BLOCKS)
        return jnp.swapaxes(got, 0, 1).reshape(BLOCK, -1)

    def heads_out(rows):
        split = jnp.swapaxes(rows.reshape(BLOCK, HEADS, -1), 0, 1)
        if n_prompt > 1:
            split = jnp.tile(split, (n_prompt, 1, 1))
            keep = (block_ids // GROUP_BLOCKS) == own_prompt
            split = jnp.where(keep[:, None, None], split, jnp.zeros_like(split))
        return to_pieces(trade(split, ROW))

    def head_parts(weight, per_head):
        cols = lax.dynamic_slice_in_dim(
            weight, head_group * (n_shard * per_head), n_shard * per_head, axis=1
        )
        return jnp.swapaxes(cols.reshape(-1, n_shard, per_head), 0, 1)

    def head_columns(weight, per_head):
        return trade(head_parts(weight, per_head), "shard").reshape(-1, per_head)

    def unit_columns(weight):
        units = weight.shape[1] // n_row
        cols = weight.reshape(weight.shape[0], n_shard, n_expert, units)
        cols = lax.dynamic_index_in_dim(cols, expert_at, axis=2, keepdims=False)
        return jnp.swapaxes(cols, 0, 1)

    paired = (n_group, n_expert) == (2, 4)
    x_at, core_at = expert_at // 2, expert_at % 2

    def sub_rows(weight):
        part = weight.shape[0] // (n_group * n_expert)
        at = (group_at * n_expert + expert_at) * part
        return lax.dynamic_slice_in_dim(weight, at, part)

    def gather_rows_at_once(weight):
        return lax.all_gather(sub_rows(weight), ("shard", "group", "expert"), tiled=True)

    def spread(part):
        return trade(jnp.broadcast_to(part, (n_shard,) + part.shape), "shard")

    def gather_rows(weight):
        if not paired:
            return gather_rows_at_once(weight)
        got = spread(sub_rows(weight))
        got = pair_gather(got, "expert", 4, 2, x_at)
        got = pair_gather(got, "group", 2, 1, group_at)
        got = pair_gather(got, "expert", 4, 1, core_at)
        return jnp.transpose(got, (3, 1, 2, 0, 4, 5)).reshape(width, -1)

    def scatter_rows(left, right, extra=None, pending=False):
        if not paired:
            whole = matmul_tn(left, right)
            if extra is not None:
                whole = jnp.concatenate([whole, extra], axis=1)
            return lax.psum_scatter(whole.astype(BF16), ALL, scatter_dimension=0, tiled=True).astype(
                F32
            )
        block = left.shape[1] // 8

        def half(core):
            cols = left.reshape(-1, 4, 2, block)
            cols = lax.dynamic_index_in_dim(cols, core, axis=2, keepdims=False)
            out = matmul_tn(cols.reshape(-1, 4 * block), right)
            if extra is not None:
                more = extra.reshape(4, 2, block, -1)
                more = lax.dynamic_index_in_dim(more, core, axis=1, keepdims=False)
                out = jnp.concatenate([out, more.reshape(4 * block, -1)], axis=1)
            return out

        def swap(rows, axis, count, flip):
            return lax.ppermute(
                rows.astype(BF16), axis, [(i, i ^ flip) for i in range(count)]
            ).astype(F32)

        rows = half(core_at) + swap(half(1 - core_at), "expert", 4, 1)
        for axis, count, flip, bit in (("group", 2, 1, group_at), ("expert", 4, 2, x_at)):
            size = rows.shape[0] // 2
            send = lax.dynamic_slice_in_dim(rows, (1 - bit) * size, size)
            keep = lax.dynamic_slice_in_dim(rows, bit * size, size)
            rows = keep + swap(send, axis, count, flip)
        rows = rows.astype(BF16).reshape(n_shard, -1, rows.shape[1])
        return rows if pending else over_shards(rows)

    def over_shards(rows):
        return jnp.sum(trade(rows, "shard").astype(F32), axis=0)

    expert_count = w_router.shape[1]
    top_count = routes.shape[1]
    route_hot = jnp.any(
        routes[:, :, None] == jnp.arange(expert_count, dtype=jnp.int32)[None, None, :], axis=1
    )
    pos_p = jnp.arange(GROUP_TOK, dtype=jnp.int32)
    pos_p = jnp.where(pos_p < PROMPT, pos_p, PROMPT + pos_p % BLOCK)
    cos_p, sin_p = angles(pos_p, ROPE)
    tok_all = lax.all_gather(tokens, ROW, axis=0, tiled=True)
    hit_b = trade(route_hot.T.astype(F32), ROW) > 0.5
    cotangent_late, cos_p, sin_p, hit_b = lax.optimization_barrier(
        (cotangent, cos_p, sin_p, hit_b)
    )
    c_all = lax.all_gather(cotangent_late, ROW, axis=0, tiled=True)
    units = w_shared_gate.shape[1] // n_row
    wq_h = head_columns(w_query, QDIM)
    wkv_h = head_columns(w_keyval, KVDIM)
    w_lr = gather_rows(jnp.concatenate([w_latent, w_router], axis=1))
    w_l, w_r = w_lr[:, : LATENT + ROPE], w_lr[:, LATENT + ROPE :]
    w_joint = jnp.concatenate([wq_h[:, :NOPE], w_l[:, :LATENT], wq_h[:, NOPE:], w_l[:, LATENT:]], 1)
    w_o_near = w_output
    if paired:
        w_o_near = pair_gather(spread(sub_rows(w_output)), "expert", 4, 2, x_at)
    w_joint, wkv_h, tok_all, w_o_near, w_gate_late, w_up_late = lax.optimization_barrier(
        (w_joint, wkv_h, tok_all, w_o_near, w_shared_gate, w_shared_up)
    )
    w_gu = trade(
        jnp.concatenate([unit_columns(w_gate_late), unit_columns(w_up_late)], axis=-1), "shard"
    ).reshape(width, 2 * units)
    if paired:
        w_o_near = pair_gather(w_o_near, "group", 2, 1, group_at)

    capacity = 3 * tok_rows * top_count // (2 * expert_count)
    ahead = capacity * (jnp.arange(n_row, dtype=jnp.int32)[:, None] % 2)
    place = jnp.where(hit_b, places_of(hit_b) + ahead, 1 << 20).reshape(-1, 1, 2 * tok_rows)

    hidden1, query, key, value, comp = project(
        tok_all.reshape(n_row, BLOCK, width),
        my_blocks,
        gain_attn,
        w_joint,
        gain_latent,
        wkv_h,
        cos_p,
        sin_p,
    )
    mixed_f, mixed_h, total_h = attend(query, key, value)
    mixed_h, w_o_near, w_gu = lax.optimization_barrier((mixed_h, w_o_near, w_gu))
    mixed = heads_home(mixed_h)
    if paired:
        w_o = pair_gather(w_o_near, "expert", 4, 1, core_at)
        w_o = jnp.transpose(w_o, (3, 1, 2, 0, 4, 5)).reshape(width, -1)
    else:
        w_o = gather_rows_at_once(w_o_near)
    padded = -(-(units + expert_count) // 128) * 128
    space = lambda cols: jnp.zeros((width, cols), BF16)
    w_sh = jnp.concatenate(
        [
            w_gu[:, :units],
            w_r,
            space(padded - units - expert_count),
            w_gu[:, units:],
            space(padded - units),
        ],
        axis=1,
    )
    w_sd = lax.dynamic_slice_in_dim(w_shared_down, expert_at * units, units)
    w_sd = jnp.pad(w_sd, ((0, padded - units), (0, 0)))

    inputs = tokens.astype(F32)
    grad_out = cotangent.astype(F32)
    normed1, inverse1 = rms_parts(inputs)
    hidden1_own = (normed1 * gain_attn).astype(BF16)
    latent_own = matmul(hidden1_own, w_l)
    normed_c, inverse_c = rms_parts(latent_own[:, :LATENT])
    after = inputs + matmul(mixed, w_o)
    normed2, inverse2 = rms_parts(after)
    hidden2 = (normed2 * gain_ffn).astype(BF16)
    logits = matmul(hidden2, w_r)
    router_prob = jax.nn.softmax(logits, axis=-1)

    hidden2, c_all = lax.optimization_barrier((hidden2, c_all))
    h2_all = lax.all_gather(hidden2, ROW, axis=0, tiled=True)
    h2_all, w_query = lax.optimization_barrier((h2_all, w_query))
    w_q = gather_rows_at_once(w_query)
    out_a, out_b, dh_part, d_prob_col, rows, d_out, e_mid, d_gate, d_up, s_mid, ds_gu = experts(
        row_at[None],
        place,
        capacity,
        h2_all,
        c_all,
        expert_gate[0],
        expert_up[0],
        expert_down[0],
        w_sh,
        w_sd,
        units,
        expert_count,
    )
    dh_part, w_q = lax.optimization_barrier((dh_part, w_q))
    d_h2 = lax.psum_scatter(dh_part, ROW, scatter_dimension=0, tiled=True)
    d_prob = trade(d_prob_col.reshape(n_row, tok_rows), ROW).T
    d_prob = jnp.where(route_hot, d_prob, 0.0)
    d_logits = (
        router_prob * (d_prob - jnp.sum(router_prob * d_prob, axis=-1, keepdims=True))
    ).astype(BF16)
    grad_router = matmul_tn(hidden2, d_logits)

    def share(whole):
        if n_group != 2:
            return lax.psum_scatter(
                whole.astype(BF16), "group", scatter_dimension=0, tiled=True
            ), None
        half = whole.shape[0] // 2
        send = lax.dynamic_slice_in_dim(whole, (1 - group_at) * half, half).astype(BF16)
        keep = lax.dynamic_slice_in_dim(whole, group_at * half, half)
        return lax.ppermute(send, "group", [(0, 1), (1, 0)]), keep

    whole_0 = matmul_tn(rows, d_gate)
    d_up, ds_gu, whole_0 = lax.optimization_barrier((d_up, ds_gu, whole_0))
    got_0, keep_0 = share(whole_0)
    whole_1 = matmul_tn(rows, d_up)
    grad_gu = matmul_tn(h2_all, ds_gu).astype(BF16)
    e_mid, s_mid, whole_1, got_0, grad_gu = lax.optimization_barrier(
        (e_mid, s_mid, whole_1, got_0, grad_gu)
    )
    got_1, keep_1 = share(whole_1)
    whole_2 = matmul_tn(e_mid, d_out)
    grad_sd_part = matmul_tn(s_mid, c_all)[:units].astype(BF16)
    whole_2, got_1, grad_sd_part = lax.optimization_barrier((whole_2, got_1, grad_sd_part))
    got_2, keep_2 = share(whole_2)
    grad_gu = jnp.concatenate(
        [grad_gu[:, :units], grad_gu[:, padded : padded + units]], axis=1
    ).reshape(n_all, width // n_all, 2 * units)
    grad_sd_part = grad_sd_part.reshape(n_group, units // n_group, width)
    d_h2, out_a, out_b, grad_gu, grad_sd_part = lax.optimization_barrier(
        (d_h2, out_a, out_b, grad_gu, grad_sd_part)
    )
    ffn_a = lax.psum_scatter(out_a, ROW, scatter_dimension=0, tiled=True)

    d_hidden2 = d_h2.astype(F32) + matmul_nt(d_logits, w_r)
    d_after, grad_gain_ffn = norm_back(d_hidden2, normed2, inverse2, gain_ffn)
    grad_after = grad_out + d_after
    grad_attn = grad_after.astype(BF16)
    d_mixed = matmul_nt(grad_attn, w_o).astype(BF16)
    d_mixed_h = heads_out(d_mixed)
    d_mixed_h, grad_gu, grad_sd_part = lax.optimization_barrier((d_mixed_h, grad_gu, grad_sd_part))
    gu_got = trade(grad_gu, ALL)
    sd_gots = []
    for turn in range(n_group):
        piece_at = (group_at + turn) % n_group
        moves = []
        for g in range(n_group):
            for e in range(n_expert):
                for s in range(n_shard):
                    target = (s * n_expert + e) * n_group + (g + turn) % n_group
                    moves.append(((g * n_expert + e) * n_shard + s, target))
        sent = lax.dynamic_index_in_dim(grad_sd_part, piece_at, axis=0, keepdims=False)
        sd_gots.append(lax.ppermute(sent, ALL, moves))

    d_query, d_key, d_value = attend_back(
        query, key, value, mixed_f, total_h, d_mixed_h, cos_p, sin_p
    )
    d_keyval, d_latent_part = latent_back(d_key, d_value, wkv_h, local_slot, mine)
    d_latent_part, ffn_a, got_2, gu_got, sd_gots, grad_attn_late = lax.optimization_barrier(
        (d_latent_part, ffn_a, got_2, gu_got, sd_gots, grad_attn)
    )
    d_lat = lax.psum_scatter(d_latent_part, ROW, scatter_dimension=0, tiled=True)
    d_query_own = heads_home(d_query)
    wo_rows = scatter_rows(mixed, grad_attn_late, pending=True)
    egrads = [
        (got.astype(F32) if keep is None else keep + got.astype(F32))[None]
        for got, keep in ((got_0, keep_0), (got_1, keep_1), (got_2, keep_2))
    ]
    d_lat, d_query_own, wo_rows, egrads, out_b, d_query, d_keyval = lax.optimization_barrier(
        (d_lat, d_query_own, wo_rows, egrads, out_b, d_query, d_keyval)
    )
    egrad_gate, egrad_up, egrad_down = egrads
    d_lat = d_lat.astype(F32)
    ffn_b = lax.psum_scatter(out_b, ROW, scatter_dimension=0, tiled=True)
    grad_wo = over_shards(wo_rows) if paired else wo_rows
    output = (after + jnp.concatenate([ffn_a, ffn_b], axis=1).astype(F32)).astype(BF16)
    got = gu_got.astype(F32)
    got = jnp.sum(got.reshape(n_group, n_expert, n_shard, -1, 2 * units), axis=0)
    got = jnp.transpose(got, (2, 1, 0, 3))
    grad_sg = got[..., :units].reshape(got.shape[0], -1)
    grad_su = got[..., units:].reshape(got.shape[0], -1)
    grad_sd = sum(got.astype(F32) for got in sd_gots)

    grad_wq_h = matmul_tn(hidden1, d_query).astype(BF16).reshape(n_all, width // n_all, QDIM)
    grad_wkv_h = matmul_tn(comp, d_keyval).astype(BF16)
    grad_wkv_h = grad_wkv_h.reshape(n_all, width // n_all, -1)
    got = trade(jnp.concatenate([grad_wq_h, grad_wkv_h], axis=-1), ALL).astype(F32)
    got = jnp.sum(got.reshape(n_group * n_prompt, HEADS, got.shape[1], got.shape[2]), axis=0)
    grad_wq = jnp.swapaxes(got[..., :QDIM], 0, 1).reshape(got.shape[1], -1)
    grad_wkv = jnp.swapaxes(
        got[..., QDIM:].reshape(HEADS, LATENT // n_all, KVDIM), 0, 1
    ).reshape(LATENT // n_all, -1)

    own_pos = lax.dynamic_slice_in_dim(positions, row_at * tok_rows, tok_rows)
    cosine, sine = angles(own_pos, ROPE)
    d_lat_c, grad_gain_latent = norm_back(d_lat[:, :LATENT], normed_c, inverse_c, gain_latent)
    d_latent = jnp.concatenate([d_lat_c, unrotate(d_lat[:, LATENT:], cosine, sine)], axis=1).astype(
        BF16
    )
    d_hidden1 = matmul_nt(d_query_own, w_q) + matmul_nt(d_latent, w_l)
    d_tok, grad_gain_attn = norm_back(d_hidden1, normed1, inverse1, gain_attn)
    grad_tokens = grad_after + d_tok
    own = width // n_all
    lat = LATENT // n_all
    gain_l = jnp.pad(grad_gain_latent.reshape(n_all, lat), ((0, 0), (0, own - lat)))
    beside = jnp.concatenate(
        [
            grad_router,
            grad_gain_attn[:, None],
            grad_gain_ffn[:, None],
            gain_l.reshape(width, 1),
        ],
        axis=1,
    )
    beside = jnp.pad(beside, ((0, 0), (0, -(LATENT + ROPE + expert_count + 3) % 128)))
    sums = scatter_rows(hidden1_own, d_latent, beside)
    grad_wl = sums[:, : LATENT + ROPE]
    at = LATENT + ROPE + expert_count
    grad_r, grad_ga, grad_gf, grad_gl = (
        sums[:, LATENT + ROPE : at],
        sums[:, at],
        sums[:, at + 1],
        sums[:lat, at + 2],
    )
    return (
        output,
        grad_tokens,
        grad_ga,
        grad_wq,
        grad_wl,
        grad_gl,
        grad_wkv,
        grad_wo,
        grad_gf,
        grad_sg,
        grad_su,
        grad_sd,
        grad_r,
        egrad_gate,
        egrad_up,
        egrad_down,
    )


def solution(mesh):
    sizes = tuple(mesh.shape[name] for name in ALL)
    return jax.shard_map(
        functools.partial(per_device, sizes),
        mesh=mesh,
        in_specs=(
            P(ALL, None),
            P(ALL, None),
            P(),
            P("shard", None),
            P("shard", None),
            P(),
            P("shard", None),
            P("shard", None),
            P(),
            P("shard", None),
            P("shard", None),
            P("shard", None),
            P("shard", None),
            P(ROW, None, None),
            P(ROW, None, None),
            P(ROW, None, None),
            P("group"),
            P("group"),
            P(ALL, None),
        ),
        out_specs=(
            P(ALL, None),
            P(ALL, None),
            P(ALL),
            P(ALL, None),
            P(ALL, None),
            P(ALL),
            P(ALL, None),
            P(ALL, None),
            P(ALL),
            P(ALL, None),
            P(ALL, None),
            P(ALL, None),
            P(ALL, None),
            P(ROW, "group", None),
            P(ROW, "group", None),
            P(ROW, "group", None),
        ),
        check_vma=False,
    )
```

time: 1970 us -> 1280 us (0.65)
  matrix products: 469 us -> 134 us
  waiting for transfers between devices: 787 us -> 514 us
  Pallas kernels: 59.1 us -> 254 us
  local copies, waits for them, and re-layouts: 287 us -> 104 us
  blocking collectives: 144 us -> 61.4 us
  other arithmetic: 148 us -> 93.8 us
  starting transfers between devices: 47.2 us -> 87.5 us
    reduce_scatter x5 -> x4, waiting for transfers between devices: 418 us -> 27.1 us  [the longest x1 14.4 us: per_device(): d_h2 = lax.psum_scatter(dh_part, ROW, scatter_dimension=0, tiled=True)]
    pallas_call x0 -> x5, Pallas kernels: none -> 252 us  [the longest x1 145 us: experts(): pl.pallas_call(functools.partial(experts_body, groups, units, count), gri...]
    gather x5 -> x0, local copies, waits for them, and re-layouts: 139 us -> none  [the longest x1 37.8 us: per_device(): picked = jnp.where(hit[:, None], e_out[place].astype(F32), 0.0)]
    dot_general x12 -> x4, matrix products: 150 us -> 20.6 us  [matmul_nt(): lax.dot_general(left, right, (((1,), (1,)), ((), ())), preferred_element_...]
    dot_general x14 -> x4, matrix products: 134 us -> 7.3 us  [matmul(): return jnp.dot(left, right, preferred_element_type=F32)]
    all_gather x2 -> x0, blocking collectives: 88.3 us -> none  [the longest x1 74.8 us: per_device(): routes_all = lax.all_gather(routes, ROW, axis=0, tiled=True)]
    all_gather x1, waiting for transfers between devices: 41.1 us -> 128 us  [per_device(): h2_all = lax.all_gather(hidden2, ROW, axis=0, tiled=True)]
    all_gather x1, waiting for transfers between devices: 81.6 us -> 0.01 us  [per_device(): tok_all = lax.all_gather(tokens, ROW, axis=0, tiled=True)]
  transfers between devices with their start and end apart: 25 -> 38, of which waited for: 13 -> 21; matrix products, arithmetic and copies ran while one was open for 33% -> 24% of each run, Pallas kernels for 3% -> 20%
where the time goes in v2:
time: 1280 us; the launch traced here: 1260 us
  waiting for transfers between devices  514 us (40%)
  Pallas kernels  254 us (20%)
  matrix products  134 us (10%)
  local copies, waits for them, and re-layouts  104 us (8%)
  other arithmetic  93.8 us (7%)
  starting transfers between devices  87.5 us (7%)
  blocking collectives  61.4 us (5%)
  between operations  15.9 us (1%)
    all_to_all x13, waiting for transfers between devices, trade(): return lax.all_to_all(buffer, axes, split_axis=0, concat_axis=0, tiled=True)  182 us
    pallas_call x1, Pallas kernels, experts(): pl.pallas_call(functools.partial(experts_body, groups, units, count), gri...  145 us
    all_gather x1, waiting for transfers between devices, per_device(): h2_all = lax.all_gather(hidden2, ROW, axis=0, tiled=True)  128 us
    dot_general x12, matrix products, matmul_tn(): lax.dot_general(left, right, (((0,), (0,)), ((), ())), preferred_element_...  106 us
    ppermute x6, waiting for transfers between devices, swap(): lax.ppermute(rows.astype(BF16), axis, [(i, i ^ flip) for i in range(count)])  76.6 us
    ppermute x3, waiting for transfers between devices, share(): return (lax.ppermute(send, 'group', [(0, 1), (1, 0)]), keep)  70.9 us
    all_to_all x1, blocking collectives, trade(): return lax.all_to_all(buffer, axes, split_axis=0, concat_axis=0, tiled=True)  61.4 us
    all_to_all x13, starting transfers between devices, trade(): return lax.all_to_all(buffer, axes, split_axis=0, concat_axis=0, tiled=True)  57.5 us
  transfers between devices with their start and end apart: 38, of which 21 were waited for; matrix products, arithmetic and copies ran while one was open for 24% of the time, Pallas kernels for 20%

profile of v2, /device:TPU:0, one launch (start us, length us, event | category | flops | bytes accessed | tf_op | source)
XLA Modules:
  0.0 1264.5 jit_solution(4379504234158272460)
XLA Ops:
  9.9 7.4 all-to-all-start.4
  17.3 9.3 multiply_sine_fusion
  27.6 5.0 all-to-all-start.2
  32.8 16.8 %all-to-all-done.2 = bf16[4,128,256]{1,2,0:T(8,128)(2,1)S(1)} async-done(((bf16[4,128,256]{1,2,0:T(8,128)(2,1)}), bf16[4,128,256]{1,2,0:T(8,128)(2,1)S(1)}, u32[]{:S(2)}, u32[]{:S(2)}) %all-to-all-start.2) | async-done | bytes 262176 | tf_op jit(solution)/shard_map/all_to_all | solution.py:83
  55.4 15.7 %all-to-all-done.1 = bf16[4,64,592]{2,1,0:T(8,128)(2,1)S(1)} async-done(((bf16[4,64,592]{2,1,0:T(8,128)(2,1)}), bf16[4,64,592]{2,1,0:T(8,128)(2,1)S(1)}, u32[]{:S(2)}, u32[]{:S(2)}) %all-to-all-start.1) | async-done | bytes 303136 | tf_op jit(solution)/shard_map/all_to_all | solution.py:83
  77.1 14.2 %collective-permute-done = bf16[4,64,592]{2,1,0:T(8,128)(2,1)S(1)} collective-permute-done((bf16[4,64,592]{2,1,0:T(8,128)(2,1)S(1)}, bf16[4,64,592]{2,1,0:T(8,128)(2,1)S(1)}, u32[]{:S(2)}, u32[]{:S(2)}) %collective-permute-start) | collective-permute-done | bytes 303136 | tf_op jit(solution)/shard_map/ppermute | solution.py:353
  97.9 31.1 %all-to-all-done.3 = bf16[4,64,2048]{2,1,0:T(8,128)(2,1)S(1)} async-done(((bf16[4,64,2048]{2,1,0:T(8,128)(2,1)}), bf16[4,64,2048]{2,1,0:T(8,128)(2,1)S(1)}, u32[]{:S(2)}, u32[]{:S(2)}) %all-to-all-start.3) | async-done | bytes 1048608 | tf_op jit(solution)/shard_map/all_to_all | solution.py:83
  128.9 5.2 all-to-all-start
  141.3 32.9 %all-to-all-done = bf16[4,512,192]{1,2,0:T(8,128)(2,1)} async-done(((bf16[4,512,192]{1,2,0:T(8,128)(2,1)}), bf16[4,512,192]{1,2,0:T(8,128)(2,1)}, u32[]{:S(2)}, u32[]{:S(2)}) %all-to-all-start) | async-done | bytes 786464 | tf_op jit(solution)/shard_map/all_to_all | solution.py:83
  205.7 35.8 %project.1 = (bf16[4096,2048]{1,0:T(8,128)(2,1)}, bf16[4096,192]{1,0:T(8,128)(2,1)S(1)}, bf16[4096,192]{1,0:T(8,128)(2,1)S(1)}, bf16[4096,128]{1,0:T(8,128)(2,1)S(1)}, bf16[4096,512]{1,0:T(8,128)(2,1)}) custom-call(s32[16]{0:T(128)S(1)} %select_reduce_fusion.at_ref.index_ref, bf16[16,256,2048]{2,1,0:T(8,128)(2,1)} %bitcast.224, ...), custom_call_target="tpu_custom_call" | custom-call | flops 14000000000 | bytes 48000000 | tf_op jit(solution)/shard_map/project/pallas_call | solution.py:157
  241.6 23.1 %attend.1 = (f32[4096,128]{1,0:T(8,128)S(1)}, bf16[4096,128]{1,0:T(8,128)(2,1)S(1)}, f32[1,4096]{1,0:T(1,128)S(1)}) custom-call(bf16[4096,192]{1,0:T(8,128)(2,1)S(1)} %get-tuple-element.99.q_ref, bf16[4096,192]{1,0:T(8,128)(2,1)S(1)} %get-tuple-element.100.k_ref, bf16[4096,128]{1,0:T(8,128)(2,1)S(1)} %get-tuple-element.101.v_ref), custom_call_target="tpu_custom_call" | custom-call | flops 6000000000 | bytes 10000000 | tf_op jit(solution)/shard_map/attend/pallas_call | solution.py:226
  266.1 6.0 fusion.3
  274.4 61.4 %all_to_all.87 = bf16[16,256,128]{2,1,0:T(8,128)(2,1)S(1)} all-to-all(bf16[16,256,128]{2,1,0:T(8,128)(2,1)S(1)} %take_blocks.3), channel_id=1, replica_groups=mesh['group'=2,'expert'=4,'shard'=4] {'expert','shard'}, dimensions={0} | all-to-all | bytes 2097152 | tf_op jit(solution)/shard_map/all_to_all | solution.py:83
  336.3 8.0 fusion.1
  350.2 14.5 %all-gather.7.cloned.1.call-done.c_ref = bf16[4096,2048]{1,0:T(8,128)(2,1)} async-done(((bf16[256,2048]{1,0:T(8,128)(2,1)}), bf16[4096,2048]{1,0:T(8,128)(2,1)}) %all-gather.7.cloned.1.call-update) | async-done | bytes 16777232 | tf_op jit(solution)/shard_map/all_gather | solution.py:653
  364.8 128.1 %all-gather.9.cloned.1.call-done.h_ref = bf16[4096,2048]{1,0:T(8,128)(2,1)} async-done(((bf16[256,2048]{1,0:T(8,128)(2,1)}), bf16[4096,2048]{1,0:T(8,128)(2,1)}) %all-gather.9.cloned.1.call-update) | async-done | bytes 16777232 | tf_op jit(solution)/shard_map/all_gather | solution.py:722
  500.6 5.1 concatenate.38.ws_ref
  505.7 144.5 %experts.1 = (bf16[4096,1024]{1,0:T(8,128)(2,1)}, bf16[4096,1024]{1,0:T(8,128)(2,1)}, bf16[4096,2048]{1,0:T(8,128)(2,1)}, f32[8,1,512]{2,1,0:T(1,128)}, bf16[230...) custom-call(s32[1]{0:T(128)} %bitcast.43.me_ref, ...), custom_call_target="tpu_custom_call" | custom-call | flops 105495134208 | bytes 130000000 | tf_op jit(solution)/shard_map/experts/pallas_call | solution.py:452
  650.4 19.3 %fusion.61 = f32[2048,1408]{1,0:T(8,128)S(1)} fusion(bf16[2304,2048]{1,0:T(8,128)(2,1)} %get-tuple-element.121, bf16[2304,1408]{1,0:T(8,128)(2,1)} %get-tuple-element.124), kind=kOutput, calls=%fused_computation.190 | convolution fusion | flops 13287555072 | bytes 27459584 | tf_op jit(solution)/shard_map/dot_general | solution.py:41
  671.6 5.2 copy-done.38
  678.2 13.6 %convolution_convert_fusion.1 = bf16[2048,512]{1,0:T(8,128)(2,1)} fusion(bf16[4096,2048]{1,0:T(8,128)(2,1)} %all-gather.9.cloned.1.call-done.h_ref, bf16[4096,512]{1,0:T(8,128)(2,1)S(1)} %copy-done.80), kind=kOutput, calls=%fused_computation.37 | convolution fusion | flops 8590983168 | bytes 23068672 | tf_op jit(solution)/shard_map/dot_general | solution.py:41
  691.9 19.8 %fusion.62 = f32[2048,1408]{1,0:T(8,128)S(1)} fusion(bf16[2304,2048]{1,0:T(8,128)(2,1)} %get-tuple-element.121, bf16[2304,1408]{1,0:T(8,128)(2,1)} %get-tuple-element.125), kind=kOutput, calls=%fused_computation.191 | convolution fusion | flops 13287555072 | bytes 27459584 | tf_op jit(solution)/shard_map/dot_general | solution.py:41
  711.7 30.0 %collective-permute-done.6 = bf16[1024,1408]{1,0:T(8,128)(2,1)} collective-permute-done((bf16[1024,1408]{1,0:T(8,128)(2,1)}, bf16[1024,1408]{1,0:T(8,128)(2,1)}, u32[]{:S(2)}, u32[]{:S(2)}) %collective-permute-start.6) | collective-permute-done | bytes 2883616 | tf_op jit(solution)/shard_map/ppermute | solution.py:756
  741.7 6.1 fusion.64
  752.3 19.6 %fusion.63 = f32[1408,2048]{1,0:T(8,128)} fusion(bf16[2304,1408]{1,0:T(8,128)(2,1)} %get-tuple-element.129, bf16[2304,2048]{1,0:T(8,128)(2,1)} %get-tuple-element.130), kind=kOutput, calls=%fused_computation.192 | convolution fusion | flops 13287555072 | bytes 27459584 | tf_op jit(solution)/shard_map/dot_general | solution.py:41
  771.9 40.9 %collective-permute-done.7 = bf16[1024,1408]{1,0:T(8,128)(2,1)} collective-permute-done((bf16[1024,1408]{1,0:T(8,128)(2,1)S(1)}, bf16[1024,1408]{1,0:T(8,128)(2,1)}, u32[]{:S(2)}, u32[]{:S(2)}) %collective-permute-start.7) | collective-permute-done | bytes 2883616 | tf_op jit(solution)/shard_map/ppermute | solution.py:756
  812.8 14.4 %reduce-scatter.5.cloned.1.call-done = bf16[256,2048]{1,0:T(8,128)(2,1)} async-done(((bf16[4096,2048]{1,0:T(8,128)(2,1)}), bf16[256,2048]{1,0:T(8,128)(2,1)}) %reduce-scatter.5.cloned.1.call-update) | async-done | bytes 1048592 | tf_op jit(solution)/shard_map/reduce_scatter | solution.py:740
  834.0 6.4 all-to-all-done.7
  846.9 6.5 convolution_convert_fusion.2
  865.1 44.5 %all-to-all-done.8.refs_0_.refs_1_.refs_2_.refs_3_.refs_4_.refs_5_.refs_6_.refs_7_ = bf16[16,256,128]{2,1,0:T(8,128)(2,1)S(1)} async-done(((bf16[16,256,128]{2,1,0:T(8,128)(2,1)}), bf16[16,256,128]{2,1,0:T(8,128)(2,1)S(1)}, u32[]{:S(2)}, u32[]{:S(2)}) %all-to-all-start.8) | async-done | bytes 1048608 | tf_op jit(solution)/shard_map/all_to_all | solution.py:83
  911.3 4.8 all-to-all-start.9
  924.3 35.3 %attend_back.1 = (bf16[4096,192]{1,0:T(8,128)(2,1)S(1)}, f32[4096,192]{1,0:T(8,128)}, f32[4096,128]{1,0:T(8,128)}) custom-call(bf16[4096,192]{1,0:T(8,128)(2,1)} %copy-done.14, bf16[4096,192]{1,0:T(8,128)(2,1)} %copy-done.15, bf16[4096,128]{1,0:T(8,128)(2,1)S(1)} %copy-done.17, bf16[4096,128]{1,0:T(8,128)(2,1)S(1)} %bitcast.171, f32[4096,128]{1,0:T(8,128)} %copy-done.18, ...), custom_call_target="tpu_custom_call" | custom-call | flops 16000000000 | bytes 20000000 | tf_op jit(solution)/shard_map/attend_back/pallas_call | solution.py:285
  959.6 13.5 %latent_back.1 = (bf16[4096,256]{1,0:T(8,128)(2,1)}, bf16[4096,576]{1,0:T(8,128)(2,1)}) custom-call(s32[16]{0:T(128)} %copy-done.10, s32[16]{0:T(128)} %get-tuple-element.292.mine_ref, f32[4096,192]{1,0:T(8,128)} %get-tuple-element.141.dk_ref, f32[4096,128]{1,0:T(8,128)} %get-tuple-element.142.dv_ref, bf16[512,256]{1,0:T(8,128)(2,1)} %bitcast.173), custom_call_target="tpu_custom_call" | custom-call | flops 1100000000 | bytes 14000000 | tf_op jit(solution)/shard_map/latent_back/pallas_call | solution.py:319
  973.1 10.4 reduce-scatter.7.cloned.1.call-done
  987.9 7.4 collective-permute-done.11
  995.3 6.9 convert_add_fusion
  1006.4 9.5 collective-permute-start.12
  1026.6 7.0 add_bitcast_fusion.2
  1033.6 28.7 %collective-permute-done.12 = bf16[512,2048]{1,0:T(8,128)(2,1)} collective-permute-done((bf16[512,2048]{1,0:T(8,128)(2,1)}, bf16[512,2048]{1,0:T(8,128)(2,1)}, u32[]{:S(2)}, u32[]{:S(2)}) %collective-permute-start.12) | collective-permute-done | bytes 2097184 | tf_op jit(solution)/shard_map/ppermute | solution.py:624
  1066.3 4.9 add_bitcast_fusion.1
  1071.2 7.3 add_bitcast_fusion
  1078.5 17.2 %collective-permute-done.13 = bf16[256,2048]{1,0:T(8,128)(2,1)S(1)} collective-permute-done((bf16[256,2048]{1,0:T(8,128)(2,1)S(1)}, bf16[256,2048]{1,0:T(8,128)(2,1)S(1)}, u32[]{:S(2)}, u32[]{:S(2)}) %collective-permute-start.13) | collective-permute-done | bytes 1048608 | tf_op jit(solution)/shard_map/ppermute | solution.py:624
  1121.8 7.6 fusion.65
  1137.2 4.7 all-to-all-start.13
  1141.8 8.6 convolution_convert_fusion.3
  1160.5 32.0 %all-to-all-done.13 = bf16[4,64,2048]{2,1,0:T(8,128)(2,1)} async-done(((bf16[4,64,2048]{2,1,0:T(8,128)(2,1)}), bf16[4,64,2048]{2,1,0:T(8,128)(2,1)}, u32[]{:S(2)}, u32[]{:S(2)}) %all-to-all-start.13) | async-done | bytes 1048608 | tf_op jit(solution)/shard_map/all_to_all | solution.py:83
  1203.9 19.5 %collective-permute-done.15 = bf16[512,640]{0,1:T(8,128)(2,1)S(1)} collective-permute-done((bf16[512,640]{0,1:T(8,128)(2,1)S(1)}, bf16[512,640]{0,1:T(8,128)(2,1)S(1)}, u32[]{:S(2)}, u32[]{:S(2)}) %collective-permute-start.15) | collective-permute-done | bytes 655392 | tf_op jit(solution)/shard_map/ppermute | solution.py:624
  1252.5 4.9 fusion.15
  (376 shorter events, 227.8 us)
Async XLA Ops:
  7.2 181.0 %all-gather.5.cloned.1.call-start = ((), (), s32[]{:S(2)}) async-start(), calls=%async_computation.18 | async-start | bytes 17825792 | tf_op jit(solution)/shard_map/all_gather | solution.py:648
  9.9 16.8 %all-to-all-start.4 = ((f32[16,1,256]{2,1,0:T(1,128)}), f32[16,1,256]{2,1,0:T(1,128)S(1)}, u32[]{:S(2)}, u32[]{:S(2)}) async-start(f32[16,1,256]{2,1,0:T(1,128)} %copy.196), calls=%async_computation.4 | async-start | bytes 32768 | tf_op jit(solution)/shard_map/all_to_all | solution.py:83
  17.2 347.5 %all-gather.7.cloned.1.call-start = ((), (), s32[]{:S(2)}) async-start(), calls=%async_computation.19 | async-start | bytes 17825792 | tf_op jit(solution)/shard_map/all_gather | solution.py:653
  27.6 22.0 %all-to-all-start.2 = ((bf16[4,128,256]{1,2,0:T(8,128)(2,1)}), bf16[4,128,256]{1,2,0:T(8,128)(2,1)S(1)}, u32[]{:S(2)}, u32[]{:S(2)}) async-start(bf16[4,128,256]{1,2,0:T(8,128)(2,1)} %bitcast.14), calls=%async_computation.2 | async-start | bytes 524288 | tf_op jit(solution)/shard_map/all_to_all | solution.py:83
  50.4 20.8 %all-to-all-start.1 = ((bf16[4,64,592]{2,1,0:T(8,128)(2,1)}), bf16[4,64,592]{2,1,0:T(8,128)(2,1)S(1)}, u32[]{:S(2)}, u32[]{:S(2)}) async-start(bf16[4,64,592]{2,1,0:T(8,128)(2,1)} %broadcast_in_dim.42), calls=%async_computation.1 | async-start | bytes 655360 | tf_op jit(solution)/shard_map/all_to_all | solution.py:83
  72.2 56.7 %all-to-all-start.3 = ((bf16[4,64,2048]{2,1,0:T(8,128)(2,1)}), bf16[4,64,2048]{2,1,0:T(8,128)(2,1)S(1)}, u32[]{:S(2)}, u32[]{:S(2)}) async-start(bf16[4,64,2048]{2,1,0:T(8,128)(2,1)} %broadcast_in_dim.43), calls=%async_computation.3 | async-start | bytes 2097152 | tf_op jit(solution)/shard_map/all_to_all | solution.py:83
  75.7 15.6 %collective-permute-start = (bf16[4,64,592]{2,1,0:T(8,128)(2,1)S(1)}, bf16[4,64,592]{2,1,0:T(8,128)(2,1)S(1)}, u32[]{:S(2)}, u32[]{:S(2)}) collective-permute-start(bf16[4,64,592]{2,1,0:T(8,128)(2,1)S(1)} %all-to-all-done.1), channel_id=1, source_target_pairs={{0,8},{4,12},{8,0},{12,4},{1,9},{5,13},{9,1},{13,5},{2,10},{6,14},... | collective-permute-start | bytes 909320 | tf_op jit(solution)/shard_map/ppermute | solution.py:353
  92.6 41.5 %collective-permute-start.1 = (bf16[2,4,64,592]{3,2,0,1:T(8,128)(2,1)}, bf16[2,4,64,592]{3,2,0,1:T(8,128)(2,1)S(1)}, u32[]{:S(2)}, u32[]{:S(2)}) collective-permute-start(bf16[2,4,64,592]{3,2,0,1:T(8,128)(2,1)} %fusion.25), channel_id=1, source_target_pairs={{0,16},{16,0},{1,17},{17,1},{2,18},{18,2},{3,19},{19,3},{4,20},{20... | collective-permute-start | bytes 1818632 | tf_op jit(solution)/shard_map/ppermute | solution.py:353
  128.9 45.2 %all-to-all-start = ((bf16[4,512,192]{1,2,0:T(8,128)(2,1)}), bf16[4,512,192]{1,2,0:T(8,128)(2,1)}, u32[]{:S(2)}, u32[]{:S(2)}) async-start(bf16[4,512,192]{1,2,0:T(8,128)(2,1)} %bitcast.1), calls=%async_computation | async-start | bytes 1572864 | tf_op jit(solution)/shard_map/all_to_all | solution.py:83
  135.9 41.6 %collective-permute-start.2 = (bf16[2,2,4,64,592]{4,3,1,0,2:T(8,128)(2,1)}, bf16[2,2,4,64,592]{4,3,1,0,2:T(8,128)(2,1)}, u32[]{:S(2)}, u32[]{:S(2)}) collective-permute-start(bf16[2,2,4,64,592]{4,3,1,0,2:T(8,128)(2,1)} %fusion.21), channel_id=1, source_target_pairs={{0,4},{4,0},{8,12},{12,8},{1,5},{5,1},{9,13},{13,9},{2,6},{6,2},{1... | collective-permute-start | bytes 3637256 | tf_op jit(solution)/shard_map/ppermute | solution.py:353
  138.2 46.3 %collective-permute-start.3 = (bf16[4,64,2048]{2,1,0:T(8,128)(2,1)S(1)}, bf16[4,64,2048]{2,1,0:T(8,128)(2,1)}, u32[]{:S(2)}, u32[]{:S(2)}) collective-permute-start(bf16[4,64,2048]{2,1,0:T(8,128)(2,1)S(1)} %all-to-all-done.3), channel_id=1, source_target_pairs={{0,8},{4,12},{8,0},{12,4},{1,9},{5,13},{9,1},{13,5},{2,10},{6,14},... | collective-permute-start | bytes 3145736 | tf_op jit(solution)/shard_map/ppermute | solution.py:353
  141.1 64.6 %copy-start.12 = (s32[16]{0:T(128)}, s32[16]{0:T(128)S(1)}, u32[]{:S(2)}) copy-start(s32[16]{0:T(128)S(1)} %select_reduce_fusion.at_ref.index_ref) | copy-start | bytes 196
  141.3 64.4 %copy-start.5 = (bf16[4,128,256]{2,1,0:T(8,128)(2,1)}, bf16[4,128,256]{2,1,0:T(8,128)(2,1)S(1)}, u32[]{:S(2)}) copy-start(bf16[4,128,256]{2,1,0:T(8,128)(2,1)S(1)} %copy.194) | copy-start | bytes 786436
  197.3 68.7 %collective-permute-start.4 = (bf16[2,4,64,2048]{3,2,0,1:T(8,128)(2,1)}, bf16[2,4,64,2048]{3,2,0,1:T(8,128)(2,1)}, u32[]{:S(2)}, u32[]{:S(2)}) collective-permute-start(bf16[2,4,64,2048]{3,2,0,1:T(8,128)(2,1)} %fusion.19), channel_id=1, source_target_pairs={{0,16},{16,0},{1,17},{17,1},{2,18},{18,2},{3,19},{19,3},{4,20},{20... | collective-permute-start | bytes 6291464 | tf_op jit(solution)/shard_map/ppermute | solution.py:353
  201.6 70.5 %all-to-all-start.5 = ((bf16[4,512,352]{1,2,0:T(8,128)(2,1)}), bf16[4,512,352]{1,2,0:T(8,128)(2,1)S(1)}, u32[]{:S(2)}, u32[]{:S(2)}) async-start(bf16[4,512,352]{1,2,0:T(8,128)(2,1)} %pad_maximum_fusion.2), calls=%async_computation.5 | async-start | bytes 2883584 | tf_op jit(solution)/shard_map/all_to_all | solution.py:83
  205.2 287.7 %all-gather.9.cloned.1.call-start = ((), (), s32[]{:S(2)}) async-start(), calls=%async_computation.20 | async-start | bytes 17825792 | tf_op jit(solution)/shard_map/all_gather | solution.py:722
  273.6 62.7 %collective-permute-start.5 = (bf16[2,2,4,64,2048]{4,3,1,0,2:T(8,128)(2,1)}, bf16[2,2,4,64,2048]{4,3,1,0,2:T(8,128)(2,1)}, u32[]{:S(2)}, u32[]{:S(2)}) collective-permute-start(bf16[2,2,4,64,2048]{4,3,1,0,2:T(8,128)(2,1)} %fusion.3), channel_id=1, source_target_pairs={{0,4},{4,0},{8,12},{12,8},{1,5},{5,1},{9,13},{13,9},{2,6},{6,2},{1... | collective-permute-start | bytes 12582920 | tf_op jit(solution)/shard_map/ppermute | solution.py:353
  364.7 134.3 %copy-start.36 = (bf16[4,512,352]{2,1,0:T(8,128)(2,1)S(1)}, bf16[4,512,352]{2,1,0:T(8,128)(2,1)}, u32[]{:S(2)}) copy-start(bf16[4,512,352]{2,1,0:T(8,128)(2,1)} %copy.201) | copy-start | bytes 4325380
  364.7 285.6 %all-gather.11.cloned.1.call-start = ((), (), s32[]{:S(2)}) async-start(), calls=%async_computation.21 | async-start | bytes 12976128 | tf_op jit(solution)/shard_map/all_gather | solution.py:589
  494.7 332.5 %reduce-scatter.5.cloned.1.call-start = ((), (), s32[]{:S(2)}) async-start(), calls=%async_computation.22 | async-start | bytes 17825792 | tf_op jit(solution)/shard_map/reduce_scatter | solution.py:740
  650.3 333.1 %reduce-scatter.7.cloned.1.call-start = ((), (), s32[]{:S(2)}) async-start(), calls=%async_computation.23 | async-start | bytes 8912896 | tf_op jit(solution)/shard_map/reduce_scatter | solution.py:778
  676.8 65.0 %collective-permute-start.6 = (bf16[1024,1408]{1,0:T(8,128)(2,1)}, bf16[1024,1408]{1,0:T(8,128)(2,1)}, u32[]{:S(2)}, u32[]{:S(2)}) collective-permute-start(bf16[1024,1408]{1,0:T(8,128)(2,1)} %dynamic-slice_convert_fusion.2), channel_id=1, source_target_pairs={{0,16},{16,0},{1,17},{17,1},{2,18},{18,2},{3,19},{19,3},{4,20},{20... | collective-permute-start | bytes 8650760 | tf_op jit(solution)/shard_map/ppermute | solution.py:756
  678.2 63.5 %slice-start = ((s8[16777216]{0:T(1024)(128)(4,1)}), s8[4194304]{0:T(1024)(128)(4,1)S(1)}, s32[]{:S(2)}) async-start(s8[16777216]{0:T(1024)(128)(4,1)} %bitcast.178), calls=%async_computation.26 | async-start | bytes 8388608
  678.2 63.5 %slice-start.1 = ((s8[16777216]{0:T(1024)(128)(4,1)}), s8[4194304]{0:T(1024)(128)(4,1)S(1)}, s32[]{:S(2)}) async-start(s8[16777216]{0:T(1024)(128)(4,1)} %bitcast.178), calls=%async_computation.27 | async-start | bytes 8388608
  691.9 49.8 %slice-start.2 = ((s8[16777216]{0:T(1024)(128)(4,1)}), s8[4194304]{0:T(1024)(128)(4,1)S(1)}, s32[]{:S(2)}) async-start(s8[16777216]{0:T(1024)(128)(4,1)} %bitcast.178), calls=%async_computation.28 | async-start | bytes 8388608
  691.9 49.8 %slice-start.3 = ((s8[16777216]{0:T(1024)(128)(4,1)}), s8[4194304]{0:T(1024)(128)(4,1)S(1)}, s32[]{:S(2)}) async-start(s8[16777216]{0:T(1024)(128)(4,1)} %bitcast.178), calls=%async_computation.29 | async-start | bytes 8388608
  748.8 63.9 %collective-permute-start.7 = (bf16[1024,1408]{1,0:T(8,128)(2,1)S(1)}, bf16[1024,1408]{1,0:T(8,128)(2,1)}, u32[]{:S(2)}, u32[]{:S(2)}) collective-permute-start(bf16[1024,1408]{1,0:T(8,128)(2,1)S(1)} %dynamic-slice_convert_fusion.1), channel_id=1, source_target_pairs={{0,16},{16,0},{1,17},{17,1},{2,18},{18,2},{3,19},{19,3},{4,20},{20... | collective-permute-start | bytes 8650760 | tf_op jit(solution)/shard_map/ppermute | solution.py:756
  830.1 10.3 all-to-all-start.7
  855.2 54.4 %all-to-all-start.8 = ((bf16[16,256,128]{2,1,0:T(8,128)(2,1)}), bf16[16,256,128]{2,1,0:T(8,128)(2,1)S(1)}, u32[]{:S(2)}, u32[]{:S(2)}) async-start(bf16[16,256,128]{2,1,0:T(8,128)(2,1)} %bitcast.53), calls=%async_computation.9 | async-start | bytes 2097152 | tf_op jit(solution)/shard_map/all_to_all | solution.py:83
  858.9 50.7 %copy-start.13 = (s32[16]{0:T(128)S(1)}, s32[16]{0:T(128)}, u32[]{:S(2)}) copy-start(s32[16]{0:T(128)} %copy-done.12) | copy-start | bytes 196
  863.5 109.5 %collective-permute-start.8 = (bf16[704,2048]{1,0:T(8,128)(2,1)}, bf16[704,2048]{1,0:T(8,128)(2,1)}, u32[]{:S(2)}, u32[]{:S(2)}) collective-permute-start(bf16[704,2048]{1,0:T(8,128)(2,1)} %dynamic-slice_convert_fusion), channel_id=1, source_target_pairs={{0,16},{16,0},{1,17},{17,1},{2,18},{18,2},{3,19},{19,3},{4,20},{20... | collective-permute-start | bytes 8650760 | tf_op jit(solution)/shard_map/ppermute | solution.py:756
  911.3 61.8 %all-to-all-start.9 = ((bf16[32,64,352]{2,1,0:T(8,128)(2,1)}), bf16[32,64,352]{2,1,0:T(8,128)(2,1)}, u32[]{:S(2)}, u32[]{:S(2)}) async-start(bf16[32,64,352]{2,1,0:T(8,128)(2,1)} %bitcast.194), calls=%async_computation.11 | async-start | bytes 3145728 | tf_op jit(solution)/shard_map/all_to_all | solution.py:83
  916.1 183.2 %reduce-scatter.9.cloned.1.call-start = ((), (), s32[]{:S(2)}) async-start(), calls=%async_computation.24 | async-start | bytes 5570560 | tf_op jit(solution)/shard_map/reduce_scatter | solution.py:807
  918.2 54.9 %collective-permute-start.10 = (bf16[88,2048]{1,0:T(8,128)(2,1)}, bf16[88,2048]{1,0:T(8,128)(2,1)S(1)}, u32[]{:S(2)}, u32[]{:S(2)}) collective-permute-start(bf16[88,2048]{1,0:T(8,128)(2,1)} %get-tuple-element.308), channel_id=1, source_target_pairs={{0,1},{1,9},{2,17},{3,25},{4,3},{5,11},{6,19},{7,27},{8,5},{9,13},... | collective-permute-start | bytes 1081352 | tf_op jit(solution)/shard_map/ppermute | solution.py:798
  919.9 53.2 %collective-permute-start.9 = (bf16[88,2048]{1,0:T(8,128)(2,1)}, bf16[88,2048]{1,0:T(8,128)(2,1)}, u32[]{:S(2)}, u32[]{:S(2)}) collective-permute-start(bf16[88,2048]{1,0:T(8,128)(2,1)} %get-tuple-element.309), channel_id=1, source_target_pairs={{0,0},{1,8},{2,16},{3,24},{4,2},{5,10},{6,18},{7,26},{8,4},{9,12},... | collective-permute-start | bytes 1081352 | tf_op jit(solution)/shard_map/ppermute | solution.py:798
  987.8 7.5 collective-permute-start.11
  1006.4 56.0 %collective-permute-start.12 = (bf16[512,2048]{1,0:T(8,128)(2,1)}, bf16[512,2048]{1,0:T(8,128)(2,1)}, u32[]{:S(2)}, u32[]{:S(2)}) collective-permute-start(bf16[512,2048]{1,0:T(8,128)(2,1)} %dynamic-slice_convert_fusion.3), channel_id=1, source_target_pairs={{0,16},{16,0},{1,17},{17,1},{2,18},{18,2},{3,19},{19,3},{4,20},{20... | collective-permute-start | bytes 6291464 | tf_op jit(solution)/shard_map/ppermute | solution.py:624
  1021.8 75.2 %all-to-all-start.10 = ((bf16[16,256,192]{1,2,0:T(8,128)(2,1)}), bf16[16,256,192]{1,2,0:T(8,128)(2,1)}, u32[]{:S(2)}, u32[]{:S(2)}) async-start(bf16[16,256,192]{1,2,0:T(8,128)(2,1)} %copy.207), calls=%async_computation.13 | async-start | bytes 3145728 | tf_op jit(solution)/shard_map/all_to_all | solution.py:83
  1026.3 226.2 %reduce-scatter.11.cloned.1.call-start = ((), (), s32[]{:S(2)}) async-start(), calls=%async_computation.25 | async-start | bytes 8912896 | tf_op jit(solution)/shard_map/reduce_scatter | solution.py:819
  1026.6 39.7 %slice-start.4 = ((s8[11534336]{0:T(1024)(128)(4,1)}), s8[4194304]{0:T(1024)(128)(4,1)S(1)}, s32[]{:S(2)}) async-start(s8[11534336]{0:T(1024)(128)(4,1)} %bitcast.192), calls=%async_computation.30 | async-start | bytes 8388608
  1026.6 39.7 %slice-start.5 = ((s8[11534336]{0:T(1024)(128)(4,1)}), s8[4194304]{0:T(1024)(128)(4,1)S(1)}, s32[]{:S(2)}) async-start(s8[11534336]{0:T(1024)(128)(4,1)} %bitcast.192), calls=%async_computation.31 | async-start | bytes 8388608
  1066.2 29.5 %collective-permute-start.13 = (bf16[256,2048]{1,0:T(8,128)(2,1)S(1)}, bf16[256,2048]{1,0:T(8,128)(2,1)S(1)}, u32[]{:S(2)}, u32[]{:S(2)}) collective-permute-start(bf16[256,2048]{1,0:T(8,128)(2,1)S(1)} %dynamic-slice_convert_fusion.4), channel_id=1, source_target_pairs={{0,8},{4,12},{8,0},{12,4},{1,9},{5,13},{9,1},{13,5},{2,10},{6,14},... | collective-permute-start | bytes 3145736 | tf_op jit(solution)/shard_map/ppermute | solution.py:624
  1137.2 58.3 %collective-permute-start.14 = (bf16[1024,640]{0,1:T(8,128)(2,1)}, bf16[1024,640]{0,1:T(8,128)(2,1)}, u32[]{:S(2)}, u32[]{:S(2)}) collective-permute-start(bf16[1024,640]{0,1:T(8,128)(2,1)} %pad_maximum_fusion.3), channel_id=1, source_target_pairs={{0,4},{4,0},{8,12},{12,8},{1,5},{5,1},{9,13},{13,9},{2,6},{6,2},{1... | collective-permute-start | bytes 3932168 | tf_op jit(solution)/shard_map/ppermute | solution.py:624
  1137.2 55.3 %all-to-all-start.13 = ((bf16[4,64,2048]{2,1,0:T(8,128)(2,1)}), bf16[4,64,2048]{2,1,0:T(8,128)(2,1)}, u32[]{:S(2)}, u32[]{:S(2)}) async-start(bf16[4,64,2048]{2,1,0:T(8,128)(2,1)} %bitcast.63), calls=%async_computation.17 | async-start | bytes 2097152 | tf_op jit(solution)/shard_map/all_to_all | solution.py:83
  1192.5 43.6 %all-to-all-start.12 = ((bf16[32,64,256]{2,1,0:T(8,128)(2,1)}), bf16[32,64,256]{2,1,0:T(8,128)(2,1)S(1)}, u32[]{:S(2)}, u32[]{:S(2)}) async-start(bf16[32,64,256]{2,1,0:T(8,128)(2,1)} %pad_maximum_fusion.4), calls=%async_computation.16 | async-start | bytes 2097152 | tf_op jit(solution)/shard_map/all_to_all | solution.py:83
  1198.2 25.2 %collective-permute-start.15 = (bf16[512,640]{0,1:T(8,128)(2,1)S(1)}, bf16[512,640]{0,1:T(8,128)(2,1)S(1)}, u32[]{:S(2)}, u32[]{:S(2)}) collective-permute-start(bf16[512,640]{0,1:T(8,128)(2,1)S(1)} %dynamic-slice_convert_fusion.5), channel_id=1, source_target_pairs={{0,16},{16,0},{1,17},{17,1},{2,18},{18,2},{3,19},{19,3},{4,20},{20... | collective-permute-start | bytes 1966088 | tf_op jit(solution)/shard_map/ppermute | solution.py:624
  1223.7 10.2 collective-permute-start.16
  1236.1 14.2 %all-to-all-start.11 = ((bf16[4,64,640]{2,1,0:T(8,128)(2,1)}), bf16[4,64,640]{2,1,0:T(8,128)(2,1)S(1)}, u32[]{:S(2)}, u32[]{:S(2)}) async-start(bf16[4,64,640]{2,1,0:T(8,128)(2,1)} %bitcast.71), calls=%async_computation.15 | async-start | bytes 655360 | tf_op jit(solution)/shard_map/all_to_all | solution.py:83
  (79 other events, 600.0 us)
Sparse Core Ops, SparseCore 0:
  10.2 177.2 all-gather.4
  189.7 174.9 all-gather.6
  366.9 125.9 all-gather.8
  496.2 94.1 all-gather.10
  650.5 176.6 reduce-scatter.4
  831.1 152.3 reduce-scatter.6
  988.1 111.1 reduce-scatter.8
  1103.3 136.1 reduce-scatter.10

commit v3 on v2

--- a/solution.py
+++ b/solution.py
@@ -20,6 +20,7 @@
 KVDIM = NOPE + VDIM
 GROUP_BLOCKS = PROMPT // BLOCK + NCONT
 GROUP_TOK = GROUP_BLOCKS * BLOCK
+SIDE = 512
 
 EPS = 1e-06
 ALL = ("group", "expert", "shard")
@@ -359,13 +360,19 @@
 
 
 def experts_body(
-    groups, units, count, me_ref, place_ref, h_ref, c_ref, wg_ref, wu_ref, wd_ref, ws_ref, wsd_ref,
-    outa_ref, outb_ref, dh_ref, dprob_ref, rows_ref, dout_ref, mid_ref, dg_ref, du_ref, smid_ref, ds_ref,
-    crow_ref,
+    groups, units, count, n_parts, me_ref, place_ref, h_ref, c_ref, wg_ref, wu_ref, wd_ref, ws_ref,
+    wsd_ref, outa_ref, outb_ref, *refs,
 ):
+    dh_refs = refs[:n_parts]
+    dprob_ref, rows_ref, dout_ref, mid_ref, dg_ref, du_ref, smid_ref, ds_ref, crow_ref = refs[
+        n_parts:
+    ]
     width, hidden = wg_ref.shape
     padded = wsd_ref.shape[0]
     h, c = h_ref[...], c_ref[...]
+    ends = [0]
+    for ref in dh_refs:
+        ends.append(ends[-1] + ref.shape[1])
 
     wide = dot(h, ws_ref[...], 1, 0)
     s_gate, s_up = wide[:, :padded], wide[:, padded:]
@@ -420,7 +427,11 @@
                 dot(pick, out[rows, :], 0, 0) + shared
             ).astype(BF16)
             shared = dot(ds_ref[toks, :], ws_ref[cols, :], 1, 1)
-            dh_ref[toks, cols] = (dot(pick, d_rows[rows, :], 0, 0) + shared).astype(BF16)
+            for ref, start, stop in zip(dh_refs, ends, ends[1:]):
+                if start <= cols.start < stop:
+                    ref[toks, cols.start - start : cols.stop - start] = (
+                        dot(pick, d_rows[rows, :], 0, 0) + shared
+                    ).astype(BF16)
     for rows, toks, here, pick in picks:
         dprob_ref[0, :, toks] = jnp.sum(
             jnp.where(here, d_prob[rows, :], 0.0), axis=0, keepdims=True
@@ -428,10 +439,12 @@
 
 
 def experts(
-    me, place, capacity, hidden2, cotangent, w_gate, w_up, w_down, w_shared, w_sdown, units, count
+    me, place, capacity, hidden2, cotangent, w_gate, w_up, w_down, w_shared, w_sdown, units, count,
+    widths,
 ):
-    tokens, width = hidden2.shape
-    hidden = w_gate.shape[1]
+    width, hidden = w_gate.shape
+    tokens = cotangent.shape[0]
+    n_parts = len(widths)
     padded = w_sdown.shape[0]
     blocks = 2
     step = blocks * BLOCK
@@ -449,8 +462,8 @@
     line = pl.BlockSpec((1, 1, step), lambda i, me: (i, 0, 0))
     shape = lambda rows, cols, kind=BF16: jax.ShapeDtypeStruct((rows, cols), kind)
     flops = 2 * steps * (6 * room * width * hidden + 6 * step * width * padded)
-    return pl.pallas_call(
-        functools.partial(experts_body, groups, units, count),
+    outs = pl.pallas_call(
+        functools.partial(experts_body, groups, units, count, n_parts),
         grid_spec=pltpu.PrefetchScalarGridSpec(
             num_scalar_prefetch=1,
             grid=(steps,),
@@ -459,7 +472,8 @@
                 once(w_gate), once(w_up), once(w_down), once(w_shared), once(w_sdown),
             ],
             out_specs=[
-                tiled(step, width // 2), tiled(step, width // 2), tiled(step, width), line,
+                tiled(step, width // 2), tiled(step, width // 2),
+                *[tiled(step, cols) for cols in widths], line,
                 tiled(room, width),
                 tiled(room, width), tiled(room, hidden), tiled(room, hidden),
                 tiled(room, hidden), tiled(step, padded), tiled(step, 2 * padded),
@@ -467,7 +481,8 @@
             scratch_shapes=[pltpu.VMEM((room, width), BF16)],
         ),
         out_shape=[
-            shape(tokens, width // 2), shape(tokens, width // 2), shape(tokens, width),
+            shape(tokens, width // 2), shape(tokens, width // 2),
+            *[shape(tokens, cols) for cols in widths],
             jax.ShapeDtypeStruct((steps, 1, step), F32),
             shape(steps * room, width), shape(steps * room, width), shape(steps * room, hidden),
             shape(steps * room, hidden), shape(steps * room, hidden), shape(tokens, padded),
@@ -479,6 +494,7 @@
         ),
         name="experts",
     )(me, place, hidden2, cotangent, w_gate, w_up, w_down, w_shared, w_sdown)
+    return [*outs[:2], list(outs[2 : 2 + n_parts]), *outs[2 + n_parts :]]
 
 def places_of(hit):
     count = hit.shape[1]
@@ -591,6 +607,18 @@
     def spread(part):
         return trade(jnp.broadcast_to(part, (n_shard,) + part.shape), "shard")
 
+    def scatter_rows_of_row(part):
+        part = part.reshape(2, 2, n_shard * tok_rows, -1)
+
+        def halve(rows, axis, bit, flip):
+            send = lax.dynamic_index_in_dim(rows, 1 - bit, axis, keepdims=False)
+            keep = lax.dynamic_index_in_dim(rows, bit, axis, keepdims=False)
+            got = lax.ppermute(send, "expert", [(i, i ^ flip) for i in range(4)])
+            return (keep.astype(F32) + got.astype(F32)).astype(BF16)
+
+        part = halve(halve(part, 1, core_at, 1), 0, x_at, 2)
+        return over_shards(part.reshape(n_shard, tok_rows, -1))
+
     def gather_rows(weight):
         if not paired:
             return gather_rows_at_once(weight)
@@ -600,14 +628,17 @@
         got = pair_gather(got, "expert", 4, 1, core_at)
         return jnp.transpose(got, (3, 1, 2, 0, 4, 5)).reshape(width, -1)
 
-    def scatter_rows(left, right, extra=None, pending=False):
+    def swap(rows, axis, count, flip):
+        return lax.ppermute(
+            rows.astype(BF16), axis, [(i, i ^ flip) for i in range(count)]
+        ).astype(F32)
+
+    def scatter_start(left, right, extra=None):
         if not paired:
             whole = matmul_tn(left, right)
             if extra is not None:
                 whole = jnp.concatenate([whole, extra], axis=1)
-            return lax.psum_scatter(whole.astype(BF16), ALL, scatter_dimension=0, tiled=True).astype(
-                F32
-            )
+            return whole
         block = left.shape[1] // 8
 
         def half(core):
@@ -620,19 +651,27 @@
                 out = jnp.concatenate([out, more.reshape(4 * block, -1)], axis=1)
             return out
 
-        def swap(rows, axis, count, flip):
-            return lax.ppermute(
-                rows.astype(BF16), axis, [(i, i ^ flip) for i in range(count)]
-            ).astype(F32)
-
-        rows = half(core_at) + swap(half(1 - core_at), "expert", 4, 1)
-        for axis, count, flip, bit in (("group", 2, 1, group_at), ("expert", 4, 2, x_at)):
-            size = rows.shape[0] // 2
-            send = lax.dynamic_slice_in_dim(rows, (1 - bit) * size, size)
-            keep = lax.dynamic_slice_in_dim(rows, bit * size, size)
-            rows = keep + swap(send, axis, count, flip)
-        rows = rows.astype(BF16).reshape(n_shard, -1, rows.shape[1])
-        return rows if pending else over_shards(rows)
+        return half(core_at) + swap(half(1 - core_at), "expert", 4, 1)
+
+    def scatter_step(rows, axis, count, flip, bit):
+        if not paired:
+            return rows
+        size = rows.shape[0] // 2
+        send = lax.dynamic_slice_in_dim(rows, (1 - bit) * size, size)
+        return lax.dynamic_slice_in_dim(rows, bit * size, size) + swap(send, axis, count, flip)
+
+    def scatter_y(rows):
+        return scatter_step(rows, "group", 2, 1, group_at)
+
+    def scatter_x(rows):
+        return scatter_step(rows, "expert", 4, 2, x_at)
+
+    def scatter_end(rows):
+        if not paired:
+            return lax.psum_scatter(rows.astype(BF16), ALL, scatter_dimension=0, tiled=True).astype(
+                F32
+            )
+        return over_shards(rows.astype(BF16).reshape(n_shard, -1, rows.shape[1]))
 
     def over_shards(rows):
         return jnp.sum(trade(rows, "shard").astype(F32), axis=0)
@@ -660,12 +699,11 @@
     w_o_near = w_output
     if paired:
         w_o_near = pair_gather(spread(sub_rows(w_output)), "expert", 4, 2, x_at)
-    w_joint, wkv_h, tok_all, w_o_near, w_gate_late, w_up_late = lax.optimization_barrier(
-        (w_joint, wkv_h, tok_all, w_o_near, w_shared_gate, w_shared_up)
-    )
-    w_gu = trade(
-        jnp.concatenate([unit_columns(w_gate_late), unit_columns(w_up_late)], axis=-1), "shard"
-    ).reshape(width, 2 * units)
+    gu_parts = jnp.concatenate([unit_columns(w_shared_gate), unit_columns(w_shared_up)], axis=-1)
+    w_joint, wkv_h, tok_all, w_o_near, gu_parts = lax.optimization_barrier(
+        (w_joint, wkv_h, tok_all, w_o_near, gu_parts)
+    )
+    w_gu = trade(gu_parts, "shard").reshape(width, 2 * units)
     if paired:
         w_o_near = pair_gather(w_o_near, "group", 2, 1, group_at)
 
@@ -718,11 +756,11 @@
     logits = matmul(hidden2, w_r)
     router_prob = jax.nn.softmax(logits, axis=-1)
 
-    hidden2, c_all = lax.optimization_barrier((hidden2, c_all))
+    hidden2, c_all, w_sh = lax.optimization_barrier((hidden2, c_all, w_sh))
     h2_all = lax.all_gather(hidden2, ROW, axis=0, tiled=True)
     h2_all, w_query = lax.optimization_barrier((h2_all, w_query))
     w_q = gather_rows_at_once(w_query)
-    out_a, out_b, dh_part, d_prob_col, rows, d_out, e_mid, d_gate, d_up, s_mid, ds_gu = experts(
+    out_a, out_b, dh_parts, d_prob_col, rows, d_out, e_mid, d_gate, d_up, s_mid, ds_gu = experts(
         row_at[None],
         place,
         capacity,
@@ -735,10 +773,13 @@
         w_sd,
         units,
         expert_count,
-    )
-    dh_part, w_q = lax.optimization_barrier((dh_part, w_q))
-    d_h2 = lax.psum_scatter(dh_part, ROW, scatter_dimension=0, tiled=True)
+        [width - SIDE, SIDE] if paired else [width],
+    )
     d_prob = trade(d_prob_col.reshape(n_row, tok_rows), ROW).T
+    dh_parts, w_q = lax.optimization_barrier((dh_parts, w_q))
+    d_h2 = lax.psum_scatter(dh_parts[0], ROW, scatter_dimension=0, tiled=True).astype(F32)
+    if paired:
+        d_h2 = jnp.concatenate([d_h2, scatter_rows_of_row(dh_parts[1])], axis=1)
     d_prob = jnp.where(route_hot, d_prob, 0.0)
     d_logits = (
         router_prob * (d_prob - jnp.sum(router_prob * d_prob, axis=-1, keepdims=True))
@@ -766,24 +807,29 @@
     got_1, keep_1 = share(whole_1)
     whole_2 = matmul_tn(e_mid, d_out)
     grad_sd_part = matmul_tn(s_mid, c_all)[:units].astype(BF16)
-    whole_2, got_1, grad_sd_part = lax.optimization_barrier((whole_2, got_1, grad_sd_part))
+    d_h2, whole_2, grad_sd_part = lax.optimization_barrier((d_h2, whole_2, grad_sd_part))
+    whole_2, _ = lax.optimization_barrier((whole_2, got_1))
     got_2, keep_2 = share(whole_2)
     grad_gu = jnp.concatenate(
         [grad_gu[:, :units], grad_gu[:, padded : padded + units]], axis=1
     ).reshape(n_all, width // n_all, 2 * units)
     grad_sd_part = grad_sd_part.reshape(n_group, units // n_group, width)
-    d_h2, out_a, out_b, grad_gu, grad_sd_part = lax.optimization_barrier(
-        (d_h2, out_a, out_b, grad_gu, grad_sd_part)
+    d_h2, out_a, out_b, grad_gu, grad_sd_part, grad_router, d_logits = lax.optimization_barrier(
+        (d_h2, out_a, out_b, grad_gu, grad_sd_part, grad_router, d_logits)
     )
     ffn_a = lax.psum_scatter(out_a, ROW, scatter_dimension=0, tiled=True)
 
-    d_hidden2 = d_h2.astype(F32) + matmul_nt(d_logits, w_r)
+    d_hidden2 = d_h2 + matmul_nt(d_logits, w_r)
     d_after, grad_gain_ffn = norm_back(d_hidden2, normed2, inverse2, gain_ffn)
     grad_after = grad_out + d_after
     grad_attn = grad_after.astype(BF16)
     d_mixed = matmul_nt(grad_attn, w_o).astype(BF16)
     d_mixed_h = heads_out(d_mixed)
-    d_mixed_h, grad_gu, grad_sd_part = lax.optimization_barrier((d_mixed_h, grad_gu, grad_sd_part))
+    wo_rows = scatter_start(mixed, grad_attn)
+    d_mixed_h, grad_gu, grad_sd_part, got_1, wo_rows = lax.optimization_barrier(
+        (d_mixed_h, grad_gu, grad_sd_part, got_1, wo_rows)
+    )
+    wo_rows = scatter_y(wo_rows)
     gu_got = trade(grad_gu, ALL)
     sd_gots = []
     for turn in range(n_group):
@@ -801,23 +847,29 @@
         query, key, value, mixed_f, total_h, d_mixed_h, cos_p, sin_p
     )
     d_keyval, d_latent_part = latent_back(d_key, d_value, wkv_h, local_slot, mine)
-    d_latent_part, ffn_a, got_2, gu_got, sd_gots, grad_attn_late = lax.optimization_barrier(
-        (d_latent_part, ffn_a, got_2, gu_got, sd_gots, grad_attn)
+    own_pos = lax.dynamic_slice_in_dim(positions, row_at * tok_rows, tok_rows)
+    cosine, sine = angles(own_pos, ROPE)
+    d_latent_part, ffn_a, gu_got, sd_gots, wo_rows, cosine, sine = lax.optimization_barrier(
+        (d_latent_part, ffn_a, gu_got, sd_gots, wo_rows, cosine, sine)
     )
     d_lat = lax.psum_scatter(d_latent_part, ROW, scatter_dimension=0, tiled=True)
     d_query_own = heads_home(d_query)
-    wo_rows = scatter_rows(mixed, grad_attn_late, pending=True)
+    grad_wq_h = matmul_tn(hidden1, d_query).astype(BF16).reshape(n_all, width // n_all, QDIM)
+    grad_wkv_h = matmul_tn(comp, d_keyval).astype(BF16)
+    grad_wkv_h = grad_wkv_h.reshape(n_all, width // n_all, -1)
+    head_got = trade(jnp.concatenate([grad_wq_h, grad_wkv_h], axis=-1), ALL)
+    wo_rows = scatter_x(wo_rows)
     egrads = [
         (got.astype(F32) if keep is None else keep + got.astype(F32))[None]
         for got, keep in ((got_0, keep_0), (got_1, keep_1), (got_2, keep_2))
     ]
-    d_lat, d_query_own, wo_rows, egrads, out_b, d_query, d_keyval = lax.optimization_barrier(
-        (d_lat, d_query_own, wo_rows, egrads, out_b, d_query, d_keyval)
+    d_lat, d_query_own, wo_rows, egrads, out_b, head_got = lax.optimization_barrier(
+        (d_lat, d_query_own, wo_rows, egrads, out_b, head_got)
     )
     egrad_gate, egrad_up, egrad_down = egrads
     d_lat = d_lat.astype(F32)
     ffn_b = lax.psum_scatter(out_b, ROW, scatter_dimension=0, tiled=True)
-    grad_wo = over_shards(wo_rows) if paired else wo_rows
+    grad_wo = scatter_end(wo_rows)
     output = (after + jnp.concatenate([ffn_a, ffn_b], axis=1).astype(F32)).astype(BF16)
     got = gu_got.astype(F32)
     got = jnp.sum(got.reshape(n_group, n_expert, n_shard, -1, 2 * units), axis=0)
@@ -826,18 +878,13 @@
     grad_su = got[..., units:].reshape(got.shape[0], -1)
     grad_sd = sum(got.astype(F32) for got in sd_gots)
 
-    grad_wq_h = matmul_tn(hidden1, d_query).astype(BF16).reshape(n_all, width // n_all, QDIM)
-    grad_wkv_h = matmul_tn(comp, d_keyval).astype(BF16)
-    grad_wkv_h = grad_wkv_h.reshape(n_all, width // n_all, -1)
-    got = trade(jnp.concatenate([grad_wq_h, grad_wkv_h], axis=-1), ALL).astype(F32)
+    got = head_got.astype(F32)
     got = jnp.sum(got.reshape(n_group * n_prompt, HEADS, got.shape[1], got.shape[2]), axis=0)
     grad_wq = jnp.swapaxes(got[..., :QDIM], 0, 1).reshape(got.shape[1], -1)
     grad_wkv = jnp.swapaxes(
         got[..., QDIM:].reshape(HEADS, LATENT // n_all, KVDIM), 0, 1
     ).reshape(LATENT // n_all, -1)
 
-    own_pos = lax.dynamic_slice_in_dim(positions, row_at * tok_rows, tok_rows)
-    cosine, sine = angles(own_pos, ROPE)
     d_lat_c, grad_gain_latent = norm_back(d_lat[:, :LATENT], normed_c, inverse_c, gain_latent)
     d_latent = jnp.concatenate([d_lat_c, unrotate(d_lat[:, LATENT:], cosine, sine)], axis=1).astype(
         BF16
@@ -858,7 +905,7 @@
         axis=1,
     )
     beside = jnp.pad(beside, ((0, 0), (0, -(LATENT + ROPE + expert_count + 3) % 128)))
-    sums = scatter_rows(hidden1_own, d_latent, beside)
+    sums = scatter_end(scatter_x(scatter_y(scatter_start(hidden1_own, d_latent, beside))))
     grad_wl = sums[:, : LATENT + ROPE]
     at = LATENT + ROPE + expert_count
     grad_r, grad_ga, grad_gf, grad_gl = (

time: 1280 us -> 1230 us (0.961); the launches traced: 1260 us -> 1230 us
  blocking collectives: 61.4 us -> 0 us
    all_to_all x13 -> x15, waiting for transfers between devices: 182 us -> 251 us  [trade(): return lax.all_to_all(buffer, axes, split_axis=0, concat_axis=0, tiled=True)]
    all_to_all x1 -> x0, blocking collectives: 61.4 us -> none  [trade(): return lax.all_to_all(buffer, axes, split_axis=0, concat_axis=0, tiled=True)]
    ppermute x6, waiting for transfers between devices: 76.6 us -> 19.7 us  [swap(): lax.ppermute(rows.astype(BF16), axis, [(i, i ^ flip) for i in range(count)])]
    ppermute x3, waiting for transfers between devices: 70.9 us -> 42 us  [share(): return (lax.ppermute(send, 'group', [(0, 1), (1, 0)]), keep)]
    all_to_all x13 -> x15, starting transfers between devices: 57.5 us -> 74 us  [trade(): return lax.all_to_all(buffer, axes, split_axis=0, concat_axis=0, tiled=True)]
    reduce_scatter x1, waiting for transfers between devices: 0.01 us -> 15.4 us  [per_device(): ffn_b = lax.psum_scatter(out_b, ROW, scatter_dimension=0, tiled=True)]
    reduce_scatter x1, waiting for transfers between devices: 14.4 us -> 0.01 us  [per_device(): lax.psum_scatter(dh_parts[0], ROW, scatter_dimension=0, tiled=True)]
    unnamed x184 -> x154, local copies, waits for them, and re-layouts: 28.7 us -> 33.1 us
  transfers between devices with their start and end apart: 38 -> 42, of which waited for: 21 -> 24; matrix products, arithmetic and copies ran while one was open for 24% -> 26% of each run, Pallas kernels for 20% -> 22%
where the time goes in v3:
time: 1230 us
  waiting for transfers between devices  504 us (41%)
  Pallas kernels  266 us (22%)
  matrix products  136 us (11%)
  local copies, waits for them, and re-layouts  106 us (9%)
  other arithmetic  104 us (8%)
  starting transfers between devices  97.3 us (8%)
  between operations  15.7 us (1%)
    all_to_all x15, waiting for transfers between devices, trade(): return lax.all_to_all(buffer, axes, split_axis=0, concat_axis=0, tiled=True)  251 us
    pallas_call x1, Pallas kernels, experts(): pl.pallas_call(functools.partial(experts_body, groups, units, count, n_pa...  155 us
    all_gather x1, waiting for transfers between devices, per_device(): h2_all = lax.all_gather(hidden2, ROW, axis=0, tiled=True)  129 us
    dot_general x12, matrix products, matmul_tn(): lax.dot_general(left, right, (((0,), (0,)), ((), ())), preferred_element_...  110 us
    all_to_all x15, starting transfers between devices, trade(): return lax.all_to_all(buffer, axes, split_axis=0, concat_axis=0, tiled=True)  74 us
    ppermute x3, waiting for transfers between devices, share(): return (lax.ppermute(send, 'group', [(0, 1), (1, 0)]), keep)  42 us
    pallas_call x1, Pallas kernels, project(): pl.pallas_call(project_body, grid_spec=pltpu.PrefetchScalarGridSpec(num_s...  36.4 us
    pallas_call x1, Pallas kernels, attend_back(): pl.pallas_call(attend_back_body, grid=(TILES,), in_specs=[tiled(QDIM), wh...  35.3 us
  transfers between devices with their start and end apart: 42, of which 24 were waited for; matrix products, arithmetic and copies ran while one was open for 26% of the time, Pallas kernels for 22%

profile of v3, /device:TPU:0, one launch (start us, length us, event | category | flops | bytes accessed | tf_op | source)
XLA Modules:
  0.0 1227.9 jit_solution(15844589356972365591)
XLA Ops:
  9.9 7.4 all-to-all-start.4
  17.8 9.3 multiply_sine_fusion
  28.1 5.0 all-to-all-start.2
  33.3 16.7 %all-to-all-done.2 = bf16[4,128,256]{1,2,0:T(8,128)(2,1)S(1)} async-done(((bf16[4,128,256]{1,2,0:T(8,128)(2,1)}), bf16[4,128,256]{1,2,0:T(8,128)(2,1)S(1)}, u32[]{:S(2)}, u32[]{:S(2)}) %all-to-all-start.2) | async-done | bytes 262176 | tf_op jit(solution)/shard_map/all_to_all | solution.py:84
  55.6 15.9 %all-to-all-done.1 = bf16[4,64,592]{2,1,0:T(8,128)(2,1)S(1)} async-done(((bf16[4,64,592]{2,1,0:T(8,128)(2,1)}), bf16[4,64,592]{2,1,0:T(8,128)(2,1)S(1)}, u32[]{:S(2)}, u32[]{:S(2)}) %all-to-all-start.1) | async-done | bytes 303136 | tf_op jit(solution)/shard_map/all_to_all | solution.py:84
  77.6 14.4 %collective-permute-done = bf16[4,64,592]{2,1,0:T(8,128)(2,1)S(1)} collective-permute-done((bf16[4,64,592]{2,1,0:T(8,128)(2,1)S(1)}, bf16[4,64,592]{2,1,0:T(8,128)(2,1)S(1)}, u32[]{:S(2)}, u32[]{:S(2)}) %collective-permute-start) | collective-permute-done | bytes 303136 | tf_op jit(solution)/shard_map/ppermute | solution.py:354
  98.4 31.1 %all-to-all-done.3 = bf16[4,64,2048]{2,1,0:T(8,128)(2,1)S(1)} async-done(((bf16[4,64,2048]{2,1,0:T(8,128)(2,1)}), bf16[4,64,2048]{2,1,0:T(8,128)(2,1)S(1)}, u32[]{:S(2)}, u32[]{:S(2)}) %all-to-all-start.3) | async-done | bytes 1048608 | tf_op jit(solution)/shard_map/all_to_all | solution.py:84
  129.5 5.5 all-to-all-start
  152.1 22.4 %all-to-all-done = bf16[4,512,192]{1,2,0:T(8,128)(2,1)} async-done(((bf16[4,512,192]{1,2,0:T(8,128)(2,1)}), bf16[4,512,192]{1,2,0:T(8,128)(2,1)}, u32[]{:S(2)}, u32[]{:S(2)}) %all-to-all-start) | async-done | bytes 786464 | tf_op jit(solution)/shard_map/all_to_all | solution.py:84
  196.0 36.4 %project.1 = (bf16[4096,2048]{1,0:T(8,128)(2,1)}, bf16[4096,192]{1,0:T(8,128)(2,1)S(1)}, bf16[4096,192]{1,0:T(8,128)(2,1)S(1)}, bf16[4096,128]{1,0:T(8,128)(2,1)S(1)}, bf16[4096,512]{1,0:T(8,128)(2,1)}) custom-call(s32[16]{0:T(128)S(1)} %select_reduce_fusion.at_ref.index_ref, bf16[16,256,2048]{2,1,0:T(8,128)(2,1)} %bitcast.234, ...), custom_call_target="tpu_custom_call" | custom-call | flops 14000000000 | bytes 48000000 | tf_op jit(solution)/shard_map/project/pallas_call | solution.py:158
  232.5 23.2 %attend.1 = (f32[4096,128]{1,0:T(8,128)S(1)}, bf16[4096,128]{1,0:T(8,128)(2,1)S(1)}, f32[1,4096]{1,0:T(1,128)S(1)}) custom-call(bf16[4096,192]{1,0:T(8,128)(2,1)S(1)} %get-tuple-element.106.q_ref, bf16[4096,192]{1,0:T(8,128)(2,1)S(1)} %get-tuple-element.107.k_ref, bf16[4096,128]{1,0:T(8,128)(2,1)S(1)} %get-tuple-element.108.v_ref), custom_call_target="tpu_custom_call" | custom-call | flops 6000000000 | bytes 10000000 | tf_op jit(solution)/shard_map/attend/pallas_call | solution.py:227
  257.0 5.8 fusion.3
  266.8 6.1 all-to-all-start.6
  276.2 5.6 concatenate.41.ws_ref
  281.8 46.5 %all-to-all-done.6 = bf16[16,256,128]{2,1,0:T(8,128)(2,1)S(1)} async-done(((bf16[16,256,128]{2,1,0:T(8,128)(2,1)}), bf16[16,256,128]{2,1,0:T(8,128)(2,1)S(1)}, u32[]{:S(2)}, u32[]{:S(2)}) %all-to-all-start.6) | async-done | bytes 1048608 | tf_op jit(solution)/shard_map/all_to_all | solution.py:84
  328.8 8.2 fusion.1
  342.8 20.2 %all-gather.7.cloned.1.call-done.c_ref = bf16[4096,2048]{1,0:T(8,128)(2,1)} async-done(((bf16[256,2048]{1,0:T(8,128)(2,1)}), bf16[4096,2048]{1,0:T(8,128)(2,1)}) %all-gather.7.cloned.1.call-update) | async-done | bytes 16777232 | tf_op jit(solution)/shard_map/all_gather | solution.py:692
  363.1 128.6 %all-gather.9.cloned.1.call-done.h_ref = bf16[4096,2048]{1,0:T(8,128)(2,1)} async-done(((bf16[256,2048]{1,0:T(8,128)(2,1)}), bf16[4096,2048]{1,0:T(8,128)(2,1)}) %all-gather.9.cloned.1.call-update) | async-done | bytes 16777232 | tf_op jit(solution)/shard_map/all_gather | solution.py:760
  496.7 154.5 %experts.1 = (bf16[4096,1024]{1,0:T(8,128)(2,1)}, bf16[4096,1024]{1,0:T(8,128)(2,1)}, bf16[4096,1536]{1,0:T(8,128)(2,1)}, bf16[4096,512]{1,0:T(8,128)(2,1)}, f32...) custom-call(s32[1]{0:T(128)} %bitcast.43.me_ref, ...), custom_call_target="tpu_custom_call" | custom-call | flops 105495134208 | bytes 130000000 | tf_op jit(solution)/shard_map/experts/pallas_call | solution.py:465
  657.8 20.6 %fusion.59 = f32[2048,1408]{1,0:T(8,128)S(1)} fusion(bf16[2304,2048]{1,0:T(8,128)(2,1)} %get-tuple-element.128, bf16[2304,1408]{1,0:T(8,128)(2,1)} %get-tuple-element.131), kind=kOutput, calls=%fused_computation.194 | convolution fusion | flops 13287555072 | bytes 27459584 | tf_op jit(solution)/shard_map/dot_general | solution.py:42
  682.0 21.7 %fusion.60 = f32[2048,1408]{1,0:T(8,128)} fusion(bf16[2304,2048]{1,0:T(8,128)(2,1)S(1)} %bitcast.240, bf16[2304,1408]{1,0:T(8,128)(2,1)} %get-tuple-element.132), kind=kOutput, calls=%fused_computation.195 | convolution fusion | flops 13287555072 | bytes 27459584 | tf_op jit(solution)/shard_map/dot_general | solution.py:42
  706.7 13.7 %convolution_convert_fusion.1 = bf16[2048,512]{1,0:T(8,128)(2,1)} fusion(bf16[4096,2048]{1,0:T(8,128)(2,1)} %all-gather.9.cloned.1.call-done.h_ref, bf16[4096,512]{1,0:T(8,128)(2,1)S(1)} %copy-done.63), kind=kOutput, calls=%fused_computation.39 | convolution fusion | flops 8590983168 | bytes 23068672 | tf_op jit(solution)/shard_map/dot_general | solution.py:42
  721.4 24.1 %collective-permute-done.8 = bf16[1024,1408]{1,0:T(8,128)(2,1)} collective-permute-done((bf16[1024,1408]{1,0:T(8,128)(2,1)}, bf16[1024,1408]{1,0:T(8,128)(2,1)}, u32[]{:S(2)}, u32[]{:S(2)}) %collective-permute-start.8) | collective-permute-done | bytes 2883616 | tf_op jit(solution)/shard_map/ppermute | solution.py:797
  749.7 19.5 %fusion.61 = f32[1408,2048]{1,0:T(8,128)} fusion(bf16[2304,1408]{1,0:T(8,128)(2,1)} %get-tuple-element.135, bf16[2304,2048]{1,0:T(8,128)(2,1)} %get-tuple-element.136), kind=kOutput, calls=%fused_computation.196 | convolution fusion | flops 13287555072 | bytes 27459584 | tf_op jit(solution)/shard_map/dot_general | solution.py:42
  769.1 11.7 collective-permute-done.7
  786.8 8.5 fusion.62
  798.1 13.1 %all-to-all-done.7 = bf16[4,256,512]{2,1,0:T(8,128)(2,1)S(1)} async-done(((bf16[4,256,512]{2,1,0:T(8,128)(2,1)}), bf16[4,256,512]{2,1,0:T(8,128)(2,1)S(1)}, u32[]{:S(2)}, u32[]{:S(2)}) %all-to-all-start.7) | async-done | bytes 1048608 | tf_op jit(solution)/shard_map/all_to_all | solution.py:84
  822.2 5.8 dynamic-slice_convert_fusion.1
  837.6 45.7 %all-to-all-done.9.refs_0_.refs_1_.refs_2_.refs_3_.refs_4_.refs_5_.refs_6_.refs_7_ = bf16[16,256,128]{2,1,0:T(8,128)(2,1)S(1)} async-done(((bf16[16,256,128]{2,1,0:T(8,128)(2,1)}), bf16[16,256,128]{2,1,0:T(8,128)(2,1)S(1)}, u32[]{:S(2)}, u32[]{:S(2)}) %all-to-all-start.9) | async-done | bytes 1048608 | tf_op jit(solution)/shard_map/all_to_all | solution.py:84
  884.9 6.7 convert_add_fusion
  910.1 35.3 %attend_back.1 = (bf16[4096,192]{1,0:T(8,128)(2,1)S(1)}, f32[4096,192]{1,0:T(8,128)}, f32[4096,128]{1,0:T(8,128)}) custom-call(bf16[4096,192]{1,0:T(8,128)(2,1)} %copy-done.14, bf16[4096,192]{1,0:T(8,128)(2,1)} %copy-done.15, bf16[4096,128]{1,0:T(8,128)(2,1)S(1)} %copy-done.17, bf16[4096,128]{1,0:T(8,128)(2,1)S(1)} %bitcast.180, f32[4096,128]{1,0:T(8,128)} %copy-done.18, ...), custom_call_target="tpu_custom_call" | custom-call | flops 16000000000 | bytes 20000000 | tf_op jit(solution)/shard_map/attend_back/pallas_call | solution.py:286
  945.4 13.3 %latent_back.1 = (bf16[4096,256]{1,0:T(8,128)(2,1)}, bf16[4096,576]{1,0:T(8,128)(2,1)}) custom-call(s32[16]{0:T(128)} %copy-done.10, s32[16]{0:T(128)} %get-tuple-element.290.mine_ref, f32[4096,192]{1,0:T(8,128)} %get-tuple-element.152.dk_ref, f32[4096,128]{1,0:T(8,128)} %get-tuple-element.153.dv_ref, bf16[512,256]{1,0:T(8,128)(2,1)} %bitcast.182), custom_call_target="tpu_custom_call" | custom-call | flops 1100000000 | bytes 14000000 | tf_op jit(solution)/shard_map/latent_back/pallas_call | solution.py:320
  958.7 5.2 collective-permute-done.13
  963.9 5.7 convert_add_fusion.2
  969.8 8.6 convolution_convert_fusion.3
  979.9 5.3 convolution_convert_fusion.5
  989.5 8.3 all-to-all-start.12
  1010.2 30.8 %all-to-all-done.12 = bf16[32,64,256]{2,1,0:T(8,128)(2,1)} async-done(((bf16[32,64,256]{2,1,0:T(8,128)(2,1)}), bf16[32,64,256]{2,1,0:T(8,128)(2,1)}, u32[]{:S(2)}, u32[]{:S(2)}) %all-to-all-start.12) | async-done | bytes 1048608 | tf_op jit(solution)/shard_map/all_to_all | solution.py:84
  1040.9 6.7 all-to-all-start.11
  1047.8 7.3 add_bitcast_fusion.2
  1057.2 17.0 %collective-permute-done.15 = bf16[704,2048]{1,0:T(8,128)(2,1)} collective-permute-done((bf16[704,2048]{1,0:T(8,128)(2,1)}, bf16[704,2048]{1,0:T(8,128)(2,1)}, u32[]{:S(2)}, u32[]{:S(2)}) %collective-permute-start.15) | collective-permute-done | bytes 2883616 | tf_op jit(solution)/shard_map/ppermute | solution.py:797
  1074.2 7.4 add_bitcast_fusion
  1081.6 4.8 add_bitcast_fusion.1
  1086.4 6.1 collective-permute-done.14
  1115.4 10.4 fusion.18
  1157.4 5.5 collective-permute-done.18
  1165.2 21.3 %all-to-all-done.14 = bf16[4,64,2048]{2,1,0:T(8,128)(2,1)} async-done(((bf16[4,64,2048]{2,1,0:T(8,128)(2,1)}), bf16[4,64,2048]{2,1,0:T(8,128)(2,1)}, u32[]{:S(2)}, u32[]{:S(2)}) %all-to-all-start.14) | async-done | bytes 1048608 | tf_op jit(solution)/shard_map/all_to_all | solution.py:84
  1202.9 15.4 %reduce-scatter.11.cloned.1.call-done = bf16[256,1024]{1,0:T(8,128)(2,1)} async-done(((bf16[4096,1024]{1,0:T(8,128)(2,1)}), bf16[256,1024]{1,0:T(8,128)(2,1)}) %reduce-scatter.11.cloned.1.call-update) | async-done | bytes 524304 | tf_op jit(solution)/shard_map/reduce_scatter | solution.py:871
  (362 shorter events, 243.8 us)
Async XLA Ops:
  7.2 181.4 %all-gather.5.cloned.1.call-start = ((), (), s32[]{:S(2)}) async-start(), calls=%async_computation.19 | async-start | bytes 17825792 | tf_op jit(solution)/shard_map/all_gather | solution.py:687
  9.9 17.2 %all-to-all-start.4 = ((f32[16,1,256]{2,1,0:T(1,128)}), f32[16,1,256]{2,1,0:T(1,128)S(1)}, u32[]{:S(2)}, u32[]{:S(2)}) async-start(f32[16,1,256]{2,1,0:T(1,128)} %copy.161), calls=%async_computation.4 | async-start | bytes 32768 | tf_op jit(solution)/shard_map/all_to_all | solution.py:84
  17.2 345.8 %all-gather.7.cloned.1.call-start = ((), (), s32[]{:S(2)}) async-start(), calls=%async_computation.20 | async-start | bytes 17825792 | tf_op jit(solution)/shard_map/all_gather | solution.py:692
  28.1 21.9 %all-to-all-start.2 = ((bf16[4,128,256]{1,2,0:T(8,128)(2,1)}), bf16[4,128,256]{1,2,0:T(8,128)(2,1)S(1)}, u32[]{:S(2)}, u32[]{:S(2)}) async-start(bf16[4,128,256]{1,2,0:T(8,128)(2,1)} %bitcast.14), calls=%async_computation.2 | async-start | bytes 524288 | tf_op jit(solution)/shard_map/all_to_all | solution.py:84
  50.7 20.7 %all-to-all-start.1 = ((bf16[4,64,592]{2,1,0:T(8,128)(2,1)}), bf16[4,64,592]{2,1,0:T(8,128)(2,1)S(1)}, u32[]{:S(2)}, u32[]{:S(2)}) async-start(bf16[4,64,592]{2,1,0:T(8,128)(2,1)} %broadcast_in_dim.42), calls=%async_computation.1 | async-start | bytes 655360 | tf_op jit(solution)/shard_map/all_to_all | solution.py:84
  72.6 56.9 %all-to-all-start.3 = ((bf16[4,64,2048]{2,1,0:T(8,128)(2,1)}), bf16[4,64,2048]{2,1,0:T(8,128)(2,1)S(1)}, u32[]{:S(2)}, u32[]{:S(2)}) async-start(bf16[4,64,2048]{2,1,0:T(8,128)(2,1)} %broadcast_in_dim.43), calls=%async_computation.3 | async-start | bytes 2097152 | tf_op jit(solution)/shard_map/all_to_all | solution.py:84
  76.1 16.0 %collective-permute-start = (bf16[4,64,592]{2,1,0:T(8,128)(2,1)S(1)}, bf16[4,64,592]{2,1,0:T(8,128)(2,1)S(1)}, u32[]{:S(2)}, u32[]{:S(2)}) collective-permute-start(bf16[4,64,592]{2,1,0:T(8,128)(2,1)S(1)} %all-to-all-done.1), channel_id=1, source_target_pairs={{0,8},{4,12},{8,0},{12,4},{1,9},{5,13},{9,1},{13,5},{2,10},{6,14},... | collective-permute-start | bytes 909320 | tf_op jit(solution)/shard_map/ppermute | solution.py:354
  93.2 41.7 %collective-permute-start.1 = (bf16[2,4,64,592]{3,2,0,1:T(8,128)(2,1)}, bf16[2,4,64,592]{3,2,0,1:T(8,128)(2,1)S(1)}, u32[]{:S(2)}, u32[]{:S(2)}) collective-permute-start(bf16[2,4,64,592]{3,2,0,1:T(8,128)(2,1)} %fusion.28), channel_id=1, source_target_pairs={{0,16},{16,0},{1,17},{17,1},{2,18},{18,2},{3,19},{19,3},{4,20},{20... | collective-permute-start | bytes 1818632 | tf_op jit(solution)/shard_map/ppermute | solution.py:354
  129.5 45.1 %all-to-all-start = ((bf16[4,512,192]{1,2,0:T(8,128)(2,1)}), bf16[4,512,192]{1,2,0:T(8,128)(2,1)}, u32[]{:S(2)}, u32[]{:S(2)}) async-start(bf16[4,512,192]{1,2,0:T(8,128)(2,1)} %bitcast.1), calls=%async_computation | async-start | bytes 1572864 | tf_op jit(solution)/shard_map/all_to_all | solution.py:84
  136.8 41.1 %collective-permute-start.2 = (bf16[2,2,4,64,592]{4,3,1,0,2:T(8,128)(2,1)}, bf16[2,2,4,64,592]{4,3,1,0,2:T(8,128)(2,1)}, u32[]{:S(2)}, u32[]{:S(2)}) collective-permute-start(bf16[2,2,4,64,592]{4,3,1,0,2:T(8,128)(2,1)} %fusion.24), channel_id=1, source_target_pairs={{0,4},{4,0},{8,12},{12,8},{1,5},{5,1},{9,13},{13,9},{2,6},{6,2},{1... | collective-permute-start | bytes 3637256 | tf_op jit(solution)/shard_map/ppermute | solution.py:354
  149.0 36.0 %collective-permute-start.3 = (bf16[4,64,2048]{2,1,0:T(8,128)(2,1)S(1)}, bf16[4,64,2048]{2,1,0:T(8,128)(2,1)}, u32[]{:S(2)}, u32[]{:S(2)}) collective-permute-start(bf16[4,64,2048]{2,1,0:T(8,128)(2,1)S(1)} %all-to-all-done.3), channel_id=1, source_target_pairs={{0,8},{4,12},{8,0},{12,4},{1,9},{5,13},{9,1},{13,5},{2,10},{6,14},... | collective-permute-start | bytes 3145736 | tf_op jit(solution)/shard_map/ppermute | solution.py:354
  152.1 43.8 %copy-start.5 = (bf16[4,128,256]{2,1,0:T(8,128)(2,1)}, bf16[4,128,256]{2,1,0:T(8,128)(2,1)S(1)}, u32[]{:S(2)}) copy-start(bf16[4,128,256]{2,1,0:T(8,128)(2,1)S(1)} %copy.157) | copy-start | bytes 786436
  188.6 68.4 %collective-permute-start.4 = (bf16[2,4,64,2048]{3,2,0,1:T(8,128)(2,1)}, bf16[2,4,64,2048]{3,2,0,1:T(8,128)(2,1)}, u32[]{:S(2)}, u32[]{:S(2)}) collective-permute-start(bf16[2,4,64,2048]{3,2,0,1:T(8,128)(2,1)} %fusion.21), channel_id=1, source_target_pairs={{0,16},{16,0},{1,17},{17,1},{2,18},{18,2},{3,19},{19,3},{4,20},{20... | collective-permute-start | bytes 6291464 | tf_op jit(solution)/shard_map/ppermute | solution.py:354
  191.3 41.1 %copy-start.12 = (s32[16]{0:T(128)}, s32[16]{0:T(128)S(1)}, u32[]{:S(2)}) copy-start(s32[16]{0:T(128)S(1)} %select_reduce_fusion.at_ref.index_ref) | copy-start | bytes 196
  191.4 71.4 %all-to-all-start.5 = ((bf16[4,512,352]{1,2,0:T(8,128)(2,1)}), bf16[4,512,352]{1,2,0:T(8,128)(2,1)}, u32[]{:S(2)}, u32[]{:S(2)}) async-start(bf16[4,512,352]{1,2,0:T(8,128)(2,1)} %pad_maximum_fusion.3), calls=%async_computation.5 | async-start | bytes 2883584 | tf_op jit(solution)/shard_map/all_to_all | solution.py:84
  264.6 64.2 %collective-permute-start.5 = (bf16[2,2,4,64,2048]{4,3,1,0,2:T(8,128)(2,1)}, bf16[2,2,4,64,2048]{4,3,1,0,2:T(8,128)(2,1)}, u32[]{:S(2)}, u32[]{:S(2)}) collective-permute-start(bf16[2,2,4,64,2048]{4,3,1,0,2:T(8,128)(2,1)} %fusion.3), channel_id=1, source_target_pairs={{0,4},{4,0},{8,12},{12,8},{1,5},{5,1},{9,13},{13,9},{2,6},{6,2},{1... | collective-permute-start | bytes 12582920 | tf_op jit(solution)/shard_map/ppermute | solution.py:354
  266.8 61.5 %all-to-all-start.6 = ((bf16[16,256,128]{2,1,0:T(8,128)(2,1)}), bf16[16,256,128]{2,1,0:T(8,128)(2,1)S(1)}, u32[]{:S(2)}, u32[]{:S(2)}) async-start(bf16[16,256,128]{2,1,0:T(8,128)(2,1)} %take_blocks.3), calls=%async_computation.6 | async-start | bytes 2097152 | tf_op jit(solution)/shard_map/all_to_all | solution.py:84
  273.0 218.8 %all-gather.9.cloned.1.call-start = ((), (), s32[]{:S(2)}) async-start(), calls=%async_computation.21 | async-start | bytes 17825792 | tf_op jit(solution)/shard_map/all_gather | solution.py:760
  363.1 288.2 %all-gather.11.cloned.1.call-start = ((), (), s32[]{:S(2)}) async-start(), calls=%async_computation.22 | async-start | bytes 12976128 | tf_op jit(solution)/shard_map/all_gather | solution.py:605
  493.5 318.6 %reduce-scatter.5.cloned.1.call-start = ((), (), s32[]{:S(2)}) async-start(), calls=%async_computation.23 | async-start | bytes 13369344 | tf_op jit(solution)/shard_map/reduce_scatter | solution.py:780
  654.3 66.1 %all-to-all-start.8 = ((f32[16,1,256]{2,1,0:T(1,128)}), f32[16,1,256]{2,1,0:T(1,128)S(1)}, u32[]{:S(2)}, u32[]{:S(2)}) async-start(f32[16,1,256]{2,1,0:T(1,128)} %bitcast.55), calls=%async_computation.9 | async-start | bytes 32768 | tf_op jit(solution)/shard_map/all_to_all | solution.py:84
  680.5 65.0 %collective-permute-start.8 = (bf16[1024,1408]{1,0:T(8,128)(2,1)}, bf16[1024,1408]{1,0:T(8,128)(2,1)}, u32[]{:S(2)}, u32[]{:S(2)}) collective-permute-start(bf16[1024,1408]{1,0:T(8,128)(2,1)} %dynamic-slice_convert_fusion.2), channel_id=1, source_target_pairs={{0,16},{16,0},{1,17},{17,1},{2,18},{18,2},{3,19},{19,3},{4,20},{20... | collective-permute-start | bytes 8650760 | tf_op jit(solution)/shard_map/ppermute | solution.py:797
  705.3 40.2 %collective-permute-start.6 = (bf16[2,1024,512]{2,1,0:T(8,128)(2,1)}, bf16[2,1024,512]{2,1,0:T(8,128)(2,1)S(1)}, u32[]{:S(2)}, u32[]{:S(2)}) collective-permute-start(bf16[2,1024,512]{2,1,0:T(8,128)(2,1)} %dynamic-slice_bitcast_fusion), channel_id=1, source_target_pairs={{0,4},{4,0},{8,12},{12,8},{1,5},{5,1},{9,13},{13,9},{2,6},{6,2},{1... | collective-permute-start | bytes 6291464 | tf_op jit(solution)/shard_map/ppermute | solution.py:616
  747.8 33.0 %collective-permute-start.7 = (bf16[1024,512]{1,0:T(8,128)(2,1)S(1)}, bf16[1024,512]{1,0:T(8,128)(2,1)S(1)}, u32[]{:S(2)}, u32[]{:S(2)}) collective-permute-start(bf16[1024,512]{1,0:T(8,128)(2,1)S(1)} %dynamic-slice_bitcast_fusion.1), channel_id=1, source_target_pairs={{0,8},{4,12},{8,0},{12,4},{1,9},{5,13},{9,1},{13,5},{2,10},{6,14},... | collective-permute-start | bytes 3145736 | tf_op jit(solution)/shard_map/ppermute | solution.py:616
  782.1 29.1 %all-to-all-start.7 = ((bf16[4,256,512]{2,1,0:T(8,128)(2,1)}), bf16[4,256,512]{2,1,0:T(8,128)(2,1)S(1)}, u32[]{:S(2)}, u32[]{:S(2)}) async-start(bf16[4,256,512]{2,1,0:T(8,128)(2,1)} %bitcast.52), calls=%async_computation.8 | async-start | bytes 2097152 | tf_op jit(solution)/shard_map/all_to_all | solution.py:84
  786.8 183.0 %reduce-scatter.7.cloned.1.call-start = ((), (), s32[]{:S(2)}) async-start(), calls=%async_computation.24 | async-start | bytes 8912896 | tf_op jit(solution)/shard_map/reduce_scatter | solution.py:820
  822.2 61.8 %collective-permute-start.10 = (bf16[1024,2048]{1,0:T(8,128)(2,1)}, bf16[1024,2048]{1,0:T(8,128)(2,1)}, u32[]{:S(2)}, u32[]{:S(2)}) collective-permute-start(bf16[1024,2048]{1,0:T(8,128)(2,1)} %convolution_convert_fusion), channel_id=1, source_target_pairs={{0,4},{4,0},{8,12},{12,8},{1,5},{5,1},{9,13},{13,9},{2,6},{6,2},{1... | collective-permute-start | bytes 12582920 | tf_op jit(solution)/shard_map/ppermute | solution.py:632
  828.0 64.4 %collective-permute-start.9 = (bf16[1024,1408]{1,0:T(8,128)(2,1)}, bf16[1024,1408]{1,0:T(8,128)(2,1)}, u32[]{:S(2)}, u32[]{:S(2)}) collective-permute-start(bf16[1024,1408]{1,0:T(8,128)(2,1)} %dynamic-slice_convert_fusion.1), channel_id=1, source_target_pairs={{0,16},{16,0},{1,17},{17,1},{2,18},{18,2},{3,19},{19,3},{4,20},{20... | collective-permute-start | bytes 8650760 | tf_op jit(solution)/shard_map/ppermute | solution.py:797
  832.5 50.8 %copy-start.13 = (s32[16]{0:T(128)S(1)}, s32[16]{0:T(128)}, u32[]{:S(2)}) copy-start(s32[16]{0:T(128)} %copy-done.12) | copy-start | bytes 196
  833.9 49.4 %all-to-all-start.9 = ((bf16[16,256,128]{2,1,0:T(8,128)(2,1)}), bf16[16,256,128]{2,1,0:T(8,128)(2,1)S(1)}, u32[]{:S(2)}, u32[]{:S(2)}) async-start(bf16[16,256,128]{2,1,0:T(8,128)(2,1)} %bitcast.59), calls=%async_computation.10 | async-start | bytes 2097152 | tf_op jit(solution)/shard_map/all_to_all | solution.py:84
  837.6 46.4 %copy-start.40 = (bf16[256,4,1,256]{0,3,2,1:T(8,128)(2,1)S(1)}, bf16[256,4,1,256]{0,3,2,1:T(8,128)(2,1)}, u32[]{:S(2)}) copy-start(bf16[256,4,1,256]{0,3,2,1:T(8,128)(2,1)} %get-tuple-element.302) | copy-start | bytes 1572868
  896.4 67.4 %collective-permute-start.13 = (bf16[512,2048]{1,0:T(8,128)(2,1)}, bf16[512,2048]{1,0:T(8,128)(2,1)}, u32[]{:S(2)}, u32[]{:S(2)}) collective-permute-start(bf16[512,2048]{1,0:T(8,128)(2,1)} %dynamic-slice_convert_fusion.3), channel_id=1, source_target_pairs={{0,16},{16,0},{1,17},{17,1},{2,18},{18,2},{3,19},{19,3},{4,20},{20... | collective-permute-start | bytes 6291464 | tf_op jit(solution)/shard_map/ppermute | solution.py:632
  897.7 72.1 %all-to-all-start.10 = ((bf16[32,64,352]{2,1,0:T(8,128)(2,1)}), bf16[32,64,352]{2,1,0:T(8,128)(2,1)}, u32[]{:S(2)}, u32[]{:S(2)}) async-start(bf16[32,64,352]{2,1,0:T(8,128)(2,1)} %bitcast.53), calls=%async_computation.12 | async-start | bytes 3145728 | tf_op jit(solution)/shard_map/all_to_all | solution.py:84
  901.2 195.3 %reduce-scatter.9.cloned.1.call-start = ((), (), s32[]{:S(2)}) async-start(), calls=%async_computation.25 | async-start | bytes 5570560 | tf_op jit(solution)/shard_map/reduce_scatter | solution.py:855
  903.4 66.2 %collective-permute-start.11 = (bf16[88,2048]{1,0:T(8,128)(2,1)}, bf16[88,2048]{1,0:T(8,128)(2,1)}, u32[]{:S(2)}, u32[]{:S(2)}) collective-permute-start(bf16[88,2048]{1,0:T(8,128)(2,1)} %get-tuple-element.307), channel_id=1, source_target_pairs={{0,0},{1,8},{2,16},{3,24},{4,2},{5,10},{6,18},{7,26},{8,4},{9,12},... | collective-permute-start | bytes 1081352 | tf_op jit(solution)/shard_map/ppermute | solution.py:844
  907.8 62.0 %collective-permute-start.12 = (bf16[88,2048]{1,0:T(8,128)(2,1)}, bf16[88,2048]{1,0:T(8,128)(2,1)}, u32[]{:S(2)}, u32[]{:S(2)}) collective-permute-start(bf16[88,2048]{1,0:T(8,128)(2,1)} %get-tuple-element.306), channel_id=1, source_target_pairs={{0,1},{1,9},{2,17},{3,25},{4,3},{5,11},{6,19},{7,27},{8,5},{9,13},... | collective-permute-start | bytes 1081352 | tf_op jit(solution)/shard_map/ppermute | solution.py:844
  989.5 51.4 %all-to-all-start.12 = ((bf16[32,64,256]{2,1,0:T(8,128)(2,1)}), bf16[32,64,256]{2,1,0:T(8,128)(2,1)}, u32[]{:S(2)}, u32[]{:S(2)}) async-start(bf16[32,64,256]{2,1,0:T(8,128)(2,1)} %pad_maximum_fusion.5), calls=%async_computation.15 | async-start | bytes 2097152 | tf_op jit(solution)/shard_map/all_to_all | solution.py:84
  1002.5 71.7 %collective-permute-start.15 = (bf16[704,2048]{1,0:T(8,128)(2,1)}, bf16[704,2048]{1,0:T(8,128)(2,1)}, u32[]{:S(2)}, u32[]{:S(2)}) collective-permute-start(bf16[704,2048]{1,0:T(8,128)(2,1)} %dynamic-slice_convert_fusion), channel_id=1, source_target_pairs={{0,16},{16,0},{1,17},{17,1},{2,18},{18,2},{3,19},{19,3},{4,20},{20... | collective-permute-start | bytes 8650760 | tf_op jit(solution)/shard_map/ppermute | solution.py:797
  1040.9 55.5 %all-to-all-start.11 = ((bf16[16,256,192]{1,2,0:T(8,128)(2,1)}), bf16[16,256,192]{1,2,0:T(8,128)(2,1)S(1)}, u32[]{:S(2)}, u32[]{:S(2)}) async-start(bf16[16,256,192]{1,2,0:T(8,128)(2,1)} %copy.171), calls=%async_computation.14 | async-start | bytes 3145728 | tf_op jit(solution)/shard_map/all_to_all | solution.py:84
  1047.7 170.6 %reduce-scatter.11.cloned.1.call-start = ((), (), s32[]{:S(2)}) async-start(), calls=%async_computation.26 | async-start | bytes 8912896 | tf_op jit(solution)/shard_map/reduce_scatter | solution.py:871
  1047.7 33.8 %slice-start.2 = ((s8[11534336]{0:T(1024)(128)(4,1)}), s8[4194304]{0:T(1024)(128)(4,1)S(1)}, s32[]{:S(2)}) async-start(s8[11534336]{0:T(1024)(128)(4,1)} %bitcast.201), calls=%async_computation.29 | async-start | bytes 8388608
  1047.8 33.8 %slice-start.3 = ((s8[11534336]{0:T(1024)(128)(4,1)}), s8[4194304]{0:T(1024)(128)(4,1)S(1)}, s32[]{:S(2)}) async-start(s8[11534336]{0:T(1024)(128)(4,1)} %bitcast.201), calls=%async_computation.30 | async-start | bytes 8388608
  1055.2 37.4 %collective-permute-start.14 = (bf16[256,2048]{1,0:T(8,128)(2,1)S(1)}, bf16[256,2048]{1,0:T(8,128)(2,1)S(1)}, u32[]{:S(2)}, u32[]{:S(2)}) collective-permute-start(bf16[256,2048]{1,0:T(8,128)(2,1)S(1)} %dynamic-slice_convert_fusion.4), channel_id=1, source_target_pairs={{0,8},{4,12},{8,0},{12,4},{1,9},{5,13},{9,1},{13,5},{2,10},{6,14},... | collective-permute-start | bytes 3145736 | tf_op jit(solution)/shard_map/ppermute | solution.py:632
  1128.3 4.4 collective-permute-start.16
  1134.7 17.3 %collective-permute-start.17 = (bf16[512,640]{0,1:T(8,128)(2,1)S(1)}, bf16[512,640]{0,1:T(8,128)(2,1)}, u32[]{:S(2)}, u32[]{:S(2)}) collective-permute-start(bf16[512,640]{0,1:T(8,128)(2,1)S(1)} %dynamic-slice_convert_fusion.5), channel_id=1, source_target_pairs={{0,16},{16,0},{1,17},{17,1},{2,18},{18,2},{3,19},{19,3},{4,20},{20... | collective-permute-start | bytes 1966088 | tf_op jit(solution)/shard_map/ppermute | solution.py:632
  1141.1 45.3 %all-to-all-start.14 = ((bf16[4,64,2048]{2,1,0:T(8,128)(2,1)}), bf16[4,64,2048]{2,1,0:T(8,128)(2,1)}, u32[]{:S(2)}, u32[]{:S(2)}) async-start(bf16[4,64,2048]{2,1,0:T(8,128)(2,1)} %bitcast.81), calls=%async_computation.18 | async-start | bytes 2097152 | tf_op jit(solution)/shard_map/all_to_all | solution.py:84
  1153.5 9.5 collective-permute-start.18
  1186.4 14.3 %all-to-all-start.13 = ((bf16[4,64,640]{2,1,0:T(8,128)(2,1)}), bf16[4,64,640]{2,1,0:T(8,128)(2,1)S(1)}, u32[]{:S(2)}, u32[]{:S(2)}) async-start(bf16[4,64,640]{2,1,0:T(8,128)(2,1)} %bitcast.77), calls=%async_computation.17 | async-start | bytes 655360 | tf_op jit(solution)/shard_map/all_to_all | solution.py:84
  (67 other events, 604.0 us)
Sparse Core Ops, SparseCore 0:
  10.2 177.7 all-gather.4
  190.3 172.7 all-gather.6
  365.8 125.8 all-gather.8
  495.0 94.1 all-gather.10
  651.4 137.6 reduce-scatter.4
  813.8 149.2 reduce-scatter.6
  969.9 115.2 reduce-scatter.8
  1097.7 120.5 reduce-scatter.10

commit v4 on v3

--- a/solution.py
+++ b/solution.py
@@ -360,16 +360,14 @@
 
 
 def experts_body(
-    groups, units, count, n_parts, me_ref, place_ref, h_ref, c_ref, wg_ref, wu_ref, wd_ref, ws_ref,
-    wsd_ref, outa_ref, outb_ref, *refs,
+    groups, units, count, n_parts, me_ref, place_ref, h_ref, crow_ref, dmid_ref, dsmid_ref, wg_ref,
+    wu_ref, wd_ref, ws_ref, wsd_ref, outa_ref, outb_ref, *refs,
 ):
     dh_refs = refs[:n_parts]
-    dprob_ref, rows_ref, dout_ref, mid_ref, dg_ref, du_ref, smid_ref, ds_ref, crow_ref = refs[
-        n_parts:
-    ]
+    dprob_ref, rows_ref, dout_ref, mid_ref, dg_ref, du_ref, smid_ref, ds_ref = refs[n_parts:]
     width, hidden = wg_ref.shape
     padded = wsd_ref.shape[0]
-    h, c = h_ref[...], c_ref[...]
+    h = h_ref[...]
     ends = [0]
     for ref in dh_refs:
         ends.append(ends[-1] + ref.shape[1])
@@ -385,7 +383,7 @@
     )
     s_act, s_slope = silu_parts(s_gate)
     smid_ref[...] = (s_act * s_up).astype(BF16)
-    ds_mid = dot(c, wsd_ref[...], 1, 1)
+    ds_mid = dsmid_ref[...]
     ds_ref[:, :padded] = (ds_mid * s_up * s_slope).astype(BF16)
     ds_ref[:, padded:] = (ds_mid * s_act).astype(BF16)
 
@@ -397,9 +395,7 @@
         scale = jnp.sum(jnp.where(here, weight[:, toks], 0.0), axis=1, keepdims=True)
         for cols in chunks_of(width, 512):
             rows_ref[rows, cols] = dot(pick, h[toks, cols], 1, 0).astype(BF16)
-            c_rows = dot(pick, c[toks, cols], 1, 0)
-            crow_ref[rows, cols] = c_rows.astype(BF16)
-            dout_ref[rows, cols] = (scale * c_rows).astype(BF16)
+            dout_ref[rows, cols] = (scale * crow_ref[rows, cols].astype(F32)).astype(BF16)
         picks.append((rows, toks, here, pick))
         weights.append(scale)
     scale = jnp.concatenate(weights, axis=0) if len(weights) > 1 else weights[0]
@@ -409,7 +405,7 @@
         up = dot(rows_ref[...], wu_ref[:, cols], 1, 0)
         act, slope = silu_parts(gate)
         mid_ref[:, cols] = (act * up).astype(BF16)
-        d_mid = dot(dout_ref[...], wd_ref[cols, :], 1, 1)
+        d_mid = scale * dmid_ref[:, cols]
         dg_ref[:, cols] = (d_mid * up * slope).astype(BF16)
         du_ref[:, cols] = (d_mid * act).astype(BF16)
 
@@ -438,37 +434,81 @@
         )
 
 
+def groups_of(capacity, blocks):
+    if capacity % 16 == 0:
+        return [
+            (slice(b * capacity, (b + 1) * capacity), slice(b * BLOCK, (b + 1) * BLOCK))
+            for b in range(blocks)
+        ]
+    return [(slice(0, blocks * capacity), slice(0, blocks * BLOCK))]
+
+
+def cotangent_body(groups, place_ref, c_ref, wd_ref, wsd_ref, crow_ref, dmid_ref, dsmid_ref):
+    dsmid_ref[...] = dot(c_ref[...], wsd_ref[...], 1, 1)
+    for rows, toks in groups:
+        shape = (rows.stop - rows.start, toks.stop - toks.start)
+        here = lax.broadcasted_iota(jnp.int32, shape, 0) + rows.start == place_ref[0, :, toks]
+        pick = jnp.where(here, 1.0, 0.0).astype(BF16)
+        for cols in chunks_of(c_ref.shape[1], 512):
+            crow_ref[rows, cols] = dot(pick, c_ref[toks, cols], 1, 0).astype(BF16)
+    for cols in chunks_of(wd_ref.shape[0], 512):
+        dmid_ref[:, cols] = dot(crow_ref[...], wd_ref[cols, :], 1, 1)
+
+
+def cotangent_rows(place, capacity, cotangent, w_down, w_sdown):
+    tokens, width = cotangent.shape
+    hidden, padded = w_down.shape[0], w_sdown.shape[0]
+    step, room, steps = 2 * BLOCK, 2 * capacity, tokens // (2 * BLOCK)
+    once = lambda a: pl.BlockSpec(a.shape, lambda i: (0, 0), pipeline_mode=pl.Buffered(1))
+    tiled = lambda rows, cols: pl.BlockSpec((rows, cols), lambda i: (i, 0))
+    return pl.pallas_call(
+        functools.partial(cotangent_body, groups_of(capacity, 2)),
+        grid=(steps,),
+        in_specs=[
+            pl.BlockSpec((1, 1, step), lambda i: (i, 0, 0)), tiled(step, width), once(w_down),
+            once(w_sdown),
+        ],
+        out_specs=[tiled(room, width), tiled(room, hidden), tiled(step, padded)],
+        out_shape=[
+            jax.ShapeDtypeStruct((steps * room, width), BF16),
+            jax.ShapeDtypeStruct((steps * room, hidden), F32),
+            jax.ShapeDtypeStruct((tokens, padded), F32),
+        ],
+        compiler_params=pltpu.CompilerParams(vmem_limit_bytes=40 << 20),
+        cost_estimate=pl.CostEstimate(
+            flops=2 * steps * width * (room * hidden + step * padded + room * step),
+            bytes_accessed=55_000_000,
+            transcendentals=0,
+        ),
+        name="cotangent_rows",
+    )(place, cotangent, w_down, w_sdown)
+
+
 def experts(
-    me, place, capacity, hidden2, cotangent, w_gate, w_up, w_down, w_shared, w_sdown, units, count,
+    me, place, capacity, hidden2, c_kept, w_gate, w_up, w_down, w_shared, w_sdown, units, count,
     widths,
 ):
     width, hidden = w_gate.shape
-    tokens = cotangent.shape[0]
+    tokens = hidden2.shape[0]
     n_parts = len(widths)
     padded = w_sdown.shape[0]
     blocks = 2
     step = blocks * BLOCK
     steps = tokens // step
     room = blocks * capacity
-    if capacity % 16 == 0:
-        groups = [
-            (slice(b * capacity, (b + 1) * capacity), slice(b * BLOCK, (b + 1) * BLOCK))
-            for b in range(blocks)
-        ]
-    else:
-        groups = [(slice(0, room), slice(0, step))]
+    groups = groups_of(capacity, blocks)
     once = lambda a: pl.BlockSpec(a.shape, lambda i, me: (0, 0), pipeline_mode=pl.Buffered(1))
     tiled = lambda rows, cols: pl.BlockSpec((rows, cols), lambda i, me: (i, 0))
     line = pl.BlockSpec((1, 1, step), lambda i, me: (i, 0, 0))
     shape = lambda rows, cols, kind=BF16: jax.ShapeDtypeStruct((rows, cols), kind)
-    flops = 2 * steps * (6 * room * width * hidden + 6 * step * width * padded)
+    flops = 2 * steps * (5 * room * width * hidden + 5 * step * width * padded)
     outs = pl.pallas_call(
         functools.partial(experts_body, groups, units, count, n_parts),
         grid_spec=pltpu.PrefetchScalarGridSpec(
             num_scalar_prefetch=1,
             grid=(steps,),
             in_specs=[
-                line, tiled(step, width), tiled(step, width),
+                line, tiled(step, width), tiled(room, width), tiled(room, hidden), tiled(step, padded),
                 once(w_gate), once(w_up), once(w_down), once(w_shared), once(w_sdown),
             ],
             out_specs=[
@@ -478,7 +518,6 @@
                 tiled(room, width), tiled(room, hidden), tiled(room, hidden),
                 tiled(room, hidden), tiled(step, padded), tiled(step, 2 * padded),
             ],
-            scratch_shapes=[pltpu.VMEM((room, width), BF16)],
         ),
         out_shape=[
             shape(tokens, width // 2), shape(tokens, width // 2),
@@ -493,7 +532,7 @@
             flops=flops, bytes_accessed=130_000_000, transcendentals=5_000_000
         ),
         name="experts",
-    )(me, place, hidden2, cotangent, w_gate, w_up, w_down, w_shared, w_sdown)
+    )(me, place, hidden2, *c_kept, w_gate, w_up, w_down, w_shared, w_sdown)
     return [*outs[:2], list(outs[2 : 2 + n_parts]), *outs[2 + n_parts :]]
 
 def places_of(hit):
@@ -758,14 +797,15 @@
 
     hidden2, c_all, w_sh = lax.optimization_barrier((hidden2, c_all, w_sh))
     h2_all = lax.all_gather(hidden2, ROW, axis=0, tiled=True)
-    h2_all, w_query = lax.optimization_barrier((h2_all, w_query))
+    c_kept = cotangent_rows(place, capacity, c_all, expert_down[0], w_sd)
+    h2_all, w_query, c_kept = lax.optimization_barrier((h2_all, w_query, c_kept))
     w_q = gather_rows_at_once(w_query)
     out_a, out_b, dh_parts, d_prob_col, rows, d_out, e_mid, d_gate, d_up, s_mid, ds_gu = experts(
         row_at[None],
         place,
         capacity,
         h2_all,
-        c_all,
+        c_kept,
         expert_gate[0],
         expert_up[0],
         expert_down[0],

time: 1230 us -> 1210 us (0.984); the launches traced: 1230 us -> 1190 us
  waiting for transfers between devices: 504 us -> 470 us
    all_gather x1, waiting for transfers between devices: 129 us -> 96 us  [per_device(): h2_all = lax.all_gather(hidden2, ROW, axis=0, tiled=True)]
    pallas_call x1, Pallas kernels: 155 us -> 126 us  [experts(): pl.pallas_call(functools.partial(experts_body, groups, units, count, n_pa...]
    pallas_call x0 -> x1, Pallas kernels: none -> 26.1 us  [cotangent_rows(): pl.pallas_call(functools.partial(cotangent_body, groups_of(capacity, 2)),...]
    unnamed x154 -> x156, local copies, waits for them, and re-layouts: 33.1 us -> 43 us
  transfers between devices with their start and end apart: 42 -> 42, of which waited for: 24 -> 22; matrix products, arithmetic and copies ran while one was open for 26% -> 27% of each run, Pallas kernels for 22% -> 22%
where the time goes in v4:
time: 1210 us; the launch traced here: 1190 us
  waiting for transfers between devices  470 us (39%)
  Pallas kernels  263 us (22%)
  matrix products  134 us (11%)
  local copies, waits for them, and re-layouts  115 us (10%)
  other arithmetic  103 us (9%)
  starting transfers between devices  93 us (8%)
  between operations  15.8 us (1%)
    all_to_all x15, waiting for transfers between devices, trade(): return lax.all_to_all(buffer, axes, split_axis=0, concat_axis=0, tiled=True)  250 us
    pallas_call x1, Pallas kernels, experts(): pl.pallas_call(functools.partial(experts_body, groups, units, count, n_pa...  126 us
    dot_general x12, matrix products, matmul_tn(): lax.dot_general(left, right, (((0,), (0,)), ((), ())), preferred_element_...  109 us
    all_gather x1, waiting for transfers between devices, per_device(): h2_all = lax.all_gather(hidden2, ROW, axis=0, tiled=True)  96 us
    all_to_all x15, starting transfers between devices, trade(): return lax.all_to_all(buffer, axes, split_axis=0, concat_axis=0, tiled=True)  70.6 us
    unnamed x156, local copies, waits for them, and re-layouts  43 us
    ppermute x3, waiting for transfers between devices, share(): return (lax.ppermute(send, 'group', [(0, 1), (1, 0)]), keep)  40 us
    pallas_call x1, Pallas kernels, project(): pl.pallas_call(project_body, grid_spec=pltpu.PrefetchScalarGridSpec(num_s...  36.4 us
  transfers between devices with their start and end apart: 42, of which 22 were waited for; matrix products, arithmetic and copies ran while one was open for 27% of the time, Pallas kernels for 22%

profile of v4, /device:TPU:0, one launch (start us, length us, event | category | flops | bytes accessed | tf_op | source)
XLA Modules:
  0.0 1194.4 jit_solution(7378719334622206999)
XLA Ops:
  9.9 7.4 all-to-all-start.4
  17.8 9.3 multiply_sine_fusion
  28.0 5.0 all-to-all-start.2
  33.3 16.7 %all-to-all-done.2 = bf16[4,128,256]{1,2,0:T(8,128)(2,1)S(1)} async-done(((bf16[4,128,256]{1,2,0:T(8,128)(2,1)}), bf16[4,128,256]{1,2,0:T(8,128)(2,1)S(1)}, u32[]{:S(2)}, u32[]{:S(2)}) %all-to-all-start.2) | async-done | bytes 262176 | tf_op jit(solution)/shard_map/all_to_all | solution.py:84
  55.6 15.9 %all-to-all-done.1 = bf16[4,64,592]{2,1,0:T(8,128)(2,1)S(1)} async-done(((bf16[4,64,592]{2,1,0:T(8,128)(2,1)}), bf16[4,64,592]{2,1,0:T(8,128)(2,1)S(1)}, u32[]{:S(2)}, u32[]{:S(2)}) %all-to-all-start.1) | async-done | bytes 303136 | tf_op jit(solution)/shard_map/all_to_all | solution.py:84
  77.6 14.4 %collective-permute-done = bf16[4,64,592]{2,1,0:T(8,128)(2,1)S(1)} collective-permute-done((bf16[4,64,592]{2,1,0:T(8,128)(2,1)S(1)}, bf16[4,64,592]{2,1,0:T(8,128)(2,1)S(1)}, u32[]{:S(2)}, u32[]{:S(2)}) %collective-permute-start) | collective-permute-done | bytes 303136 | tf_op jit(solution)/shard_map/ppermute | solution.py:354
  98.3 31.1 %all-to-all-done.3 = bf16[4,64,2048]{2,1,0:T(8,128)(2,1)S(1)} async-done(((bf16[4,64,2048]{2,1,0:T(8,128)(2,1)}), bf16[4,64,2048]{2,1,0:T(8,128)(2,1)S(1)}, u32[]{:S(2)}, u32[]{:S(2)}) %all-to-all-start.3) | async-done | bytes 1048608 | tf_op jit(solution)/shard_map/all_to_all | solution.py:84
  129.5 5.5 all-to-all-start
  152.2 22.4 %all-to-all-done = bf16[4,512,192]{1,2,0:T(8,128)(2,1)} async-done(((bf16[4,512,192]{1,2,0:T(8,128)(2,1)}), bf16[4,512,192]{1,2,0:T(8,128)(2,1)}, u32[]{:S(2)}, u32[]{:S(2)}) %all-to-all-start) | async-done | bytes 786464 | tf_op jit(solution)/shard_map/all_to_all | solution.py:84
  196.1 36.4 %project.1 = (bf16[4096,2048]{1,0:T(8,128)(2,1)}, bf16[4096,192]{1,0:T(8,128)(2,1)S(1)}, bf16[4096,192]{1,0:T(8,128)(2,1)S(1)}, bf16[4096,128]{1,0:T(8,128)(2,1)S(1)}, bf16[4096,512]{1,0:T(8,128)(2,1)}) custom-call(s32[16]{0:T(128)S(1)} %select_reduce_fusion.at_ref.index_ref, bf16[16,256,2048]{2,1,0:T(8,128)(2,1)} %bitcast.236, ...), custom_call_target="tpu_custom_call" | custom-call | flops 14000000000 | bytes 48000000 | tf_op jit(solution)/shard_map/project/pallas_call | solution.py:158
  232.6 23.2 %attend.1 = (f32[4096,128]{1,0:T(8,128)S(1)}, bf16[4096,128]{1,0:T(8,128)(2,1)S(1)}, f32[1,4096]{1,0:T(1,128)S(1)}) custom-call(bf16[4096,192]{1,0:T(8,128)(2,1)S(1)} %get-tuple-element.112.q_ref, bf16[4096,192]{1,0:T(8,128)(2,1)S(1)} %get-tuple-element.113.k_ref, bf16[4096,128]{1,0:T(8,128)(2,1)S(1)} %get-tuple-element.114.v_ref), custom_call_target="tpu_custom_call" | custom-call | flops 6000000000 | bytes 10000000 | tf_op jit(solution)/shard_map/attend/pallas_call | solution.py:227
  257.1 5.8 fusion.3
  266.9 6.1 all-to-all-start.6
  276.3 5.6 concatenate.41.ws_ref
  281.9 46.5 %all-to-all-done.6 = bf16[16,256,128]{2,1,0:T(8,128)(2,1)S(1)} async-done(((bf16[16,256,128]{2,1,0:T(8,128)(2,1)}), bf16[16,256,128]{2,1,0:T(8,128)(2,1)S(1)}, u32[]{:S(2)}, u32[]{:S(2)}) %all-to-all-start.6) | async-done | bytes 1048608 | tf_op jit(solution)/shard_map/all_to_all | solution.py:84
  329.0 7.8 fusion.1
  342.7 20.5 %all-gather.7.cloned.1.call-done.c_ref = bf16[4096,2048]{1,0:T(8,128)(2,1)} async-done(((bf16[256,2048]{1,0:T(8,128)(2,1)}), bf16[4096,2048]{1,0:T(8,128)(2,1)}) %all-gather.7.cloned.1.call-update) | async-done | bytes 16777232 | tf_op jit(solution)/shard_map/all_gather | solution.py:731
  367.8 26.1 %cotangent_rows.1 = (bf16[2304,2048]{1,0:T(8,128)(2,1)}, f32[2304,1408]{1,0:T(8,128)}, f32[4096,256]{1,0:T(8,128)S(1)}) custom-call(s32[8,1,512]{2,1,0:T(1,128)S(1)} %reshape.288.place_ref, bf16[4096,2048]{1,0:T(8,128)(2,1)} %all-gather.7.cloned.1.call-done.c_ref, bf16[1408,2048]{1,0:T(8,128)(2,1)S(1)} %bitcast.186, bf16[256,2048]{1,0:T(8,128)(2,1)S(1)} %pad.12.wsd_ref), custom_call_target="tpu_custom_call" | custom-call | flops 22414360576 | bytes 55000000 | tf_op jit(solution)/shard_map/cotangent_rows/pallas_call | solution.py:464
  395.9 96.0 %all-gather.9.cloned.1.call-done.h_ref = bf16[4096,2048]{1,0:T(8,128)(2,1)} async-done(((bf16[256,2048]{1,0:T(8,128)(2,1)}), bf16[4096,2048]{1,0:T(8,128)(2,1)}) %all-gather.9.cloned.1.call-update) | async-done | bytes 16777232 | tf_op jit(solution)/shard_map/all_gather | solution.py:799
  493.7 125.9 %experts.1 = (bf16[4096,1024]{1,0:T(8,128)(2,1)}, bf16[4096,1024]{1,0:T(8,128)(2,1)}, bf16[4096,1536]{1,0:T(8,128)(2,1)}, bf16[4096,512]{1,0:T(8,128)(2,1)}, f32...) custom-call(s32[1]{0:T(128)} %bitcast.43.me_ref, ...), custom_call_target="tpu_custom_call" | custom-call | flops 87912611840 | bytes 130000000 | tf_op jit(solution)/shard_map/experts/pallas_call | solution.py:505
  622.6 20.4 %fusion.59 = f32[2048,1408]{1,0:T(8,128)S(1)} fusion(bf16[2304,2048]{1,0:T(8,128)(2,1)} %get-tuple-element.140, bf16[2304,1408]{1,0:T(8,128)(2,1)} %get-tuple-element.143), kind=kOutput, calls=%fused_computation.194 | convolution fusion | flops 13287555072 | bytes 27459584 | tf_op jit(solution)/shard_map/dot_general | solution.py:42
  654.2 20.8 %fusion.60 = f32[2048,1408]{1,0:T(8,128)} fusion(bf16[2304,2048]{1,0:T(8,128)(2,1)} %get-tuple-element.140, bf16[2304,1408]{1,0:T(8,128)(2,1)} %get-tuple-element.144), kind=kOutput, calls=%fused_computation.195 | convolution fusion | flops 13287555072 | bytes 27459584 | tf_op jit(solution)/shard_map/dot_general | solution.py:42
  678.0 13.6 %convolution_convert_fusion.1 = bf16[2048,512]{1,0:T(8,128)(2,1)} fusion(bf16[4096,2048]{1,0:T(8,128)(2,1)} %all-gather.9.cloned.1.call-done.h_ref, bf16[4096,512]{1,0:T(8,128)(2,1)S(1)} %copy-done.67), kind=kOutput, calls=%fused_computation.39 | convolution fusion | flops 8590983168 | bytes 23068672 | tf_op jit(solution)/shard_map/dot_general | solution.py:42
  692.5 21.6 %collective-permute-done.8 = bf16[1024,1408]{1,0:T(8,128)(2,1)} collective-permute-done((bf16[1024,1408]{1,0:T(8,128)(2,1)}, bf16[1024,1408]{1,0:T(8,128)(2,1)}, u32[]{:S(2)}, u32[]{:S(2)}) %collective-permute-start.8) | collective-permute-done | bytes 2883616 | tf_op jit(solution)/shard_map/ppermute | solution.py:837
  716.7 19.5 %fusion.61 = f32[1408,2048]{1,0:T(8,128)} fusion(bf16[2304,1408]{1,0:T(8,128)(2,1)} %get-tuple-element.147, bf16[2304,2048]{1,0:T(8,128)(2,1)} %get-tuple-element.148), kind=kOutput, calls=%fused_computation.196 | convolution fusion | flops 13287555072 | bytes 27459584 | tf_op jit(solution)/shard_map/dot_general | solution.py:42
  736.1 13.2 %collective-permute-done.7 = bf16[1024,512]{1,0:T(8,128)(2,1)S(1)} collective-permute-done((bf16[1024,512]{1,0:T(8,128)(2,1)S(1)}, bf16[1024,512]{1,0:T(8,128)(2,1)S(1)}, u32[]{:S(2)}, u32[]{:S(2)}) %collective-permute-start.7) | collective-permute-done | bytes 1048608 | tf_op jit(solution)/shard_map/ppermute | solution.py:655
  754.2 8.7 fusion.62
  765.7 13.6 %all-to-all-done.7 = bf16[4,256,512]{2,1,0:T(8,128)(2,1)S(1)} async-done(((bf16[4,256,512]{2,1,0:T(8,128)(2,1)}), bf16[4,256,512]{2,1,0:T(8,128)(2,1)S(1)}, u32[]{:S(2)}, u32[]{:S(2)}) %all-to-all-start.7) | async-done | bytes 1048608 | tf_op jit(solution)/shard_map/all_to_all | solution.py:84
  790.3 5.8 dynamic-slice_convert_fusion.1
  805.7 46.3 %all-to-all-done.9.refs_0_.refs_1_.refs_2_.refs_3_.refs_4_.refs_5_.refs_6_.refs_7_ = bf16[16,256,128]{2,1,0:T(8,128)(2,1)S(1)} async-done(((bf16[16,256,128]{2,1,0:T(8,128)(2,1)}), bf16[16,256,128]{2,1,0:T(8,128)(2,1)S(1)}, u32[]{:S(2)}, u32[]{:S(2)}) %all-to-all-start.9) | async-done | bytes 1048608 | tf_op jit(solution)/shard_map/all_to_all | solution.py:84
  853.6 6.8 convert_add_fusion
  878.3 35.3 %attend_back.1 = (bf16[4096,192]{1,0:T(8,128)(2,1)S(1)}, f32[4096,192]{1,0:T(8,128)}, f32[4096,128]{1,0:T(8,128)}) custom-call(bf16[4096,192]{1,0:T(8,128)(2,1)} %copy-done.17, bf16[4096,192]{1,0:T(8,128)(2,1)} %copy-done.18, bf16[4096,128]{1,0:T(8,128)(2,1)S(1)} %copy-done.20, bf16[4096,128]{1,0:T(8,128)(2,1)S(1)} %bitcast.180, f32[4096,128]{1,0:T(8,128)} %copy-done.21, ...), custom_call_target="tpu_custom_call" | custom-call | flops 16000000000 | bytes 20000000 | tf_op jit(solution)/shard_map/attend_back/pallas_call | solution.py:286
  913.6 13.3 %latent_back.1 = (bf16[4096,256]{1,0:T(8,128)(2,1)}, bf16[4096,576]{1,0:T(8,128)(2,1)}) custom-call(s32[16]{0:T(128)} %copy-done.12, s32[16]{0:T(128)} %get-tuple-element.302.mine_ref, f32[4096,192]{1,0:T(8,128)} %get-tuple-element.164.dk_ref, f32[4096,128]{1,0:T(8,128)} %get-tuple-element.165.dv_ref, bf16[512,256]{1,0:T(8,128)(2,1)} %bitcast.182), custom_call_target="tpu_custom_call" | custom-call | flops 1100000000 | bytes 14000000 | tf_op jit(solution)/shard_map/latent_back/pallas_call | solution.py:320
  926.9 8.5 collective-permute-done.13
  935.4 5.7 convert_add_fusion.2
  946.4 9.5 convolution_convert_fusion.3
  959.7 5.6 all-to-all-start.12
  977.6 29.4 %all-to-all-done.12 = bf16[32,64,256]{2,1,0:T(8,128)(2,1)} async-done(((bf16[32,64,256]{2,1,0:T(8,128)(2,1)}), bf16[32,64,256]{2,1,0:T(8,128)(2,1)}, u32[]{:S(2)}, u32[]{:S(2)}) %all-to-all-start.12) | async-done | bytes 1048608 | tf_op jit(solution)/shard_map/all_to_all | solution.py:84
  1007.0 7.0 all-to-all-start.11
  1014.2 7.1 add_bitcast_fusion.2
  1023.4 18.3 %collective-permute-done.15 = bf16[704,2048]{1,0:T(8,128)(2,1)} collective-permute-done((bf16[704,2048]{1,0:T(8,128)(2,1)}, bf16[704,2048]{1,0:T(8,128)(2,1)}, u32[]{:S(2)}, u32[]{:S(2)}) %collective-permute-start.15) | collective-permute-done | bytes 2883616 | tf_op jit(solution)/shard_map/ppermute | solution.py:837
  1041.7 7.4 add_bitcast_fusion
  1049.1 4.8 add_bitcast_fusion.1
  1054.0 5.0 collective-permute-done.14
  1082.1 10.4 fusion.18
  1124.1 5.5 collective-permute-done.18
  1131.8 21.1 %all-to-all-done.14 = bf16[4,64,2048]{2,1,0:T(8,128)(2,1)} async-done(((bf16[4,64,2048]{2,1,0:T(8,128)(2,1)}), bf16[4,64,2048]{2,1,0:T(8,128)(2,1)}, u32[]{:S(2)}, u32[]{:S(2)}) %all-to-all-start.14) | async-done | bytes 1048608 | tf_op jit(solution)/shard_map/all_to_all | solution.py:84
  1171.7 13.2 %reduce-scatter.11.cloned.1.call-done = bf16[256,1024]{1,0:T(8,128)(2,1)} async-done(((bf16[4096,1024]{1,0:T(8,128)(2,1)}), bf16[256,1024]{1,0:T(8,128)(2,1)}) %reduce-scatter.11.cloned.1.call-update) | async-done | bytes 524304 | tf_op jit(solution)/shard_map/reduce_scatter | solution.py:911
  (364 shorter events, 253.7 us)
Async XLA Ops:
  7.2 181.3 %all-gather.5.cloned.1.call-start = ((), (), s32[]{:S(2)}) async-start(), calls=%async_computation.19 | async-start | bytes 17825792 | tf_op jit(solution)/shard_map/all_gather | solution.py:726
  9.9 17.2 %all-to-all-start.4 = ((f32[16,1,256]{2,1,0:T(1,128)}), f32[16,1,256]{2,1,0:T(1,128)S(1)}, u32[]{:S(2)}, u32[]{:S(2)}) async-start(f32[16,1,256]{2,1,0:T(1,128)} %copy.161), calls=%async_computation.4 | async-start | bytes 32768 | tf_op jit(solution)/shard_map/all_to_all | solution.py:84
  17.2 346.0 %all-gather.7.cloned.1.call-start = ((), (), s32[]{:S(2)}) async-start(), calls=%async_computation.20 | async-start | bytes 17825792 | tf_op jit(solution)/shard_map/all_gather | solution.py:731
  28.0 21.9 %all-to-all-start.2 = ((bf16[4,128,256]{1,2,0:T(8,128)(2,1)}), bf16[4,128,256]{1,2,0:T(8,128)(2,1)S(1)}, u32[]{:S(2)}, u32[]{:S(2)}) async-start(bf16[4,128,256]{1,2,0:T(8,128)(2,1)} %bitcast.14), calls=%async_computation.2 | async-start | bytes 524288 | tf_op jit(solution)/shard_map/all_to_all | solution.py:84
  50.7 20.7 %all-to-all-start.1 = ((bf16[4,64,592]{2,1,0:T(8,128)(2,1)}), bf16[4,64,592]{2,1,0:T(8,128)(2,1)S(1)}, u32[]{:S(2)}, u32[]{:S(2)}) async-start(bf16[4,64,592]{2,1,0:T(8,128)(2,1)} %broadcast_in_dim.42), calls=%async_computation.1 | async-start | bytes 655360 | tf_op jit(solution)/shard_map/all_to_all | solution.py:84
  72.5 56.9 %all-to-all-start.3 = ((bf16[4,64,2048]{2,1,0:T(8,128)(2,1)}), bf16[4,64,2048]{2,1,0:T(8,128)(2,1)S(1)}, u32[]{:S(2)}, u32[]{:S(2)}) async-start(bf16[4,64,2048]{2,1,0:T(8,128)(2,1)} %broadcast_in_dim.43), calls=%async_computation.3 | async-start | bytes 2097152 | tf_op jit(solution)/shard_map/all_to_all | solution.py:84
  76.1 16.0 %collective-permute-start = (bf16[4,64,592]{2,1,0:T(8,128)(2,1)S(1)}, bf16[4,64,592]{2,1,0:T(8,128)(2,1)S(1)}, u32[]{:S(2)}, u32[]{:S(2)}) collective-permute-start(bf16[4,64,592]{2,1,0:T(8,128)(2,1)S(1)} %all-to-all-done.1), channel_id=1, source_target_pairs={{0,8},{4,12},{8,0},{12,4},{1,9},{5,13},{9,1},{13,5},{2,10},{6,14},... | collective-permute-start | bytes 909320 | tf_op jit(solution)/shard_map/ppermute | solution.py:354
  93.2 41.7 %collective-permute-start.1 = (bf16[2,4,64,592]{3,2,0,1:T(8,128)(2,1)}, bf16[2,4,64,592]{3,2,0,1:T(8,128)(2,1)S(1)}, u32[]{:S(2)}, u32[]{:S(2)}) collective-permute-start(bf16[2,4,64,592]{3,2,0,1:T(8,128)(2,1)} %fusion.28), channel_id=1, source_target_pairs={{0,16},{16,0},{1,17},{17,1},{2,18},{18,2},{3,19},{19,3},{4,20},{20... | collective-permute-start | bytes 1818632 | tf_op jit(solution)/shard_map/ppermute | solution.py:354
  129.5 45.1 %all-to-all-start = ((bf16[4,512,192]{1,2,0:T(8,128)(2,1)}), bf16[4,512,192]{1,2,0:T(8,128)(2,1)}, u32[]{:S(2)}, u32[]{:S(2)}) async-start(bf16[4,512,192]{1,2,0:T(8,128)(2,1)} %bitcast.1), calls=%async_computation | async-start | bytes 1572864 | tf_op jit(solution)/shard_map/all_to_all | solution.py:84
  136.8 41.1 %collective-permute-start.2 = (bf16[2,2,4,64,592]{4,3,1,0,2:T(8,128)(2,1)}, bf16[2,2,4,64,592]{4,3,1,0,2:T(8,128)(2,1)}, u32[]{:S(2)}, u32[]{:S(2)}) collective-permute-start(bf16[2,2,4,64,592]{4,3,1,0,2:T(8,128)(2,1)} %fusion.24), channel_id=1, source_target_pairs={{0,4},{4,0},{8,12},{12,8},{1,5},{5,1},{9,13},{13,9},{2,6},{6,2},{1... | collective-permute-start | bytes 3637256 | tf_op jit(solution)/shard_map/ppermute | solution.py:354
  149.0 35.9 %collective-permute-start.3 = (bf16[4,64,2048]{2,1,0:T(8,128)(2,1)S(1)}, bf16[4,64,2048]{2,1,0:T(8,128)(2,1)}, u32[]{:S(2)}, u32[]{:S(2)}) collective-permute-start(bf16[4,64,2048]{2,1,0:T(8,128)(2,1)S(1)} %all-to-all-done.3), channel_id=1, source_target_pairs={{0,8},{4,12},{8,0},{12,4},{1,9},{5,13},{9,1},{13,5},{2,10},{6,14},... | collective-permute-start | bytes 3145736 | tf_op jit(solution)/shard_map/ppermute | solution.py:354
  152.2 43.9 %copy-start.5 = (bf16[4,128,256]{2,1,0:T(8,128)(2,1)}, bf16[4,128,256]{2,1,0:T(8,128)(2,1)S(1)}, u32[]{:S(2)}) copy-start(bf16[4,128,256]{2,1,0:T(8,128)(2,1)S(1)} %copy.157) | copy-start | bytes 786436
  188.5 68.6 %collective-permute-start.4 = (bf16[2,4,64,2048]{3,2,0,1:T(8,128)(2,1)}, bf16[2,4,64,2048]{3,2,0,1:T(8,128)(2,1)}, u32[]{:S(2)}, u32[]{:S(2)}) collective-permute-start(bf16[2,4,64,2048]{3,2,0,1:T(8,128)(2,1)} %fusion.21), channel_id=1, source_target_pairs={{0,16},{16,0},{1,17},{17,1},{2,18},{18,2},{3,19},{19,3},{4,20},{20... | collective-permute-start | bytes 6291464 | tf_op jit(solution)/shard_map/ppermute | solution.py:354
  191.3 41.2 %copy-start.14 = (s32[16]{0:T(128)}, s32[16]{0:T(128)S(1)}, u32[]{:S(2)}) copy-start(s32[16]{0:T(128)S(1)} %select_reduce_fusion.at_ref.index_ref) | copy-start | bytes 196
  191.3 71.6 %all-to-all-start.5 = ((bf16[4,512,352]{1,2,0:T(8,128)(2,1)}), bf16[4,512,352]{1,2,0:T(8,128)(2,1)}, u32[]{:S(2)}, u32[]{:S(2)}) async-start(bf16[4,512,352]{1,2,0:T(8,128)(2,1)} %pad_maximum_fusion.3), calls=%async_computation.5 | async-start | bytes 2883584 | tf_op jit(solution)/shard_map/all_to_all | solution.py:84
  264.8 64.2 %collective-permute-start.5 = (bf16[2,2,4,64,2048]{4,3,1,0,2:T(8,128)(2,1)}, bf16[2,2,4,64,2048]{4,3,1,0,2:T(8,128)(2,1)}, u32[]{:S(2)}, u32[]{:S(2)}) collective-permute-start(bf16[2,2,4,64,2048]{4,3,1,0,2:T(8,128)(2,1)} %fusion.3), channel_id=1, source_target_pairs={{0,4},{4,0},{8,12},{12,8},{1,5},{5,1},{9,13},{13,9},{2,6},{6,2},{1... | collective-permute-start | bytes 12582920 | tf_op jit(solution)/shard_map/ppermute | solution.py:354
  266.9 61.5 %all-to-all-start.6 = ((bf16[16,256,128]{2,1,0:T(8,128)(2,1)}), bf16[16,256,128]{2,1,0:T(8,128)(2,1)S(1)}, u32[]{:S(2)}, u32[]{:S(2)}) async-start(bf16[16,256,128]{2,1,0:T(8,128)(2,1)} %take_blocks.3), calls=%async_computation.6 | async-start | bytes 2097152 | tf_op jit(solution)/shard_map/all_to_all | solution.py:84
  273.1 218.8 %all-gather.9.cloned.1.call-start = ((), (), s32[]{:S(2)}) async-start(), calls=%async_computation.21 | async-start | bytes 17825792 | tf_op jit(solution)/shard_map/all_gather | solution.py:799
  363.2 256.4 %all-gather.11.cloned.1.call-start = ((), (), s32[]{:S(2)}) async-start(), calls=%async_computation.22 | async-start | bytes 12976128 | tf_op jit(solution)/shard_map/all_gather | solution.py:644
  493.7 286.5 %reduce-scatter.5.cloned.1.call-start = ((), (), s32[]{:S(2)}) async-start(), calls=%async_computation.23 | async-start | bytes 13369344 | tf_op jit(solution)/shard_map/reduce_scatter | solution.py:820
  649.2 64.9 %collective-permute-start.8 = (bf16[1024,1408]{1,0:T(8,128)(2,1)}, bf16[1024,1408]{1,0:T(8,128)(2,1)}, u32[]{:S(2)}, u32[]{:S(2)}) collective-permute-start(bf16[1024,1408]{1,0:T(8,128)(2,1)} %dynamic-slice_convert_fusion.2), channel_id=1, source_target_pairs={{0,16},{16,0},{1,17},{17,1},{2,18},{18,2},{3,19},{19,3},{4,20},{20... | collective-permute-start | bytes 8650760 | tf_op jit(solution)/shard_map/ppermute | solution.py:837
  650.7 40.8 %all-to-all-start.8 = ((f32[16,1,256]{2,1,0:T(1,128)}), f32[16,1,256]{2,1,0:T(1,128)S(1)}, u32[]{:S(2)}, u32[]{:S(2)}) async-start(f32[16,1,256]{2,1,0:T(1,128)} %bitcast.55), calls=%async_computation.9 | async-start | bytes 32768 | tf_op jit(solution)/shard_map/all_to_all | solution.py:84
  676.5 37.6 %collective-permute-start.6 = (bf16[2,1024,512]{2,1,0:T(8,128)(2,1)}, bf16[2,1024,512]{2,1,0:T(8,128)(2,1)S(1)}, u32[]{:S(2)}, u32[]{:S(2)}) collective-permute-start(bf16[2,1024,512]{2,1,0:T(8,128)(2,1)} %dynamic-slice_bitcast_fusion), channel_id=1, source_target_pairs={{0,4},{4,0},{8,12},{12,8},{1,5},{5,1},{9,13},{13,9},{2,6},{6,2},{1... | collective-permute-start | bytes 6291464 | tf_op jit(solution)/shard_map/ppermute | solution.py:655
  716.4 33.0 %collective-permute-start.7 = (bf16[1024,512]{1,0:T(8,128)(2,1)S(1)}, bf16[1024,512]{1,0:T(8,128)(2,1)S(1)}, u32[]{:S(2)}, u32[]{:S(2)}) collective-permute-start(bf16[1024,512]{1,0:T(8,128)(2,1)S(1)} %dynamic-slice_bitcast_fusion.1), channel_id=1, source_target_pairs={{0,8},{4,12},{8,0},{12,4},{1,9},{5,13},{9,1},{13,5},{2,10},{6,14},... | collective-permute-start | bytes 3145736 | tf_op jit(solution)/shard_map/ppermute | solution.py:655
  750.6 28.6 %all-to-all-start.7 = ((bf16[4,256,512]{2,1,0:T(8,128)(2,1)}), bf16[4,256,512]{2,1,0:T(8,128)(2,1)S(1)}, u32[]{:S(2)}, u32[]{:S(2)}) async-start(bf16[4,256,512]{2,1,0:T(8,128)(2,1)} %bitcast.52), calls=%async_computation.8 | async-start | bytes 2097152 | tf_op jit(solution)/shard_map/all_to_all | solution.py:84
  754.2 187.0 %reduce-scatter.7.cloned.1.call-start = ((), (), s32[]{:S(2)}) async-start(), calls=%async_computation.24 | async-start | bytes 8912896 | tf_op jit(solution)/shard_map/reduce_scatter | solution.py:860
  790.3 62.3 %collective-permute-start.10 = (bf16[1024,2048]{1,0:T(8,128)(2,1)}, bf16[1024,2048]{1,0:T(8,128)(2,1)}, u32[]{:S(2)}, u32[]{:S(2)}) collective-permute-start(bf16[1024,2048]{1,0:T(8,128)(2,1)} %convolution_convert_fusion), channel_id=1, source_target_pairs={{0,4},{4,0},{8,12},{12,8},{1,5},{5,1},{9,13},{13,9},{2,6},{6,2},{1... | collective-permute-start | bytes 12582920 | tf_op jit(solution)/shard_map/ppermute | solution.py:671
  796.1 64.4 %collective-permute-start.9 = (bf16[1024,1408]{1,0:T(8,128)(2,1)}, bf16[1024,1408]{1,0:T(8,128)(2,1)}, u32[]{:S(2)}, u32[]{:S(2)}) collective-permute-start(bf16[1024,1408]{1,0:T(8,128)(2,1)} %dynamic-slice_convert_fusion.1), channel_id=1, source_target_pairs={{0,16},{16,0},{1,17},{17,1},{2,18},{18,2},{3,19},{19,3},{4,20},{20... | collective-permute-start | bytes 8650760 | tf_op jit(solution)/shard_map/ppermute | solution.py:837
  800.7 51.3 %copy-start.15 = (s32[16]{0:T(128)S(1)}, s32[16]{0:T(128)}, u32[]{:S(2)}) copy-start(s32[16]{0:T(128)} %copy-done.14) | copy-start | bytes 196
  802.0 49.9 %all-to-all-start.9 = ((bf16[16,256,128]{2,1,0:T(8,128)(2,1)}), bf16[16,256,128]{2,1,0:T(8,128)(2,1)S(1)}, u32[]{:S(2)}, u32[]{:S(2)}) async-start(bf16[16,256,128]{2,1,0:T(8,128)(2,1)} %bitcast.59), calls=%async_computation.10 | async-start | bytes 2097152 | tf_op jit(solution)/shard_map/all_to_all | solution.py:84
  805.7 47.0 %copy-start.44 = (bf16[256,4,1,256]{0,3,2,1:T(8,128)(2,1)S(1)}, bf16[256,4,1,256]{0,3,2,1:T(8,128)(2,1)}, u32[]{:S(2)}) copy-start(bf16[256,4,1,256]{0,3,2,1:T(8,128)(2,1)} %get-tuple-element.314) | copy-start | bytes 1572868
  860.5 80.6 %all-to-all-start.10 = ((bf16[32,64,352]{2,1,0:T(8,128)(2,1)}), bf16[32,64,352]{2,1,0:T(8,128)(2,1)}, u32[]{:S(2)}, u32[]{:S(2)}) async-start(bf16[32,64,352]{2,1,0:T(8,128)(2,1)} %bitcast.53), calls=%async_computation.12 | async-start | bytes 3145728 | tf_op jit(solution)/shard_map/all_to_all | solution.py:84
  864.0 198.8 %reduce-scatter.9.cloned.1.call-start = ((), (), s32[]{:S(2)}) async-start(), calls=%async_computation.25 | async-start | bytes 5570560 | tf_op jit(solution)/shard_map/reduce_scatter | solution.py:895
  868.1 67.3 %collective-permute-start.13 = (bf16[512,2048]{1,0:T(8,128)(2,1)}, bf16[512,2048]{1,0:T(8,128)(2,1)}, u32[]{:S(2)}, u32[]{:S(2)}) collective-permute-start(bf16[512,2048]{1,0:T(8,128)(2,1)} %dynamic-slice_convert_fusion.3), channel_id=1, source_target_pairs={{0,16},{16,0},{1,17},{17,1},{2,18},{18,2},{3,19},{19,3},{4,20},{20... | collective-permute-start | bytes 6291464 | tf_op jit(solution)/shard_map/ppermute | solution.py:671
  872.0 69.1 %collective-permute-start.11 = (bf16[88,2048]{1,0:T(8,128)(2,1)}, bf16[88,2048]{1,0:T(8,128)(2,1)}, u32[]{:S(2)}, u32[]{:S(2)}) collective-permute-start(bf16[88,2048]{1,0:T(8,128)(2,1)} %get-tuple-element.319), channel_id=1, source_target_pairs={{0,0},{1,8},{2,16},{3,24},{4,2},{5,10},{6,18},{7,26},{8,4},{9,12},... | collective-permute-start | bytes 1081352 | tf_op jit(solution)/shard_map/ppermute | solution.py:884
  876.3 64.8 %collective-permute-start.12 = (bf16[88,2048]{1,0:T(8,128)(2,1)}, bf16[88,2048]{1,0:T(8,128)(2,1)}, u32[]{:S(2)}, u32[]{:S(2)}) collective-permute-start(bf16[88,2048]{1,0:T(8,128)(2,1)} %get-tuple-element.318), channel_id=1, source_target_pairs={{0,1},{1,9},{2,17},{3,25},{4,3},{5,11},{6,19},{7,27},{8,5},{9,13},... | collective-permute-start | bytes 1081352 | tf_op jit(solution)/shard_map/ppermute | solution.py:884
  959.7 47.3 %all-to-all-start.12 = ((bf16[32,64,256]{2,1,0:T(8,128)(2,1)}), bf16[32,64,256]{2,1,0:T(8,128)(2,1)}, u32[]{:S(2)}, u32[]{:S(2)}) async-start(bf16[32,64,256]{2,1,0:T(8,128)(2,1)} %pad_maximum_fusion.5), calls=%async_computation.15 | async-start | bytes 2097152 | tf_op jit(solution)/shard_map/all_to_all | solution.py:84
  970.0 71.7 %collective-permute-start.15 = (bf16[704,2048]{1,0:T(8,128)(2,1)}, bf16[704,2048]{1,0:T(8,128)(2,1)}, u32[]{:S(2)}, u32[]{:S(2)}) collective-permute-start(bf16[704,2048]{1,0:T(8,128)(2,1)} %dynamic-slice_convert_fusion), channel_id=1, source_target_pairs={{0,16},{16,0},{1,17},{17,1},{2,18},{18,2},{3,19},{19,3},{4,20},{20... | collective-permute-start | bytes 8650760 | tf_op jit(solution)/shard_map/ppermute | solution.py:837
  1007.0 55.8 %all-to-all-start.11 = ((bf16[16,256,192]{1,2,0:T(8,128)(2,1)}), bf16[16,256,192]{1,2,0:T(8,128)(2,1)S(1)}, u32[]{:S(2)}, u32[]{:S(2)}) async-start(bf16[16,256,192]{1,2,0:T(8,128)(2,1)} %copy.171), calls=%async_computation.14 | async-start | bytes 3145728 | tf_op jit(solution)/shard_map/all_to_all | solution.py:84
  1014.1 170.8 %reduce-scatter.11.cloned.1.call-start = ((), (), s32[]{:S(2)}) async-start(), calls=%async_computation.26 | async-start | bytes 8912896 | tf_op jit(solution)/shard_map/reduce_scatter | solution.py:911
  1014.1 35.0 %slice-start.2 = ((s8[11534336]{0:T(1024)(128)(4,1)}), s8[4194304]{0:T(1024)(128)(4,1)S(1)}, s32[]{:S(2)}) async-start(s8[11534336]{0:T(1024)(128)(4,1)} %bitcast.203), calls=%async_computation.29 | async-start | bytes 8388608
  1014.1 34.9 %slice-start.3 = ((s8[11534336]{0:T(1024)(128)(4,1)}), s8[4194304]{0:T(1024)(128)(4,1)S(1)}, s32[]{:S(2)}) async-start(s8[11534336]{0:T(1024)(128)(4,1)} %bitcast.203), calls=%async_computation.30 | async-start | bytes 8388608
  1021.4 37.6 %collective-permute-start.14 = (bf16[256,2048]{1,0:T(8,128)(2,1)S(1)}, bf16[256,2048]{1,0:T(8,128)(2,1)S(1)}, u32[]{:S(2)}, u32[]{:S(2)}) collective-permute-start(bf16[256,2048]{1,0:T(8,128)(2,1)S(1)} %dynamic-slice_convert_fusion.4), channel_id=1, source_target_pairs={{0,8},{4,12},{8,0},{12,4},{1,9},{5,13},{9,1},{13,5},{2,10},{6,14},... | collective-permute-start | bytes 3145736 | tf_op jit(solution)/shard_map/ppermute | solution.py:671
  1095.0 4.3 collective-permute-start.16
  1101.4 17.3 %collective-permute-start.17 = (bf16[512,640]{0,1:T(8,128)(2,1)S(1)}, bf16[512,640]{0,1:T(8,128)(2,1)}, u32[]{:S(2)}, u32[]{:S(2)}) collective-permute-start(bf16[512,640]{0,1:T(8,128)(2,1)S(1)} %dynamic-slice_convert_fusion.5), channel_id=1, source_target_pairs={{0,16},{16,0},{1,17},{17,1},{2,18},{18,2},{3,19},{19,3},{4,20},{20... | collective-permute-start | bytes 1966088 | tf_op jit(solution)/shard_map/ppermute | solution.py:671
  1107.9 45.1 %all-to-all-start.14 = ((bf16[4,64,2048]{2,1,0:T(8,128)(2,1)}), bf16[4,64,2048]{2,1,0:T(8,128)(2,1)}, u32[]{:S(2)}, u32[]{:S(2)}) async-start(bf16[4,64,2048]{2,1,0:T(8,128)(2,1)} %bitcast.81), calls=%async_computation.18 | async-start | bytes 2097152 | tf_op jit(solution)/shard_map/all_to_all | solution.py:84
  1120.1 9.5 collective-permute-start.18
  1153.0 14.4 %all-to-all-start.13 = ((bf16[4,64,640]{2,1,0:T(8,128)(2,1)}), bf16[4,64,640]{2,1,0:T(8,128)(2,1)S(1)}, u32[]{:S(2)}, u32[]{:S(2)}) async-start(bf16[4,64,640]{2,1,0:T(8,128)(2,1)} %bitcast.77), calls=%async_computation.17 | async-start | bytes 655360 | tf_op jit(solution)/shard_map/all_to_all | solution.py:84
  (68 other events, 562.4 us)
Sparse Core Ops, SparseCore 0:
  10.2 177.7 all-gather.4
  190.2 172.9 all-gather.6
  366.0 125.8 all-gather.8
  495.2 94.2 all-gather.10
  619.8 137.6 reduce-scatter.4
  781.9 147.8 reduce-scatter.6
  941.3 110.3 reduce-scatter.8
  1064.1 120.7 reduce-scatter.10

commit v5 on v4

--- a/solution.py
+++ b/solution.py
@@ -360,11 +360,31 @@
 
 
 def experts_body(
-    groups, units, count, n_parts, me_ref, place_ref, h_ref, crow_ref, dmid_ref, dsmid_ref, wg_ref,
-    wu_ref, wd_ref, ws_ref, wsd_ref, outa_ref, outb_ref, *refs,
+    groups, units, count, n_parts, me_ref, place_ref, h_ref, crow_ref, dmid_ref, dsmid_ref, wg_hbm,
+    wu_hbm, wd_hbm, ws_hbm, wsd_hbm, outa_ref, outb_ref, *refs,
 ):
     dh_refs = refs[:n_parts]
-    dprob_ref, rows_ref, dout_ref, mid_ref, dg_ref, du_ref, smid_ref, ds_ref = refs[n_parts:]
+    dprob_ref, rows_ref, dout_ref, mid_ref, dg_ref, du_ref, smid_ref, ds_ref = refs[
+        n_parts : n_parts + 8
+    ]
+    wg_ref, wu_ref, wd_ref, ws_ref, wsd_ref, sems = refs[n_parts + 8 :]
+    copies = [
+        pltpu.make_async_copy(source, target, sems.at[at])
+        for at, (source, target) in enumerate(
+            (
+                (ws_hbm, ws_ref), (wg_hbm, wg_ref), (wu_hbm, wu_ref), (wd_hbm, wd_ref),
+                (wsd_hbm, wsd_ref),
+            )
+        )
+    ]
+    opening = pl.program_id(0) == 0
+
+    @pl.when(opening)
+    def _():
+        for copy in copies:
+            copy.start()
+        copies[0].wait()
+
     width, hidden = wg_ref.shape
     padded = wsd_ref.shape[0]
     h = h_ref[...]
@@ -400,6 +420,11 @@
         weights.append(scale)
     scale = jnp.concatenate(weights, axis=0) if len(weights) > 1 else weights[0]
 
+    @pl.when(opening)
+    def _():
+        copies[1].wait()
+        copies[2].wait()
+
     for cols in chunks_of(hidden, 512):
         gate = dot(rows_ref[...], wg_ref[:, cols], 1, 0)
         up = dot(rows_ref[...], wu_ref[:, cols], 1, 0)
@@ -408,6 +433,11 @@
         d_mid = scale * dmid_ref[:, cols]
         dg_ref[:, cols] = (d_mid * up * slope).astype(BF16)
         du_ref[:, cols] = (d_mid * act).astype(BF16)
+
+    @pl.when(opening)
+    def _():
+        copies[3].wait()
+        copies[4].wait()
 
     d_prob = jnp.zeros(scale.shape, F32)
     for cols in chunks_of(width, 512):
@@ -497,7 +527,6 @@
     steps = tokens // step
     room = blocks * capacity
     groups = groups_of(capacity, blocks)
-    once = lambda a: pl.BlockSpec(a.shape, lambda i, me: (0, 0), pipeline_mode=pl.Buffered(1))
     tiled = lambda rows, cols: pl.BlockSpec((rows, cols), lambda i, me: (i, 0))
     line = pl.BlockSpec((1, 1, step), lambda i, me: (i, 0, 0))
     shape = lambda rows, cols, kind=BF16: jax.ShapeDtypeStruct((rows, cols), kind)
@@ -509,7 +538,7 @@
             grid=(steps,),
             in_specs=[
                 line, tiled(step, width), tiled(room, width), tiled(room, hidden), tiled(step, padded),
-                once(w_gate), once(w_up), once(w_down), once(w_shared), once(w_sdown),
+                *[pl.BlockSpec(memory_space=pl.ANY)] * 5,
             ],
             out_specs=[
                 tiled(step, width // 2), tiled(step, width // 2),
@@ -517,6 +546,10 @@
                 tiled(room, width),
                 tiled(room, width), tiled(room, hidden), tiled(room, hidden),
                 tiled(room, hidden), tiled(step, padded), tiled(step, 2 * padded),
+            ],
+            scratch_shapes=[
+                *[pltpu.VMEM(w.shape, BF16) for w in (w_gate, w_up, w_down, w_shared, w_sdown)],
+                pltpu.SemaphoreType.DMA((5,)),
             ],
         ),
         out_shape=[

time: 1210 us -> 1210 us (level)
  transfers between devices with their start and end apart: 42 -> 42, of which waited for: 22 -> 23; matrix products, arithmetic and copies ran while one was open for 27% -> 27% of each run, Pallas kernels for 22% -> 22%
where the time goes in v5:
time: 1210 us; the launch traced here: 1190 us
  waiting for transfers between devices  471 us (39%)
  Pallas kernels  263 us (22%)
  matrix products  134 us (11%)
  local copies, waits for them, and re-layouts  115 us (10%)
  other arithmetic  103 us (9%)
  starting transfers between devices  93.2 us (8%)
  between operations  15.8 us (1%)
    all_to_all x15, waiting for transfers between devices, trade(): return lax.all_to_all(buffer, axes, split_axis=0, concat_axis=0, tiled=True)  250 us
    pallas_call x1, Pallas kernels, experts(): pl.pallas_call(functools.partial(experts_body, groups, units, count, n_pa...  126 us
    dot_general x12, matrix products, matmul_tn(): lax.dot_general(left, right, (((0,), (0,)), ((), ())), preferred_element_...  109 us
    all_gather x1, waiting for transfers between devices, per_device(): h2_all = lax.all_gather(hidden2, ROW, axis=0, tiled=True)  96.2 us
    all_to_all x15, starting transfers between devices, trade(): return lax.all_to_all(buffer, axes, split_axis=0, concat_axis=0, tiled=True)  71.1 us
    unnamed x156, local copies, waits for them, and re-layouts  42.9 us
    ppermute x3, waiting for transfers between devices, share(): return (lax.ppermute(send, 'group', [(0, 1), (1, 0)]), keep)  41 us
    pallas_call x1, Pallas kernels, project(): pl.pallas_call(project_body, grid_spec=pltpu.PrefetchScalarGridSpec(num_s...  36.4 us
  transfers between devices with their start and end apart: 42, of which 23 were waited for; matrix products, arithmetic and copies ran while one was open for 27% of the time, Pallas kernels for 22%

profile of v5, /device:TPU:0, one launch (start us, length us, event | category | flops | bytes accessed | tf_op | source)
XLA Modules:
  0.0 1194.6 jit_solution(14308179594388170209)
XLA Ops:
  9.9 7.4 all-to-all-start.4
  17.8 9.3 multiply_sine_fusion
  28.0 5.0 all-to-all-start.2
  33.3 16.7 %all-to-all-done.2 = bf16[4,128,256]{1,2,0:T(8,128)(2,1)S(1)} async-done(((bf16[4,128,256]{1,2,0:T(8,128)(2,1)}), bf16[4,128,256]{1,2,0:T(8,128)(2,1)S(1)}, u32[]{:S(2)}, u32[]{:S(2)}) %all-to-all-start.2) | async-done | bytes 262176 | tf_op jit(solution)/shard_map/all_to_all | solution.py:84
  55.6 15.9 %all-to-all-done.1 = bf16[4,64,592]{2,1,0:T(8,128)(2,1)S(1)} async-done(((bf16[4,64,592]{2,1,0:T(8,128)(2,1)}), bf16[4,64,592]{2,1,0:T(8,128)(2,1)S(1)}, u32[]{:S(2)}, u32[]{:S(2)}) %all-to-all-start.1) | async-done | bytes 303136 | tf_op jit(solution)/shard_map/all_to_all | solution.py:84
  77.6 14.4 %collective-permute-done = bf16[4,64,592]{2,1,0:T(8,128)(2,1)S(1)} collective-permute-done((bf16[4,64,592]{2,1,0:T(8,128)(2,1)S(1)}, bf16[4,64,592]{2,1,0:T(8,128)(2,1)S(1)}, u32[]{:S(2)}, u32[]{:S(2)}) %collective-permute-start) | collective-permute-done | bytes 303136 | tf_op jit(solution)/shard_map/ppermute | solution.py:354
  98.3 31.1 %all-to-all-done.3 = bf16[4,64,2048]{2,1,0:T(8,128)(2,1)S(1)} async-done(((bf16[4,64,2048]{2,1,0:T(8,128)(2,1)}), bf16[4,64,2048]{2,1,0:T(8,128)(2,1)S(1)}, u32[]{:S(2)}, u32[]{:S(2)}) %all-to-all-start.3) | async-done | bytes 1048608 | tf_op jit(solution)/shard_map/all_to_all | solution.py:84
  129.5 5.5 all-to-all-start
  152.2 22.4 %all-to-all-done = bf16[4,512,192]{1,2,0:T(8,128)(2,1)} async-done(((bf16[4,512,192]{1,2,0:T(8,128)(2,1)}), bf16[4,512,192]{1,2,0:T(8,128)(2,1)}, u32[]{:S(2)}, u32[]{:S(2)}) %all-to-all-start) | async-done | bytes 786464 | tf_op jit(solution)/shard_map/all_to_all | solution.py:84
  196.1 36.4 %project.1 = (bf16[4096,2048]{1,0:T(8,128)(2,1)}, bf16[4096,192]{1,0:T(8,128)(2,1)S(1)}, bf16[4096,192]{1,0:T(8,128)(2,1)S(1)}, bf16[4096,128]{1,0:T(8,128)(2,1)S(1)}, bf16[4096,512]{1,0:T(8,128)(2,1)}) custom-call(s32[16]{0:T(128)S(1)} %select_reduce_fusion.at_ref.index_ref, bf16[16,256,2048]{2,1,0:T(8,128)(2,1)} %bitcast.236, ...), custom_call_target="tpu_custom_call" | custom-call | flops 14000000000 | bytes 48000000 | tf_op jit(solution)/shard_map/project/pallas_call | solution.py:158
  232.6 23.2 %attend.1 = (f32[4096,128]{1,0:T(8,128)S(1)}, bf16[4096,128]{1,0:T(8,128)(2,1)S(1)}, f32[1,4096]{1,0:T(1,128)S(1)}) custom-call(bf16[4096,192]{1,0:T(8,128)(2,1)S(1)} %get-tuple-element.112.q_ref, bf16[4096,192]{1,0:T(8,128)(2,1)S(1)} %get-tuple-element.113.k_ref, bf16[4096,128]{1,0:T(8,128)(2,1)S(1)} %get-tuple-element.114.v_ref), custom_call_target="tpu_custom_call" | custom-call | flops 6000000000 | bytes 10000000 | tf_op jit(solution)/shard_map/attend/pallas_call | solution.py:227
  257.1 5.8 fusion.3
  266.9 6.1 all-to-all-start.6
  276.3 5.6 concatenate.41.ws_hbm
  281.9 46.5 %all-to-all-done.6 = bf16[16,256,128]{2,1,0:T(8,128)(2,1)S(1)} async-done(((bf16[16,256,128]{2,1,0:T(8,128)(2,1)}), bf16[16,256,128]{2,1,0:T(8,128)(2,1)S(1)}, u32[]{:S(2)}, u32[]{:S(2)}) %all-to-all-start.6) | async-done | bytes 1048608 | tf_op jit(solution)/shard_map/all_to_all | solution.py:84
  329.0 7.8 fusion.1
  342.7 20.5 %all-gather.7.cloned.1.call-done.c_ref = bf16[4096,2048]{1,0:T(8,128)(2,1)} async-done(((bf16[256,2048]{1,0:T(8,128)(2,1)}), bf16[4096,2048]{1,0:T(8,128)(2,1)}) %all-gather.7.cloned.1.call-update) | async-done | bytes 16777232 | tf_op jit(solution)/shard_map/all_gather | solution.py:764
  367.6 26.1 %cotangent_rows.1 = (bf16[2304,2048]{1,0:T(8,128)(2,1)}, f32[2304,1408]{1,0:T(8,128)}, f32[4096,256]{1,0:T(8,128)S(1)}) custom-call(s32[8,1,512]{2,1,0:T(1,128)S(1)} %reshape.288.place_ref, bf16[4096,2048]{1,0:T(8,128)(2,1)} %all-gather.7.cloned.1.call-done.c_ref, bf16[1408,2048]{1,0:T(8,128)(2,1)S(1)} %bitcast.186, bf16[256,2048]{1,0:T(8,128)(2,1)S(1)} %pad.12.wsd_ref.wsd_hbm), custom_call_target="tpu_custom_call" | custom-call | flops 22414360576 | bytes 55000000 | tf_op jit(solution)/shard_map/cotangent_rows/pallas_call | solution.py:494
  395.7 96.2 %all-gather.9.cloned.1.call-done.h_ref = bf16[4096,2048]{1,0:T(8,128)(2,1)} async-done(((bf16[256,2048]{1,0:T(8,128)(2,1)}), bf16[4096,2048]{1,0:T(8,128)(2,1)}) %all-gather.9.cloned.1.call-update) | async-done | bytes 16777232 | tf_op jit(solution)/shard_map/all_gather | solution.py:832
  494.0 125.6 %experts.1 = (bf16[4096,1024]{1,0:T(8,128)(2,1)}, bf16[4096,1024]{1,0:T(8,128)(2,1)}, bf16[4096,1536]{1,0:T(8,128)(2,1)}, bf16[4096,512]{1,0:T(8,128)(2,1)}, f32...) custom-call(s32[1]{0:T(128)} %bitcast.43.me_ref, ...), custom_call_target="tpu_custom_call" | custom-call | flops 87912611840 | bytes 130000000 | tf_op jit(solution)/shard_map/experts/pallas_call | solution.py:534
  622.5 20.4 %fusion.59 = f32[2048,1408]{1,0:T(8,128)S(1)} fusion(bf16[2304,2048]{1,0:T(8,128)(2,1)} %get-tuple-element.140, bf16[2304,1408]{1,0:T(8,128)(2,1)} %get-tuple-element.143), kind=kOutput, calls=%fused_computation.194 | convolution fusion | flops 13287555072 | bytes 27459584 | tf_op jit(solution)/shard_map/dot_general | solution.py:42
  654.2 20.8 %fusion.60 = f32[2048,1408]{1,0:T(8,128)} fusion(bf16[2304,2048]{1,0:T(8,128)(2,1)} %get-tuple-element.140, bf16[2304,1408]{1,0:T(8,128)(2,1)} %get-tuple-element.144), kind=kOutput, calls=%fused_computation.195 | convolution fusion | flops 13287555072 | bytes 27459584 | tf_op jit(solution)/shard_map/dot_general | solution.py:42
  678.0 13.6 %convolution_convert_fusion.1 = bf16[2048,512]{1,0:T(8,128)(2,1)} fusion(bf16[4096,2048]{1,0:T(8,128)(2,1)} %all-gather.9.cloned.1.call-done.h_ref, bf16[4096,512]{1,0:T(8,128)(2,1)S(1)} %copy-done.67), kind=kOutput, calls=%fused_computation.39 | convolution fusion | flops 8590983168 | bytes 23068672 | tf_op jit(solution)/shard_map/dot_general | solution.py:42
  692.5 21.6 %collective-permute-done.8 = bf16[1024,1408]{1,0:T(8,128)(2,1)} collective-permute-done((bf16[1024,1408]{1,0:T(8,128)(2,1)}, bf16[1024,1408]{1,0:T(8,128)(2,1)}, u32[]{:S(2)}, u32[]{:S(2)}) %collective-permute-start.8) | collective-permute-done | bytes 2883616 | tf_op jit(solution)/shard_map/ppermute | solution.py:870
  716.7 19.5 %fusion.61 = f32[1408,2048]{1,0:T(8,128)} fusion(bf16[2304,1408]{1,0:T(8,128)(2,1)} %get-tuple-element.147, bf16[2304,2048]{1,0:T(8,128)(2,1)} %get-tuple-element.148), kind=kOutput, calls=%fused_computation.196 | convolution fusion | flops 13287555072 | bytes 27459584 | tf_op jit(solution)/shard_map/dot_general | solution.py:42
  736.2 13.4 %collective-permute-done.7 = bf16[1024,512]{1,0:T(8,128)(2,1)S(1)} collective-permute-done((bf16[1024,512]{1,0:T(8,128)(2,1)S(1)}, bf16[1024,512]{1,0:T(8,128)(2,1)S(1)}, u32[]{:S(2)}, u32[]{:S(2)}) %collective-permute-start.7) | collective-permute-done | bytes 1048608 | tf_op jit(solution)/shard_map/ppermute | solution.py:688
  754.4 8.7 fusion.62
  765.9 13.6 %all-to-all-done.7 = bf16[4,256,512]{2,1,0:T(8,128)(2,1)S(1)} async-done(((bf16[4,256,512]{2,1,0:T(8,128)(2,1)}), bf16[4,256,512]{2,1,0:T(8,128)(2,1)S(1)}, u32[]{:S(2)}, u32[]{:S(2)}) %all-to-all-start.7) | async-done | bytes 1048608 | tf_op jit(solution)/shard_map/all_to_all | solution.py:84
  790.5 5.8 dynamic-slice_convert_fusion.1
  805.6 45.6 %all-to-all-done.9.refs_0_.refs_1_.refs_2_.refs_3_.refs_4_.refs_5_.refs_6_.refs_7_ = bf16[16,256,128]{2,1,0:T(8,128)(2,1)S(1)} async-done(((bf16[16,256,128]{2,1,0:T(8,128)(2,1)}), bf16[16,256,128]{2,1,0:T(8,128)(2,1)S(1)}, u32[]{:S(2)}, u32[]{:S(2)}) %all-to-all-start.9) | async-done | bytes 1048608 | tf_op jit(solution)/shard_map/all_to_all | solution.py:84
  852.8 6.9 convert_add_fusion
  878.5 35.3 %attend_back.1 = (bf16[4096,192]{1,0:T(8,128)(2,1)S(1)}, f32[4096,192]{1,0:T(8,128)}, f32[4096,128]{1,0:T(8,128)}) custom-call(bf16[4096,192]{1,0:T(8,128)(2,1)} %copy-done.17, bf16[4096,192]{1,0:T(8,128)(2,1)} %copy-done.18, bf16[4096,128]{1,0:T(8,128)(2,1)S(1)} %copy-done.20, bf16[4096,128]{1,0:T(8,128)(2,1)S(1)} %bitcast.180, f32[4096,128]{1,0:T(8,128)} %copy-done.21, ...), custom_call_target="tpu_custom_call" | custom-call | flops 16000000000 | bytes 20000000 | tf_op jit(solution)/shard_map/attend_back/pallas_call | solution.py:286
  913.8 13.3 %latent_back.1 = (bf16[4096,256]{1,0:T(8,128)(2,1)}, bf16[4096,576]{1,0:T(8,128)(2,1)}) custom-call(s32[16]{0:T(128)} %copy-done.12, s32[16]{0:T(128)} %get-tuple-element.302.mine_ref, f32[4096,192]{1,0:T(8,128)} %get-tuple-element.164.dk_ref, f32[4096,128]{1,0:T(8,128)} %get-tuple-element.165.dv_ref, bf16[512,256]{1,0:T(8,128)(2,1)} %bitcast.182), custom_call_target="tpu_custom_call" | custom-call | flops 1100000000 | bytes 14000000 | tf_op jit(solution)/shard_map/latent_back/pallas_call | solution.py:320
  927.1 8.2 collective-permute-done.13
  935.3 5.7 convert_add_fusion.2
  946.3 9.4 convolution_convert_fusion.3
  959.5 6.0 all-to-all-start.12
  977.8 29.4 %all-to-all-done.12 = bf16[32,64,256]{2,1,0:T(8,128)(2,1)} async-done(((bf16[32,64,256]{2,1,0:T(8,128)(2,1)}), bf16[32,64,256]{2,1,0:T(8,128)(2,1)}, u32[]{:S(2)}, u32[]{:S(2)}) %all-to-all-start.12) | async-done | bytes 1048608 | tf_op jit(solution)/shard_map/all_to_all | solution.py:84
  1007.2 7.0 all-to-all-start.11
  1014.4 7.1 add_bitcast_fusion.2
  1023.6 18.3 %collective-permute-done.15 = bf16[704,2048]{1,0:T(8,128)(2,1)} collective-permute-done((bf16[704,2048]{1,0:T(8,128)(2,1)}, bf16[704,2048]{1,0:T(8,128)(2,1)}, u32[]{:S(2)}, u32[]{:S(2)}) %collective-permute-start.15) | collective-permute-done | bytes 2883616 | tf_op jit(solution)/shard_map/ppermute | solution.py:870
  1041.9 7.4 add_bitcast_fusion
  1049.3 4.8 add_bitcast_fusion.1
  1054.2 5.0 collective-permute-done.14
  1082.3 10.4 fusion.18
  1124.4 5.5 collective-permute-done.18
  1132.0 21.1 %all-to-all-done.14 = bf16[4,64,2048]{2,1,0:T(8,128)(2,1)} async-done(((bf16[4,64,2048]{2,1,0:T(8,128)(2,1)}), bf16[4,64,2048]{2,1,0:T(8,128)(2,1)}, u32[]{:S(2)}, u32[]{:S(2)}) %all-to-all-start.14) | async-done | bytes 1048608 | tf_op jit(solution)/shard_map/all_to_all | solution.py:84
  1171.9 13.1 %reduce-scatter.11.cloned.1.call-done = bf16[256,1024]{1,0:T(8,128)(2,1)} async-done(((bf16[4096,1024]{1,0:T(8,128)(2,1)}), bf16[256,1024]{1,0:T(8,128)(2,1)}) %reduce-scatter.11.cloned.1.call-update) | async-done | bytes 524304 | tf_op jit(solution)/shard_map/reduce_scatter | solution.py:944
  (364 shorter events, 254.4 us)
Async XLA Ops:
  7.2 181.3 %all-gather.5.cloned.1.call-start = ((), (), s32[]{:S(2)}) async-start(), calls=%async_computation.19 | async-start | bytes 17825792 | tf_op jit(solution)/shard_map/all_gather | solution.py:759
  9.9 17.2 %all-to-all-start.4 = ((f32[16,1,256]{2,1,0:T(1,128)}), f32[16,1,256]{2,1,0:T(1,128)S(1)}, u32[]{:S(2)}, u32[]{:S(2)}) async-start(f32[16,1,256]{2,1,0:T(1,128)} %copy.161), calls=%async_computation.4 | async-start | bytes 32768 | tf_op jit(solution)/shard_map/all_to_all | solution.py:84
  17.2 346.0 %all-gather.7.cloned.1.call-start = ((), (), s32[]{:S(2)}) async-start(), calls=%async_computation.20 | async-start | bytes 17825792 | tf_op jit(solution)/shard_map/all_gather | solution.py:764
  28.0 21.9 %all-to-all-start.2 = ((bf16[4,128,256]{1,2,0:T(8,128)(2,1)}), bf16[4,128,256]{1,2,0:T(8,128)(2,1)S(1)}, u32[]{:S(2)}, u32[]{:S(2)}) async-start(bf16[4,128,256]{1,2,0:T(8,128)(2,1)} %bitcast.14), calls=%async_computation.2 | async-start | bytes 524288 | tf_op jit(solution)/shard_map/all_to_all | solution.py:84
  50.7 20.7 %all-to-all-start.1 = ((bf16[4,64,592]{2,1,0:T(8,128)(2,1)}), bf16[4,64,592]{2,1,0:T(8,128)(2,1)S(1)}, u32[]{:S(2)}, u32[]{:S(2)}) async-start(bf16[4,64,592]{2,1,0:T(8,128)(2,1)} %broadcast_in_dim.42), calls=%async_computation.1 | async-start | bytes 655360 | tf_op jit(solution)/shard_map/all_to_all | solution.py:84
  72.5 56.9 %all-to-all-start.3 = ((bf16[4,64,2048]{2,1,0:T(8,128)(2,1)}), bf16[4,64,2048]{2,1,0:T(8,128)(2,1)S(1)}, u32[]{:S(2)}, u32[]{:S(2)}) async-start(bf16[4,64,2048]{2,1,0:T(8,128)(2,1)} %broadcast_in_dim.43), calls=%async_computation.3 | async-start | bytes 2097152 | tf_op jit(solution)/shard_map/all_to_all | solution.py:84
  76.1 16.0 %collective-permute-start = (bf16[4,64,592]{2,1,0:T(8,128)(2,1)S(1)}, bf16[4,64,592]{2,1,0:T(8,128)(2,1)S(1)}, u32[]{:S(2)}, u32[]{:S(2)}) collective-permute-start(bf16[4,64,592]{2,1,0:T(8,128)(2,1)S(1)} %all-to-all-done.1), channel_id=1, source_target_pairs={{0,8},{4,12},{8,0},{12,4},{1,9},{5,13},{9,1},{13,5},{2,10},{6,14},... | collective-permute-start | bytes 909320 | tf_op jit(solution)/shard_map/ppermute | solution.py:354
  93.2 41.7 %collective-permute-start.1 = (bf16[2,4,64,592]{3,2,0,1:T(8,128)(2,1)}, bf16[2,4,64,592]{3,2,0,1:T(8,128)(2,1)S(1)}, u32[]{:S(2)}, u32[]{:S(2)}) collective-permute-start(bf16[2,4,64,592]{3,2,0,1:T(8,128)(2,1)} %fusion.28), channel_id=1, source_target_pairs={{0,16},{16,0},{1,17},{17,1},{2,18},{18,2},{3,19},{19,3},{4,20},{20... | collective-permute-start | bytes 1818632 | tf_op jit(solution)/shard_map/ppermute | solution.py:354
  129.5 45.1 %all-to-all-start = ((bf16[4,512,192]{1,2,0:T(8,128)(2,1)}), bf16[4,512,192]{1,2,0:T(8,128)(2,1)}, u32[]{:S(2)}, u32[]{:S(2)}) async-start(bf16[4,512,192]{1,2,0:T(8,128)(2,1)} %bitcast.1), calls=%async_computation | async-start | bytes 1572864 | tf_op jit(solution)/shard_map/all_to_all | solution.py:84
  136.8 41.1 %collective-permute-start.2 = (bf16[2,2,4,64,592]{4,3,1,0,2:T(8,128)(2,1)}, bf16[2,2,4,64,592]{4,3,1,0,2:T(8,128)(2,1)}, u32[]{:S(2)}, u32[]{:S(2)}) collective-permute-start(bf16[2,2,4,64,592]{4,3,1,0,2:T(8,128)(2,1)} %fusion.24), channel_id=1, source_target_pairs={{0,4},{4,0},{8,12},{12,8},{1,5},{5,1},{9,13},{13,9},{2,6},{6,2},{1... | collective-permute-start | bytes 3637256 | tf_op jit(solution)/shard_map/ppermute | solution.py:354
  149.0 35.9 %collective-permute-start.3 = (bf16[4,64,2048]{2,1,0:T(8,128)(2,1)S(1)}, bf16[4,64,2048]{2,1,0:T(8,128)(2,1)}, u32[]{:S(2)}, u32[]{:S(2)}) collective-permute-start(bf16[4,64,2048]{2,1,0:T(8,128)(2,1)S(1)} %all-to-all-done.3), channel_id=1, source_target_pairs={{0,8},{4,12},{8,0},{12,4},{1,9},{5,13},{9,1},{13,5},{2,10},{6,14},... | collective-permute-start | bytes 3145736 | tf_op jit(solution)/shard_map/ppermute | solution.py:354
  152.2 43.9 %copy-start.5 = (bf16[4,128,256]{2,1,0:T(8,128)(2,1)}, bf16[4,128,256]{2,1,0:T(8,128)(2,1)S(1)}, u32[]{:S(2)}) copy-start(bf16[4,128,256]{2,1,0:T(8,128)(2,1)S(1)} %copy.157) | copy-start | bytes 786436
  188.5 68.6 %collective-permute-start.4 = (bf16[2,4,64,2048]{3,2,0,1:T(8,128)(2,1)}, bf16[2,4,64,2048]{3,2,0,1:T(8,128)(2,1)}, u32[]{:S(2)}, u32[]{:S(2)}) collective-permute-start(bf16[2,4,64,2048]{3,2,0,1:T(8,128)(2,1)} %fusion.21), channel_id=1, source_target_pairs={{0,16},{16,0},{1,17},{17,1},{2,18},{18,2},{3,19},{19,3},{4,20},{20... | collective-permute-start | bytes 6291464 | tf_op jit(solution)/shard_map/ppermute | solution.py:354
  191.3 41.2 %copy-start.14 = (s32[16]{0:T(128)}, s32[16]{0:T(128)S(1)}, u32[]{:S(2)}) copy-start(s32[16]{0:T(128)S(1)} %select_reduce_fusion.at_ref.index_ref) | copy-start | bytes 196
  191.3 71.6 %all-to-all-start.5 = ((bf16[4,512,352]{1,2,0:T(8,128)(2,1)}), bf16[4,512,352]{1,2,0:T(8,128)(2,1)}, u32[]{:S(2)}, u32[]{:S(2)}) async-start(bf16[4,512,352]{1,2,0:T(8,128)(2,1)} %pad_maximum_fusion.3), calls=%async_computation.5 | async-start | bytes 2883584 | tf_op jit(solution)/shard_map/all_to_all | solution.py:84
  264.8 64.2 %collective-permute-start.5 = (bf16[2,2,4,64,2048]{4,3,1,0,2:T(8,128)(2,1)}, bf16[2,2,4,64,2048]{4,3,1,0,2:T(8,128)(2,1)}, u32[]{:S(2)}, u32[]{:S(2)}) collective-permute-start(bf16[2,2,4,64,2048]{4,3,1,0,2:T(8,128)(2,1)} %fusion.3), channel_id=1, source_target_pairs={{0,4},{4,0},{8,12},{12,8},{1,5},{5,1},{9,13},{13,9},{2,6},{6,2},{1... | collective-permute-start | bytes 12582920 | tf_op jit(solution)/shard_map/ppermute | solution.py:354
  266.9 61.5 %all-to-all-start.6 = ((bf16[16,256,128]{2,1,0:T(8,128)(2,1)}), bf16[16,256,128]{2,1,0:T(8,128)(2,1)S(1)}, u32[]{:S(2)}, u32[]{:S(2)}) async-start(bf16[16,256,128]{2,1,0:T(8,128)(2,1)} %take_blocks.3), calls=%async_computation.6 | async-start | bytes 2097152 | tf_op jit(solution)/shard_map/all_to_all | solution.py:84
  273.1 218.9 %all-gather.9.cloned.1.call-start = ((), (), s32[]{:S(2)}) async-start(), calls=%async_computation.21 | async-start | bytes 17825792 | tf_op jit(solution)/shard_map/all_gather | solution.py:832
  363.2 256.4 %all-gather.11.cloned.1.call-start = ((), (), s32[]{:S(2)}) async-start(), calls=%async_computation.22 | async-start | bytes 12976128 | tf_op jit(solution)/shard_map/all_gather | solution.py:677
  493.7 286.7 %reduce-scatter.5.cloned.1.call-start = ((), (), s32[]{:S(2)}) async-start(), calls=%async_computation.23 | async-start | bytes 13369344 | tf_op jit(solution)/shard_map/reduce_scatter | solution.py:853
  649.1 65.1 %collective-permute-start.8 = (bf16[1024,1408]{1,0:T(8,128)(2,1)}, bf16[1024,1408]{1,0:T(8,128)(2,1)}, u32[]{:S(2)}, u32[]{:S(2)}) collective-permute-start(bf16[1024,1408]{1,0:T(8,128)(2,1)} %dynamic-slice_convert_fusion.2), channel_id=1, source_target_pairs={{0,16},{16,0},{1,17},{17,1},{2,18},{18,2},{3,19},{19,3},{4,20},{20... | collective-permute-start | bytes 8650760 | tf_op jit(solution)/shard_map/ppermute | solution.py:870
  650.7 40.8 %all-to-all-start.8 = ((f32[16,1,256]{2,1,0:T(1,128)}), f32[16,1,256]{2,1,0:T(1,128)S(1)}, u32[]{:S(2)}, u32[]{:S(2)}) async-start(f32[16,1,256]{2,1,0:T(1,128)} %bitcast.55), calls=%async_computation.9 | async-start | bytes 32768 | tf_op jit(solution)/shard_map/all_to_all | solution.py:84
  676.5 37.7 %collective-permute-start.6 = (bf16[2,1024,512]{2,1,0:T(8,128)(2,1)}, bf16[2,1024,512]{2,1,0:T(8,128)(2,1)S(1)}, u32[]{:S(2)}, u32[]{:S(2)}) collective-permute-start(bf16[2,1024,512]{2,1,0:T(8,128)(2,1)} %dynamic-slice_bitcast_fusion), channel_id=1, source_target_pairs={{0,4},{4,0},{8,12},{12,8},{1,5},{5,1},{9,13},{13,9},{2,6},{6,2},{1... | collective-permute-start | bytes 6291464 | tf_op jit(solution)/shard_map/ppermute | solution.py:688
  716.4 33.1 %collective-permute-start.7 = (bf16[1024,512]{1,0:T(8,128)(2,1)S(1)}, bf16[1024,512]{1,0:T(8,128)(2,1)S(1)}, u32[]{:S(2)}, u32[]{:S(2)}) collective-permute-start(bf16[1024,512]{1,0:T(8,128)(2,1)S(1)} %dynamic-slice_bitcast_fusion.1), channel_id=1, source_target_pairs={{0,8},{4,12},{8,0},{12,4},{1,9},{5,13},{9,1},{13,5},{2,10},{6,14},... | collective-permute-start | bytes 3145736 | tf_op jit(solution)/shard_map/ppermute | solution.py:688
  750.8 28.7 %all-to-all-start.7 = ((bf16[4,256,512]{2,1,0:T(8,128)(2,1)}), bf16[4,256,512]{2,1,0:T(8,128)(2,1)S(1)}, u32[]{:S(2)}, u32[]{:S(2)}) async-start(bf16[4,256,512]{2,1,0:T(8,128)(2,1)} %bitcast.52), calls=%async_computation.8 | async-start | bytes 2097152 | tf_op jit(solution)/shard_map/all_to_all | solution.py:84
  754.4 186.7 %reduce-scatter.7.cloned.1.call-start = ((), (), s32[]{:S(2)}) async-start(), calls=%async_computation.24 | async-start | bytes 8912896 | tf_op jit(solution)/shard_map/reduce_scatter | solution.py:893
  790.5 61.4 %collective-permute-start.10 = (bf16[1024,2048]{1,0:T(8,128)(2,1)}, bf16[1024,2048]{1,0:T(8,128)(2,1)}, u32[]{:S(2)}, u32[]{:S(2)}) collective-permute-start(bf16[1024,2048]{1,0:T(8,128)(2,1)} %convolution_convert_fusion), channel_id=1, source_target_pairs={{0,4},{4,0},{8,12},{12,8},{1,5},{5,1},{9,13},{13,9},{2,6},{6,2},{1... | collective-permute-start | bytes 12582920 | tf_op jit(solution)/shard_map/ppermute | solution.py:704
  796.3 64.4 %collective-permute-start.9 = (bf16[1024,1408]{1,0:T(8,128)(2,1)}, bf16[1024,1408]{1,0:T(8,128)(2,1)}, u32[]{:S(2)}, u32[]{:S(2)}) collective-permute-start(bf16[1024,1408]{1,0:T(8,128)(2,1)} %dynamic-slice_convert_fusion.1), channel_id=1, source_target_pairs={{0,16},{16,0},{1,17},{17,1},{2,18},{18,2},{3,19},{19,3},{4,20},{20... | collective-permute-start | bytes 8650760 | tf_op jit(solution)/shard_map/ppermute | solution.py:870
  800.6 50.6 %copy-start.15 = (s32[16]{0:T(128)S(1)}, s32[16]{0:T(128)}, u32[]{:S(2)}) copy-start(s32[16]{0:T(128)} %copy-done.14) | copy-start | bytes 196
  802.0 49.3 %all-to-all-start.9 = ((bf16[16,256,128]{2,1,0:T(8,128)(2,1)}), bf16[16,256,128]{2,1,0:T(8,128)(2,1)S(1)}, u32[]{:S(2)}, u32[]{:S(2)}) async-start(bf16[16,256,128]{2,1,0:T(8,128)(2,1)} %bitcast.59), calls=%async_computation.10 | async-start | bytes 2097152 | tf_op jit(solution)/shard_map/all_to_all | solution.py:84
  805.6 46.3 %copy-start.44 = (bf16[256,4,1,256]{0,3,2,1:T(8,128)(2,1)S(1)}, bf16[256,4,1,256]{0,3,2,1:T(8,128)(2,1)}, u32[]{:S(2)}) copy-start(bf16[256,4,1,256]{0,3,2,1:T(8,128)(2,1)} %get-tuple-element.314) | copy-start | bytes 1572868
  860.7 80.3 %all-to-all-start.10 = ((bf16[32,64,352]{2,1,0:T(8,128)(2,1)}), bf16[32,64,352]{2,1,0:T(8,128)(2,1)}, u32[]{:S(2)}, u32[]{:S(2)}) async-start(bf16[32,64,352]{2,1,0:T(8,128)(2,1)} %bitcast.53), calls=%async_computation.12 | async-start | bytes 3145728 | tf_op jit(solution)/shard_map/all_to_all | solution.py:84
  864.2 198.8 %reduce-scatter.9.cloned.1.call-start = ((), (), s32[]{:S(2)}) async-start(), calls=%async_computation.25 | async-start | bytes 5570560 | tf_op jit(solution)/shard_map/reduce_scatter | solution.py:928
  868.3 67.0 %collective-permute-start.13 = (bf16[512,2048]{1,0:T(8,128)(2,1)}, bf16[512,2048]{1,0:T(8,128)(2,1)}, u32[]{:S(2)}, u32[]{:S(2)}) collective-permute-start(bf16[512,2048]{1,0:T(8,128)(2,1)} %dynamic-slice_convert_fusion.3), channel_id=1, source_target_pairs={{0,16},{16,0},{1,17},{17,1},{2,18},{18,2},{3,19},{19,3},{4,20},{20... | collective-permute-start | bytes 6291464 | tf_op jit(solution)/shard_map/ppermute | solution.py:704
  872.1 68.9 %collective-permute-start.11 = (bf16[88,2048]{1,0:T(8,128)(2,1)}, bf16[88,2048]{1,0:T(8,128)(2,1)}, u32[]{:S(2)}, u32[]{:S(2)}) collective-permute-start(bf16[88,2048]{1,0:T(8,128)(2,1)} %get-tuple-element.319), channel_id=1, source_target_pairs={{0,0},{1,8},{2,16},{3,24},{4,2},{5,10},{6,18},{7,26},{8,4},{9,12},... | collective-permute-start | bytes 1081352 | tf_op jit(solution)/shard_map/ppermute | solution.py:917
  876.5 64.5 %collective-permute-start.12 = (bf16[88,2048]{1,0:T(8,128)(2,1)}, bf16[88,2048]{1,0:T(8,128)(2,1)}, u32[]{:S(2)}, u32[]{:S(2)}) collective-permute-start(bf16[88,2048]{1,0:T(8,128)(2,1)} %get-tuple-element.318), channel_id=1, source_target_pairs={{0,1},{1,9},{2,17},{3,25},{4,3},{5,11},{6,19},{7,27},{8,5},{9,13},... | collective-permute-start | bytes 1081352 | tf_op jit(solution)/shard_map/ppermute | solution.py:917
  959.5 47.7 %all-to-all-start.12 = ((bf16[32,64,256]{2,1,0:T(8,128)(2,1)}), bf16[32,64,256]{2,1,0:T(8,128)(2,1)}, u32[]{:S(2)}, u32[]{:S(2)}) async-start(bf16[32,64,256]{2,1,0:T(8,128)(2,1)} %pad_maximum_fusion.5), calls=%async_computation.15 | async-start | bytes 2097152 | tf_op jit(solution)/shard_map/all_to_all | solution.py:84
  970.2 71.7 %collective-permute-start.15 = (bf16[704,2048]{1,0:T(8,128)(2,1)}, bf16[704,2048]{1,0:T(8,128)(2,1)}, u32[]{:S(2)}, u32[]{:S(2)}) collective-permute-start(bf16[704,2048]{1,0:T(8,128)(2,1)} %dynamic-slice_convert_fusion), channel_id=1, source_target_pairs={{0,16},{16,0},{1,17},{17,1},{2,18},{18,2},{3,19},{19,3},{4,20},{20... | collective-permute-start | bytes 8650760 | tf_op jit(solution)/shard_map/ppermute | solution.py:870
  1007.2 55.8 %all-to-all-start.11 = ((bf16[16,256,192]{1,2,0:T(8,128)(2,1)}), bf16[16,256,192]{1,2,0:T(8,128)(2,1)S(1)}, u32[]{:S(2)}, u32[]{:S(2)}) async-start(bf16[16,256,192]{1,2,0:T(8,128)(2,1)} %copy.171), calls=%async_computation.14 | async-start | bytes 3145728 | tf_op jit(solution)/shard_map/all_to_all | solution.py:84
  1014.3 170.8 %reduce-scatter.11.cloned.1.call-start = ((), (), s32[]{:S(2)}) async-start(), calls=%async_computation.26 | async-start | bytes 8912896 | tf_op jit(solution)/shard_map/reduce_scatter | solution.py:944
  1014.3 35.0 %slice-start.2 = ((s8[11534336]{0:T(1024)(128)(4,1)}), s8[4194304]{0:T(1024)(128)(4,1)S(1)}, s32[]{:S(2)}) async-start(s8[11534336]{0:T(1024)(128)(4,1)} %bitcast.203), calls=%async_computation.29 | async-start | bytes 8388608
  1014.4 34.9 %slice-start.3 = ((s8[11534336]{0:T(1024)(128)(4,1)}), s8[4194304]{0:T(1024)(128)(4,1)S(1)}, s32[]{:S(2)}) async-start(s8[11534336]{0:T(1024)(128)(4,1)} %bitcast.203), calls=%async_computation.30 | async-start | bytes 8388608
  1021.6 37.6 %collective-permute-start.14 = (bf16[256,2048]{1,0:T(8,128)(2,1)S(1)}, bf16[256,2048]{1,0:T(8,128)(2,1)S(1)}, u32[]{:S(2)}, u32[]{:S(2)}) collective-permute-start(bf16[256,2048]{1,0:T(8,128)(2,1)S(1)} %dynamic-slice_convert_fusion.4), channel_id=1, source_target_pairs={{0,8},{4,12},{8,0},{12,4},{1,9},{5,13},{9,1},{13,5},{2,10},{6,14},... | collective-permute-start | bytes 3145736 | tf_op jit(solution)/shard_map/ppermute | solution.py:704
  1095.2 4.3 collective-permute-start.16
  1101.6 17.3 %collective-permute-start.17 = (bf16[512,640]{0,1:T(8,128)(2,1)S(1)}, bf16[512,640]{0,1:T(8,128)(2,1)}, u32[]{:S(2)}, u32[]{:S(2)}) collective-permute-start(bf16[512,640]{0,1:T(8,128)(2,1)S(1)} %dynamic-slice_convert_fusion.5), channel_id=1, source_target_pairs={{0,16},{16,0},{1,17},{17,1},{2,18},{18,2},{3,19},{19,3},{4,20},{20... | collective-permute-start | bytes 1966088 | tf_op jit(solution)/shard_map/ppermute | solution.py:704
  1108.1 45.1 %all-to-all-start.14 = ((bf16[4,64,2048]{2,1,0:T(8,128)(2,1)}), bf16[4,64,2048]{2,1,0:T(8,128)(2,1)}, u32[]{:S(2)}, u32[]{:S(2)}) async-start(bf16[4,64,2048]{2,1,0:T(8,128)(2,1)} %bitcast.81), calls=%async_computation.18 | async-start | bytes 2097152 | tf_op jit(solution)/shard_map/all_to_all | solution.py:84
  1120.3 9.5 collective-permute-start.18
  1153.2 14.4 %all-to-all-start.13 = ((bf16[4,64,640]{2,1,0:T(8,128)(2,1)}), bf16[4,64,640]{2,1,0:T(8,128)(2,1)S(1)}, u32[]{:S(2)}, u32[]{:S(2)}) async-start(bf16[4,64,640]{2,1,0:T(8,128)(2,1)} %bitcast.77), calls=%async_computation.17 | async-start | bytes 655360 | tf_op jit(solution)/shard_map/all_to_all | solution.py:84
  (68 other events, 561.3 us)
Sparse Core Ops, SparseCore 0:
  10.2 177.7 all-gather.4
  190.2 172.9 all-gather.6
  366.0 125.8 all-gather.8
  495.2 94.1 all-gather.10
  619.8 137.7 reduce-scatter.4
  782.2 147.6 reduce-scatter.6
  941.2 110.6 reduce-scatter.8
  1064.3 120.7 reduce-scatter.10
